TPU v7x, 256 devices: a whole 4x4x8 slice. The times are simulated.
256 devices in a mesh: gx: 4 (over x), gy: 16 (over y_hi, z), gz: 4 (over y_lo, core).
Axes of the slice: x: 4, y: 4 (y_hi: 2, y_lo: 2; y = y_hi * 2 + y_lo), z: 8, core: 2. Of those that a mesh axis runs over, the one named last changes fastest.
Arguments:
- acoustic_iterate: float32 [2, 32, 512, 1024], P(None, 'gx', 'gy', 'gz'), may hold values from -6 to 6
- coarse_update: float32 [2, 16, 256, 512], P(None, 'gx', 'gy', 'gz'), may hold values from -6 to 6
- class_codes_volume: int32 [32, 512, 1024], P('gx', 'gy', 'gz'), may hold values from 0 to 3
- element_location: int32 [1024, 3], replicated, may hold values from 0 to 1023, as said below
- element_excitation: float32 [2, 1024], replicated, may hold values from -24 to 24
- class_wavespeed: float32 [4], replicated, may hold values from 1 to 2
- class_damping: float32 [4], replicated, may hold values from 0.2 to 1
- washout_fraction: float32 [4], replicated, may hold values from 0.005 to 0.05
- thermal_excess: float32 [16, 256, 512], P('gx', 'gy', 'gz'), may hold values from 12 to 22
- injury_integral: float32 [16, 256, 512], P('gx', 'gy', 'gz'), may hold values from 0.01 to 1
Outputs:
- pressure_out: float32 [2, 32, 512, 1024], P(None, 'gx', 'gy', 'gz')
- temperature_out: float32 [16, 256, 512], P('gx', 'gy', 'gz')
- log_dose: float32 [16, 256, 512], P('gx', 'gy', 'gz')
Inputs may be any that keep to these rules, and one draw needn't show every extreme that they name: `element_location`: each row holds the first, second and third grid index of one element's cell, below 32, 512 and 1024 respectively; several elements may share a cell.
All inputs are finite; a program needn't handle non-finite values.
Results may differ from a plain program's by a relative error of at most 0.000035.
Values sent between devices are 32-bit elements; how exact they have to be, the bound alone decides.
No kernel may reach another device: no remote copies, remote signals or barrier semaphores. Data moves between devices by JAX's collectives and lax.ppermute only.
A program may use at most 128 MiB of HBM per device.

v0:
```python
import jax
import jax.numpy as jnp
from jax import lax
from jax.sharding import PartitionSpec as P

SWEEPS = 2
STEPS = 4


RELAXATION = 0.8
DAMPING_SHIFT = 0.5
DIFFUSION = 0.15
HEATING = 0.25
LN_PREFACTOR = 226.78
ENERGY_BARRIER = 75535.0
CORE_WARMTH = 310.15


def with_halo(array, sides, width):
    for axis, dim in sides:
        devices, length = (lax.axis_size(axis), array.shape[dim])
        up = [(i, (i + 1) % devices) for i in range(devices - 1)]
        down = [(j, i) for i, j in up]
        last = lax.slice_in_dim(array, length - width, length, axis=dim)
        first = lax.slice_in_dim(array, 0, width, axis=dim)
        before = lax.ppermute(last, axis, up)
        after = lax.ppermute(first, axis, down)
        array = jnp.concatenate([before, array, after], axis=dim)
    return array


def lookup(class_codes_volume, table):
    total = jnp.zeros(class_codes_volume.shape, table.dtype)
    for tissue in range(table.shape[0]):
        total = total + (class_codes_volume == tissue).astype(table.dtype) * table[tissue]
    return total


def neighbours(bordered_volume):
    total = bordered_volume[:, 2:, 1:-1, 1:-1] + bordered_volume[:, :-2, 1:-1, 1:-1]
    total = total + bordered_volume[:, 1:-1, 2:, 1:-1] + bordered_volume[:, 1:-1, :-2, 1:-1]
    return total + bordered_volume[:, 1:-1, 1:-1, 2:] + bordered_volume[:, 1:-1, 1:-1, :-2]


def jacobi(bordered_volume, diag_real, diag_imag, gain_real, gain_imag, source):
    wave_state = bordered_volume[:, 1:-1, 1:-1, 1:-1]
    beside_all = neighbours(bordered_volume)
    apply_real = diag_real * wave_state[0] - diag_imag * wave_state[1] - beside_all[0]
    apply_imag = diag_real * wave_state[1] + diag_imag * wave_state[0] - beside_all[1]
    resid_real = source[0] - apply_real
    resid_imag = source[1] - apply_imag
    new_real = wave_state[0] + gain_real * resid_real + gain_imag * resid_imag
    new_imag = wave_state[1] + gain_real * resid_imag - gain_imag * resid_real
    return jnp.stack([new_real, new_imag])


def prolong_axis(bordered_volume, axis):
    length = bordered_volume.shape[axis] - 2
    center = lax.slice_in_dim(bordered_volume, 1, length + 1, axis=axis)
    lower = lax.slice_in_dim(bordered_volume, 0, length, axis=axis)
    upper = lax.slice_in_dim(bordered_volume, 2, length + 2, axis=axis)
    even = 0.75 * center + 0.25 * lower
    odd = 0.75 * center + 0.25 * upper
    paired = jnp.stack([even, odd], axis=axis + 1)
    new_shape = list(center.shape)
    new_shape[axis] = 2 * length
    return paired.reshape(new_shape)


def prolong(bordered_volume):
    result = bordered_volume
    for axis in (1, 2, 3):
        result = prolong_axis(result, axis)
    return result


def restrict(fields):
    count, size_a, size_b, size_c = fields.shape
    blocks = fields.reshape(count, size_a // 2, 2, size_b // 2, 2, size_c // 2, 2)
    return jnp.sum(blocks, axis=(2, 4, 6)) * 0.125


def thermal_advance(bordered_volume, perf_coarse, power_coarse):
    centre = bordered_volume[1:-1, 1:-1, 1:-1]
    beside_all = neighbours(bordered_volume[None])[0]
    return (
        centre
        + DIFFUSION * (beside_all - 6.0 * centre)
        - perf_coarse * centre
        + HEATING * power_coarse
    )


def injury_kinetics(warming_excess):
    return jnp.exp(LN_PREFACTOR - ENERGY_BARRIER / (CORE_WARMTH + warming_excess))


def place_sources(element_location, element_excitation, anchor, extent):
    corner = jnp.stack(anchor)
    bounds = jnp.array(extent, jnp.int32)
    local = element_location - corner[None, :]
    owned = jnp.all((local >= 0) & (local < bounds[None, :]), axis=1)
    clipped = jnp.clip(local, 0, bounds[None, :] - 1)
    values = element_excitation * owned.astype(jnp.float32)[None, :]
    empty = jnp.zeros((2,) + tuple(extent), jnp.float32)
    return empty.at[:, clipped[:, 0], clipped[:, 1], clipped[:, 2]].add(values)


def on_device(
    acoustic_iterate,
    coarse_update,
    class_codes_volume,
    element_location,
    element_excitation,
    class_wavespeed,
    class_damping,
    washout_fraction,
    thermal_excess,
    injury_integral,
):
    cells_x, cells_y, cells_z = class_codes_volume.shape
    anchor = [
        lax.axis_index("gx") * cells_x,
        lax.axis_index("gy") * cells_y,
        lax.axis_index("gz") * cells_z,
    ]
    speed_cells = lookup(class_codes_volume, class_wavespeed)
    atten_cells = lookup(class_codes_volume, class_damping)
    perf_cells = lookup(class_codes_volume, washout_fraction)
    wave = 1.0 / (speed_cells * speed_cells)
    diag_real = 6.0 - wave
    diag_imag = DAMPING_SHIFT * wave + atten_cells
    modulus = diag_real * diag_real + diag_imag * diag_imag
    gain_real = RELAXATION * diag_real / modulus
    gain_imag = RELAXATION * diag_imag / modulus
    coarse = with_halo(coarse_update, (("gx", 1), ("gy", 2), ("gz", 3)), 1)
    wave_state = acoustic_iterate + prolong(coarse)
    source = place_sources(
        element_location, element_excitation, anchor, (cells_x, cells_y, cells_z)
    )
    for sweep_index in range(SWEEPS):
        bordered_volume = with_halo(wave_state, (("gx", 1), ("gy", 2), ("gz", 3)), 1)
        wave_state = jacobi(bordered_volume, diag_real, diag_imag, gain_real, gain_imag, source)
    power = atten_cells * (wave_state[0] * wave_state[0] + wave_state[1] * wave_state[1])
    coarsened_volumes = restrict(jnp.stack([power, perf_cells]))
    injury_gain = injury_integral
    warming_excess = thermal_excess
    for step_index in range(STEPS):
        bordered_volume = with_halo(warming_excess, (("gx", 0), ("gy", 1), ("gz", 2)), 1)
        warming_excess = thermal_advance(
            bordered_volume, coarsened_volumes[1], coarsened_volumes[0]
        )
        injury_gain = injury_gain + injury_kinetics(warming_excess)
    return (wave_state, warming_excess, jnp.log(injury_gain))


def solution(mesh):
    placed = (
        P(None, "gx", "gy", "gz"),
        P(None, "gx", "gy", "gz"),
        P("gx", "gy", "gz"),
        P(),
        P(),
        P(),
        P(),
        P(),
        P("gx", "gy", "gz"),
        P("gx", "gy", "gz"),
    )
    return jax.shard_map(
        on_device,
        mesh=mesh,
        in_specs=placed,
        out_specs=(P(None, "gx", "gy", "gz"), P("gx", "gy", "gz"), P("gx", "gy", "gz")),
        check_vma=False,
    )
```

profile of v0, /device:TPU:30, one launch (start us, length us, event | category | flops | bytes accessed | tf_op | source)
XLA Modules:
  0.0 338.7 jit_solution(9980337558654248771)
XLA Ops:
  2.7 4.5 %collective-permute-start.1 = (f32[2,1,16,128]{3,2,1,0:T(8,128)S(1)}, f32[2,1,16,128]{3,2,1,0:T(8,128)S(1)}, u32[]{:S(2)}, u32[]{:S(2)}) collective-permute-start(f32[2,1,16,128]{3,2,1,0:T(8,128)S(1)} %get-tuple-element.60), channel_id=1, source_target_pairs={{64,0},{128,64},{192,128},{65,1},{129,65},{193,129},{66,2},{130,66... | collective-permute-start | bytes 49160 | tf_op jit(solution)/shard_map/ppermute | solution.py:27
  9.2 4.5 %collective-permute-start.19 = (f32[1,16,128]{2,1,0:T(8,128)S(1)}, f32[1,16,128]{2,1,0:T(8,128)S(1)}, u32[]{:S(2)}, u32[]{:S(2)}) collective-permute-start(f32[1,16,128]{2,1,0:T(8,128)S(1)} %get-tuple-element.76), channel_id=1, source_target_pairs={{64,0},{128,64},{192,128},{65,1},{129,65},{193,129},{66,2},{130,66... | collective-permute-start | bytes 24584 | tf_op jit(solution)/shard_map/ppermute | solution.py:27
  18.6 19.2 %scatter_custom_fusion = f32[2,65536]{0,1:T(8,128)} fusion(s32[1024]{0:T(1024)S(1)} %broadcast_select_fusion, f32[1024,2]{1,0:T(8,128)S(1)} %copy.149, f32[]{:T(128)} %constant.31.clone.1), kind=kCustom, calls=%fused_computation.3 | custom fusion | flops 2048 | bytes 524292
  37.8 36.4 %slice_reduce_fusion = (f32[65536]{0:T(1024)S(1)}, f32[65536]{0:T(1024)S(1)}) fusion(f32[2,65536]{0,1:T(8,128)} %scatter_custom_fusion), kind=kLoop, calls=%fused_computation.1 | loop fusion | bytes 1048576 | tf_op jit(solution)/shard_map/slice | solution.py:51
  74.3 3.3 select_add_fusion
  78.3 8.4 %collective-permute-start.3 = (f32[2,6,1,128]{3,2,1,0:T(1,128)S(1)}, f32[2,6,1,128]{3,2,1,0:T(1,128)S(1)}, u32[]{:S(2)}, u32[]{:S(2)}) collective-permute-start(f32[2,6,1,128]{3,2,1,0:T(1,128)S(1)} %get-tuple-element.51), channel_id=1, source_target_pairs={{4,0},{8,4},{12,8},{16,12},{20,16},{24,20},{28,24},{32,28},{36,32}... | collective-permute-start | bytes 18440 | tf_op jit(solution)/shard_map/ppermute | solution.py:27
  86.8 2.1 collective-permute-start.2
  89.7 18.1 %stack.86 = f32[1,4,2,16,2,128,2]{6,5,4,3,2,1,0:T(8,128)} reshape(f32[8,32,256]{2,1,0:T(8,128)S(1)} %get-tuple-element.18) | data formatting | bytes 524288 | tf_op jit(solution)/shard_map/stack | solution.py:145
  107.8 10.0 %copy.165 = f32[1,4,2,16,2,128,2]{5,3,6,4,2,1,0:T(8,128)S(1)} copy(f32[1,4,2,16,2,128,2]{6,5,4,3,2,1,0:T(8,128)} %stack.86) | data formatting | bytes 524288 | tf_op jit(solution)/shard_map/stack | solution.py:145
  117.9 1.9 collective-permute-start.5
  119.8 2.4 collective-permute-start.4
  122.8 3.4 %collective-permute-done.4 = f32[2,6,18,1]{3,2,1,0:T(8,128)S(1)} collective-permute-done((f32[2,6,18,1]{3,2,1,0:T(8,128)S(1)}, f32[2,6,18,1]{3,2,1,0:T(8,128)S(1)}, u32[]{:S(2)}, u32[]{:S(2)}) %collective-permute-start.4) | collective-permute-done | bytes 896 | tf_op jit(solution)/shard_map/ppermute | solution.py:26
  130.8 2.7 collective-permute-start.6
  136.2 3.5 %collective-permute-done.7 = f32[2,1,32,256]{3,2,1,0:T(8,128)S(1)} collective-permute-done((f32[2,1,32,256]{3,2,1,0:T(8,128)S(1)}, f32[2,1,32,256]{3,2,1,0:T(8,128)S(1)}, u32[]{:S(2)}, u32[]{:S(2)}) %collective-permute-start.7) | collective-permute-done | bytes 65568 | tf_op jit(solution)/shard_map/ppermute | solution.py:26
  139.8 1.9 collective-permute-start.9
  142.4 7.5 %collective-permute-start.8 = (f32[2,10,1,256]{3,0,2,1:T(2,128)S(1)}, f32[2,10,1,256]{3,0,2,1:T(2,128)S(1)}, u32[]{:S(2)}, u32[]{:S(2)}) collective-permute-start(f32[2,10,1,256]{3,0,2,1:T(2,128)S(1)} %copy.150), channel_id=1, source_target_pairs={{4,0},{8,4},{12,8},{16,12},{20,16},{24,20},{28,24},{32,28},{36,32}... | collective-permute-start | bytes 61448 | tf_op jit(solution)/shard_map/ppermute | solution.py:27
  151.8 1.9 collective-permute-start.10
  153.8 2.4 collective-permute-start.11
  157.0 7.9 %collective-permute-start.21 = (f32[6,1,128]{2,1,0:T(1,128)S(1)}, f32[6,1,128]{2,1,0:T(1,128)S(1)}, u32[]{:S(2)}, u32[]{:S(2)}) collective-permute-start(f32[6,1,128]{2,1,0:T(1,128)S(1)} %get-tuple-element.69), channel_id=1, source_target_pairs={{4,0},{8,4},{12,8},{16,12},{20,16},{24,20},{28,24},{32,28},{36,32}... | collective-permute-start | bytes 9224 | tf_op jit(solution)/shard_map/ppermute | solution.py:27
  164.9 1.9 collective-permute-start.20
  168.5 6.3 %fusion.28 = (f32[1,8,32,256]{3,2,1,0:T(8,128)S(1)}, f32[8,32,256]{2,1,0:T(8,128)S(1)}, f32[8,32,256]{2,1,0:T(8,128)S(1)}) fusion(f32[2,8,32,256]{3,2,1,0:T(8,128)S(1)} %add.250, pred[8,32,256]{2,1,0:T(8,128)(4,1)} %get-tuple-element.22, f32[]{:T(128)} %bitcast.17, pred[8,32,256]{2,1,0:T(8,128)(4,1)} %get-tuple-element.21, f32[]{:T(128)} %bitcast.16, ...), kind=kLoop, calls=%fused_computation.88 | loop fusion | flops 2621440 | bytes 2621472 | tf_op jit(solution)/shard_map/stack | solution.py:54
  174.9 6.3 %fusion.33 = f32[1,8,32,256]{3,2,1,0:T(8,128)S(1)} fusion(f32[8,32,256]{2,1,0:T(8,128)S(1)} %get-tuple-element.25, f32[8,32,256]{2,1,0:T(8,128)S(1)} %get-tuple-element.24, f32[2,8,32,256]{3,2,1,0:T(8,128)S(1)} %add.250, pred[8,32,256]{2,1,0:T(8,128)(4,1)} %get-tuple-element.22, f32[]{:T(128)} %bitcast.17, pred[8,32,256]{2,1,0:T(8,128)(4,1)} %get-tuple-element.21, ...), kind=kLoop, calls=%fused_computation.105 | loop fusion | flops 1966080 | bytes 1310752 | tf_op jit(solution)/shard_map/stack | solution.py:54
  181.2 2.4 collective-permute-start.12
  185.8 4.0 %collective-permute-done.13 = f32[2,1,32,256]{3,2,1,0:T(8,128)S(1)} collective-permute-done((f32[2,1,32,256]{3,2,1,0:T(8,128)S(1)}, f32[2,1,32,256]{3,2,1,0:T(8,128)S(1)}, u32[]{:S(2)}, u32[]{:S(2)}) %collective-permute-start.13) | collective-permute-done | bytes 65568 | tf_op jit(solution)/shard_map/ppermute | solution.py:26
  189.9 1.9 collective-permute-start.15
  193.8 2.4 collective-permute-start.22
  196.2 7.5 %collective-permute-start.14 = (f32[2,10,1,256]{3,0,2,1:T(2,128)S(1)}, f32[2,10,1,256]{3,0,2,1:T(2,128)S(1)}, u32[]{:S(2)}, u32[]{:S(2)}) collective-permute-start(f32[2,10,1,256]{3,0,2,1:T(2,128)S(1)} %copy.178), channel_id=1, source_target_pairs={{4,0},{8,4},{12,8},{16,12},{20,16},{24,20},{28,24},{32,28},{36,32}... | collective-permute-start | bytes 61448 | tf_op jit(solution)/shard_map/ppermute | solution.py:27
  205.7 1.9 collective-permute-start.16
  207.7 2.6 collective-permute-start.17
  212.5 3.8 %collective-permute-done.17 = f32[2,10,34,1]{3,0,2,1:T(2,128)S(1)} collective-permute-done((f32[2,10,34,1]{3,0,2,1:T(2,128)S(1)}, f32[2,10,34,1]{3,0,2,1:T(2,128)S(1)}, u32[]{:S(2)}, u32[]{:S(2)}) %collective-permute-start.17) | collective-permute-done | bytes 2752 | tf_op jit(solution)/shard_map/ppermute | solution.py:26
  217.9 6.5 %add_multiply_fusion = (f32[8,32,256]{2,1,0:T(8,128)S(1)}, f32[8,32,256]{2,1,0:T(8,128)S(1)}, f32[8,32,256]{2,1,0:T(8,128)S(1)}) fusion(pred[8,32,256]{2,1,0:T(8,128)(4,1)} %get-tuple-element.22, pred[8,32,256]{2,1,0:T(8,128)(4,1)} %get-tuple-element.21, pred[8,32,256]{2,1,0:T(8,128)(4,1)S(1)} %get-tuple-element.20, ...), kind=kLoop, calls=%fused_computation.77 | loop fusion | flops 3670016 | bytes 3145760 | tf_op jit(solution)/shard_map/mul | solution.py:144
  224.4 18.1 %stack.85 = f32[1,4,2,16,2,128,2]{6,5,4,3,2,1,0:T(8,128)} reshape(f32[8,32,256]{2,1,0:T(8,128)S(1)} %get-tuple-element.15) | data formatting | bytes 524288 | tf_op jit(solution)/shard_map/stack | solution.py:145
  242.4 10.0 %copy.164 = f32[1,4,2,16,2,128,2]{5,3,6,4,2,1,0:T(8,128)S(1)} copy(f32[1,4,2,16,2,128,2]{6,5,4,3,2,1,0:T(8,128)} %stack.85) | data formatting | bytes 524288 | tf_op jit(solution)/shard_map/stack | solution.py:145
  255.9 4.2 %collective-permute-done.24 = f32[1,16,128]{2,1,0:T(8,128)S(1)} collective-permute-done((f32[1,16,128]{2,1,0:T(8,128)S(1)}, f32[1,16,128]{2,1,0:T(8,128)S(1)}, u32[]{:S(2)}, u32[]{:S(2)}) %collective-permute-start.24) | collective-permute-done | bytes 8224 | tf_op jit(solution)/shard_map/ppermute | solution.py:26
  260.1 7.9 %collective-permute-start.27 = (f32[6,1,128]{2,1,0:T(1,128)S(1)}, f32[6,1,128]{2,1,0:T(1,128)S(1)}, u32[]{:S(2)}, u32[]{:S(2)}) collective-permute-start(f32[6,1,128]{2,1,0:T(1,128)S(1)} %get-tuple-element.67), channel_id=1, source_target_pairs={{4,0},{8,4},{12,8},{16,12},{20,16},{24,20},{28,24},{32,28},{36,32}... | collective-permute-start | bytes 9224 | tf_op jit(solution)/shard_map/ppermute | solution.py:27
  269.9 7.2 %collective-permute-done.26 = f32[6,1,128]{2,1,0:T(1,128)S(1)} collective-permute-done((f32[6,1,128]{2,1,0:T(1,128)S(1)}, f32[6,1,128]{2,1,0:T(1,128)S(1)}, u32[]{:S(2)}, u32[]{:S(2)}) %collective-permute-start.26) | collective-permute-done | bytes 3104 | tf_op jit(solution)/shard_map/ppermute | solution.py:26
  279.1 2.4 collective-permute-start.28
  281.6 3.2 collective-permute-done.28
  288.4 4.2 %collective-permute-done.30 = f32[1,16,128]{2,1,0:T(8,128)S(1)} collective-permute-done((f32[1,16,128]{2,1,0:T(8,128)S(1)}, f32[1,16,128]{2,1,0:T(8,128)S(1)}, u32[]{:S(2)}, u32[]{:S(2)}) %collective-permute-start.30) | collective-permute-done | bytes 8224 | tf_op jit(solution)/shard_map/ppermute | solution.py:26
  294.5 3.9 %collective-permute-start.32 = (f32[6,1,128]{2,1,0:T(1,128)S(1)}, f32[6,1,128]{2,1,0:T(1,128)S(1)}, u32[]{:S(2)}, u32[]{:S(2)}) collective-permute-start(f32[6,1,128]{2,1,0:T(1,128)S(1)} %get-tuple-element.64), channel_id=1, source_target_pairs={{0,4},{4,8},{8,12},{12,16},{16,20},{20,24},{24,28},{28,32},{32,36}... | collective-permute-start | bytes 9224 | tf_op jit(solution)/shard_map/ppermute | solution.py:26
  298.4 5.2 %collective-permute-done.32 = f32[6,1,128]{2,1,0:T(1,128)S(1)} collective-permute-done((f32[6,1,128]{2,1,0:T(1,128)S(1)}, f32[6,1,128]{2,1,0:T(1,128)S(1)}, u32[]{:S(2)}, u32[]{:S(2)}) %collective-permute-start.32) | collective-permute-done | bytes 3104 | tf_op jit(solution)/shard_map/ppermute | solution.py:26
  305.6 2.4 collective-permute-start.34
  308.1 3.2 collective-permute-done.34
  314.9 4.2 %collective-permute-done.36 = f32[1,16,128]{2,1,0:T(8,128)S(1)} collective-permute-done((f32[1,16,128]{2,1,0:T(8,128)S(1)}, f32[1,16,128]{2,1,0:T(8,128)S(1)}, u32[]{:S(2)}, u32[]{:S(2)}) %collective-permute-start.36) | collective-permute-done | bytes 8224 | tf_op jit(solution)/shard_map/ppermute | solution.py:26
  321.0 3.9 %collective-permute-start.38 = (f32[6,1,128]{2,1,0:T(1,128)S(1)}, f32[6,1,128]{2,1,0:T(1,128)S(1)}, u32[]{:S(2)}, u32[]{:S(2)}) collective-permute-start(f32[6,1,128]{2,1,0:T(1,128)S(1)} %get-tuple-element.62), channel_id=1, source_target_pairs={{0,4},{4,8},{8,12},{12,16},{16,20},{20,24},{24,28},{28,32},{32,36}... | collective-permute-start | bytes 9224 | tf_op jit(solution)/shard_map/ppermute | solution.py:26
  324.9 5.2 %collective-permute-done.38 = f32[6,1,128]{2,1,0:T(1,128)S(1)} collective-permute-done((f32[6,1,128]{2,1,0:T(1,128)S(1)}, f32[6,1,128]{2,1,0:T(1,128)S(1)}, u32[]{:S(2)}, u32[]{:S(2)}) %collective-permute-start.38) | collective-permute-done | bytes 3104 | tf_op jit(solution)/shard_map/ppermute | solution.py:26
  332.1 2.4 collective-permute-start.40
  335.4 2.4 collective-permute-done.40
  (147 shorter events, 57.1 us)
Async XLA Ops:
  1.4 76.9 %collective-permute-start = (f32[2,1,16,128]{3,2,1,0:T(8,128)S(1)}, f32[2,1,16,128]{3,2,1,0:T(8,128)S(1)}, u32[]{:S(2)}, u32[]{:S(2)}) collective-permute-start(f32[2,1,16,128]{3,2,1,0:T(8,128)S(1)} %get-tuple-element.61), channel_id=1, source_target_pairs={{0,64},{64,128},{128,192},{1,65},{65,129},{129,193},{2,66},{66,130... | collective-permute-start | bytes 49160 | tf_op jit(solution)/shard_map/ppermute | solution.py:26
  2.7 75.6 %collective-permute-start.1 = (f32[2,1,16,128]{3,2,1,0:T(8,128)S(1)}, f32[2,1,16,128]{3,2,1,0:T(8,128)S(1)}, u32[]{:S(2)}, u32[]{:S(2)}) collective-permute-start(f32[2,1,16,128]{3,2,1,0:T(8,128)S(1)} %get-tuple-element.60), channel_id=1, source_target_pairs={{64,0},{128,64},{192,128},{65,1},{129,65},{193,129},{66,2},{130,66... | collective-permute-start | bytes 49160 | tf_op jit(solution)/shard_map/ppermute | solution.py:27
  7.9 114.3 %collective-permute-start.18 = (f32[1,16,128]{2,1,0:T(8,128)S(1)}, f32[1,16,128]{2,1,0:T(8,128)S(1)}, u32[]{:S(2)}, u32[]{:S(2)}) collective-permute-start(f32[1,16,128]{2,1,0:T(8,128)S(1)} %get-tuple-element.77), channel_id=1, source_target_pairs={{0,64},{64,128},{128,192},{1,65},{65,129},{129,193},{2,66},{66,130... | collective-permute-start | bytes 24584 | tf_op jit(solution)/shard_map/ppermute | solution.py:26
  9.2 132.5 %collective-permute-start.19 = (f32[1,16,128]{2,1,0:T(8,128)S(1)}, f32[1,16,128]{2,1,0:T(8,128)S(1)}, u32[]{:S(2)}, u32[]{:S(2)}) collective-permute-start(f32[1,16,128]{2,1,0:T(8,128)S(1)} %get-tuple-element.76), channel_id=1, source_target_pairs={{64,0},{128,64},{192,128},{65,1},{129,65},{193,129},{66,2},{130,66... | collective-permute-start | bytes 24584 | tf_op jit(solution)/shard_map/ppermute | solution.py:27
  37.8 36.4 %copy-start = (s32[8,32,256]{2,1,0:T(8,128)S(1)}, s32[8,32,256]{2,1,0:T(8,128)}, u32[]{:S(2)}) copy-start(s32[8,32,256]{2,1,0:T(8,128)} %param.13) | copy-start | bytes 786436
  37.8 39.8 %copy-start.4 = (f32[4]{0:T(128)S(1)}, f32[4]{0:T(128)}, u32[]{:S(2)}) copy-start(f32[4]{0:T(128)} %param.17) | copy-start | bytes 52
  37.8 40.4 %copy-start.2 = (f32[2,4,16,128]{3,2,1,0:T(8,128)S(1)}, f32[2,4,16,128]{3,2,1,0:T(8,128)}, u32[]{:S(2)}) copy-start(f32[2,4,16,128]{3,2,1,0:T(8,128)} %param.12) | copy-start | bytes 196612
  37.8 51.1 %copy-start.5 = (f32[4]{0:T(128)S(1)}, f32[4]{0:T(128)}, u32[]{:S(2)}) copy-start(f32[4]{0:T(128)} %param.16) | copy-start | bytes 52
  78.3 39.4 %collective-permute-start.3 = (f32[2,6,1,128]{3,2,1,0:T(1,128)S(1)}, f32[2,6,1,128]{3,2,1,0:T(1,128)S(1)}, u32[]{:S(2)}, u32[]{:S(2)}) collective-permute-start(f32[2,6,1,128]{3,2,1,0:T(1,128)S(1)} %get-tuple-element.51), channel_id=1, source_target_pairs={{4,0},{8,4},{12,8},{16,12},{20,16},{24,20},{28,24},{32,28},{36,32}... | collective-permute-start | bytes 18440 | tf_op jit(solution)/shard_map/ppermute | solution.py:27
  86.8 31.0 %collective-permute-start.2 = (f32[2,6,1,128]{3,2,1,0:T(1,128)S(1)}, f32[2,6,1,128]{3,2,1,0:T(1,128)S(1)}, u32[]{:S(2)}, u32[]{:S(2)}) collective-permute-start(f32[2,6,1,128]{3,2,1,0:T(1,128)S(1)} %get-tuple-element.50), channel_id=1, source_target_pairs={{0,4},{4,8},{8,12},{12,16},{16,20},{20,24},{24,28},{28,32},{32,36}... | collective-permute-start | bytes 18440 | tf_op jit(solution)/shard_map/ppermute | solution.py:26
  117.9 5.0 %collective-permute-start.5 = (f32[2,6,18,1]{3,2,1,0:T(8,128)S(1)}, f32[2,6,18,1]{3,2,1,0:T(8,128)S(1)}, u32[]{:S(2)}, u32[]{:S(2)}) collective-permute-start(f32[2,6,18,1]{3,2,1,0:T(8,128)S(1)} %get-tuple-element.49), channel_id=1, source_target_pairs={{1,0},{2,1},{3,2},{5,4},{6,5},{7,6},{9,8},{10,9},{11,10},{13,12},{... | collective-permute-start | bytes 2600 | tf_op jit(solution)/shard_map/ppermute | solution.py:27
  119.8 6.5 %collective-permute-start.4 = (f32[2,6,18,1]{3,2,1,0:T(8,128)S(1)}, f32[2,6,18,1]{3,2,1,0:T(8,128)S(1)}, u32[]{:S(2)}, u32[]{:S(2)}) collective-permute-start(f32[2,6,18,1]{3,2,1,0:T(8,128)S(1)} %get-tuple-element.48), channel_id=1, source_target_pairs={{0,1},{1,2},{2,3},{4,5},{5,6},{6,7},{8,9},{9,10},{10,11},{12,13},{... | collective-permute-start | bytes 2600 | tf_op jit(solution)/shard_map/ppermute | solution.py:26
  129.6 122.9 %copy-start.1 = (f32[4,16,128]{2,1,0:T(8,128)S(1)}, f32[4,16,128]{2,1,0:T(8,128)}, u32[]{:S(2)}) copy-start(f32[4,16,128]{2,1,0:T(8,128)} %param.19) | copy-start | bytes 98308
  130.7 207.2 %copy-start.3 = (f32[4,16,128]{2,1,0:T(8,128)S(1)}, f32[4,16,128]{2,1,0:T(8,128)}, u32[]{:S(2)}) copy-start(f32[4,16,128]{2,1,0:T(8,128)} %param.20) | copy-start | bytes 98308
  130.8 5.4 %collective-permute-start.6 = (f32[2,1,32,256]{3,2,1,0:T(8,128)S(1)}, f32[2,1,32,256]{3,2,1,0:T(8,128)S(1)}, u32[]{:S(2)}, u32[]{:S(2)}) collective-permute-start(f32[2,1,32,256]{3,2,1,0:T(8,128)S(1)} %get-tuple-element.41), channel_id=1, source_target_pairs={{64,0},{128,64},{192,128},{65,1},{129,65},{193,129},{66,2},{130,66... | collective-permute-start | bytes 196616 | tf_op jit(solution)/shard_map/ppermute | solution.py:27
  133.5 6.2 %collective-permute-start.7 = (f32[2,1,32,256]{3,2,1,0:T(8,128)S(1)}, f32[2,1,32,256]{3,2,1,0:T(8,128)S(1)}, u32[]{:S(2)}, u32[]{:S(2)}) collective-permute-start(f32[2,1,32,256]{3,2,1,0:T(8,128)S(1)} %get-tuple-element.40), channel_id=1, source_target_pairs={{0,64},{64,128},{128,192},{1,65},{65,129},{129,193},{2,66},{66,130... | collective-permute-start | bytes 196616 | tf_op jit(solution)/shard_map/ppermute | solution.py:26
  139.8 10.1 %collective-permute-start.9 = (f32[2,10,1,256]{3,0,2,1:T(2,128)S(1)}, f32[2,10,1,256]{3,0,2,1:T(2,128)S(1)}, u32[]{:S(2)}, u32[]{:S(2)}) collective-permute-start(f32[2,10,1,256]{3,0,2,1:T(2,128)S(1)} %copy.152), channel_id=1, source_target_pairs={{0,4},{4,8},{8,12},{12,16},{16,20},{20,24},{24,28},{28,32},{32,36}... | collective-permute-start | bytes 61448 | tf_op jit(solution)/shard_map/ppermute | solution.py:26
  142.4 9.0 %collective-permute-start.8 = (f32[2,10,1,256]{3,0,2,1:T(2,128)S(1)}, f32[2,10,1,256]{3,0,2,1:T(2,128)S(1)}, u32[]{:S(2)}, u32[]{:S(2)}) collective-permute-start(f32[2,10,1,256]{3,0,2,1:T(2,128)S(1)} %copy.150), channel_id=1, source_target_pairs={{4,0},{8,4},{12,8},{16,12},{20,16},{24,20},{28,24},{32,28},{36,32}... | collective-permute-start | bytes 61448 | tf_op jit(solution)/shard_map/ppermute | solution.py:27
  151.8 15.0 %collective-permute-start.10 = (f32[2,10,34,1]{3,0,2,1:T(2,128)S(1)}, f32[2,10,34,1]{3,0,2,1:T(2,128)S(1)}, u32[]{:S(2)}, u32[]{:S(2)}) collective-permute-start(f32[2,10,34,1]{3,0,2,1:T(2,128)S(1)} %get-tuple-element.32), channel_id=1, source_target_pairs={{1,0},{2,1},{3,2},{5,4},{6,5},{7,6},{9,8},{10,9},{11,10},{13,12},{... | collective-permute-start | bytes 8168 | tf_op jit(solution)/shard_map/ppermute | solution.py:27
  153.8 13.1 %collective-permute-start.11 = (f32[2,10,34,1]{3,0,2,1:T(2,128)S(1)}, f32[2,10,34,1]{3,0,2,1:T(2,128)S(1)}, u32[]{:S(2)}, u32[]{:S(2)}) collective-permute-start(f32[2,10,34,1]{3,0,2,1:T(2,128)S(1)} %get-tuple-element.33), channel_id=1, source_target_pairs={{0,1},{1,2},{2,3},{4,5},{5,6},{6,7},{8,9},{9,10},{10,11},{12,13},{... | collective-permute-start | bytes 8168 | tf_op jit(solution)/shard_map/ppermute | solution.py:26
  157.0 27.9 %collective-permute-start.21 = (f32[6,1,128]{2,1,0:T(1,128)S(1)}, f32[6,1,128]{2,1,0:T(1,128)S(1)}, u32[]{:S(2)}, u32[]{:S(2)}) collective-permute-start(f32[6,1,128]{2,1,0:T(1,128)S(1)} %get-tuple-element.69), channel_id=1, source_target_pairs={{4,0},{8,4},{12,8},{16,12},{20,16},{24,20},{28,24},{32,28},{36,32}... | collective-permute-start | bytes 9224 | tf_op jit(solution)/shard_map/ppermute | solution.py:27
  164.9 20.0 %collective-permute-start.20 = (f32[6,1,128]{2,1,0:T(1,128)S(1)}, f32[6,1,128]{2,1,0:T(1,128)S(1)}, u32[]{:S(2)}, u32[]{:S(2)}) collective-permute-start(f32[6,1,128]{2,1,0:T(1,128)S(1)} %get-tuple-element.68), channel_id=1, source_target_pairs={{0,4},{4,8},{8,12},{12,16},{16,20},{20,24},{24,28},{28,32},{32,36}... | collective-permute-start | bytes 9224 | tf_op jit(solution)/shard_map/ppermute | solution.py:26
  181.2 4.6 %collective-permute-start.12 = (f32[2,1,32,256]{3,2,1,0:T(8,128)S(1)}, f32[2,1,32,256]{3,2,1,0:T(8,128)S(1)}, u32[]{:S(2)}, u32[]{:S(2)}) collective-permute-start(f32[2,1,32,256]{3,2,1,0:T(8,128)S(1)} %get-tuple-element.39), channel_id=1, source_target_pairs={{64,0},{128,64},{192,128},{65,1},{129,65},{193,129},{66,2},{130,66... | collective-permute-start | bytes 196616 | tf_op jit(solution)/shard_map/ppermute | solution.py:27
  183.6 6.2 %collective-permute-start.13 = (f32[2,1,32,256]{3,2,1,0:T(8,128)S(1)}, f32[2,1,32,256]{3,2,1,0:T(8,128)S(1)}, u32[]{:S(2)}, u32[]{:S(2)}) collective-permute-start(f32[2,1,32,256]{3,2,1,0:T(8,128)S(1)} %get-tuple-element.38), channel_id=1, source_target_pairs={{0,64},{64,128},{128,192},{1,65},{65,129},{129,193},{2,66},{66,130... | collective-permute-start | bytes 196616 | tf_op jit(solution)/shard_map/ppermute | solution.py:26
  189.9 13.9 %collective-permute-start.15 = (f32[2,10,1,256]{3,0,2,1:T(2,128)S(1)}, f32[2,10,1,256]{3,0,2,1:T(2,128)S(1)}, u32[]{:S(2)}, u32[]{:S(2)}) collective-permute-start(f32[2,10,1,256]{3,0,2,1:T(2,128)S(1)} %copy.177), channel_id=1, source_target_pairs={{0,4},{4,8},{8,12},{12,16},{16,20},{20,24},{24,28},{28,32},{32,36}... | collective-permute-start | bytes 61448 | tf_op jit(solution)/shard_map/ppermute | solution.py:26
  191.9 18.4 %collective-permute-start.23 = (f32[6,18,1]{2,1,0:T(8,128)S(1)}, f32[6,18,1]{2,1,0:T(8,128)S(1)}, u32[]{:S(2)}, u32[]{:S(2)}) collective-permute-start(f32[6,18,1]{2,1,0:T(8,128)S(1)} %get-tuple-element.59), channel_id=1, source_target_pairs={{1,0},{2,1},{3,2},{5,4},{6,5},{7,6},{9,8},{10,9},{11,10},{13,12},{... | collective-permute-start | bytes 1304 | tf_op jit(solution)/shard_map/ppermute | solution.py:27
  193.8 16.5 %collective-permute-start.22 = (f32[6,18,1]{2,1,0:T(8,128)S(1)}, f32[6,18,1]{2,1,0:T(8,128)S(1)}, u32[]{:S(2)}, u32[]{:S(2)}) collective-permute-start(f32[6,18,1]{2,1,0:T(8,128)S(1)} %get-tuple-element.58), channel_id=1, source_target_pairs={{0,1},{1,2},{2,3},{4,5},{5,6},{6,7},{8,9},{9,10},{10,11},{12,13},{... | collective-permute-start | bytes 1304 | tf_op jit(solution)/shard_map/ppermute | solution.py:26
  196.2 9.0 %collective-permute-start.14 = (f32[2,10,1,256]{3,0,2,1:T(2,128)S(1)}, f32[2,10,1,256]{3,0,2,1:T(2,128)S(1)}, u32[]{:S(2)}, u32[]{:S(2)}) collective-permute-start(f32[2,10,1,256]{3,0,2,1:T(2,128)S(1)} %copy.178), channel_id=1, source_target_pairs={{4,0},{8,4},{12,8},{16,12},{20,16},{24,20},{28,24},{32,28},{36,32}... | collective-permute-start | bytes 61448 | tf_op jit(solution)/shard_map/ppermute | solution.py:27
  205.7 6.7 %collective-permute-start.16 = (f32[2,10,34,1]{3,0,2,1:T(2,128)S(1)}, f32[2,10,34,1]{3,0,2,1:T(2,128)S(1)}, u32[]{:S(2)}, u32[]{:S(2)}) collective-permute-start(f32[2,10,34,1]{3,0,2,1:T(2,128)S(1)} %get-tuple-element.28), channel_id=1, source_target_pairs={{1,0},{2,1},{3,2},{5,4},{6,5},{7,6},{9,8},{10,9},{11,10},{13,12},{... | collective-permute-start | bytes 8168 | tf_op jit(solution)/shard_map/ppermute | solution.py:27
  207.7 8.6 %collective-permute-start.17 = (f32[2,10,34,1]{3,0,2,1:T(2,128)S(1)}, f32[2,10,34,1]{3,0,2,1:T(2,128)S(1)}, u32[]{:S(2)}, u32[]{:S(2)}) collective-permute-start(f32[2,10,34,1]{3,0,2,1:T(2,128)S(1)} %get-tuple-element.29), channel_id=1, source_target_pairs={{0,1},{1,2},{2,3},{4,5},{5,6},{6,7},{8,9},{9,10},{10,11},{12,13},{... | collective-permute-start | bytes 8168 | tf_op jit(solution)/shard_map/ppermute | solution.py:26
  252.6 3.3 collective-permute-start.25
  254.5 5.5 %collective-permute-start.24 = (f32[1,16,128]{2,1,0:T(8,128)S(1)}, f32[1,16,128]{2,1,0:T(8,128)S(1)}, u32[]{:S(2)}, u32[]{:S(2)}) collective-permute-start(f32[1,16,128]{2,1,0:T(8,128)S(1)} %get-tuple-element.74), channel_id=1, source_target_pairs={{0,64},{64,128},{128,192},{1,65},{65,129},{129,193},{2,66},{66,130... | collective-permute-start | bytes 24584 | tf_op jit(solution)/shard_map/ppermute | solution.py:26
  260.1 9.8 %collective-permute-start.27 = (f32[6,1,128]{2,1,0:T(1,128)S(1)}, f32[6,1,128]{2,1,0:T(1,128)S(1)}, u32[]{:S(2)}, u32[]{:S(2)}) collective-permute-start(f32[6,1,128]{2,1,0:T(1,128)S(1)} %get-tuple-element.67), channel_id=1, source_target_pairs={{4,0},{8,4},{12,8},{16,12},{20,16},{24,20},{28,24},{32,28},{36,32}... | collective-permute-start | bytes 9224 | tf_op jit(solution)/shard_map/ppermute | solution.py:27
  268.0 9.1 %collective-permute-start.26 = (f32[6,1,128]{2,1,0:T(1,128)S(1)}, f32[6,1,128]{2,1,0:T(1,128)S(1)}, u32[]{:S(2)}, u32[]{:S(2)}) collective-permute-start(f32[6,1,128]{2,1,0:T(1,128)S(1)} %get-tuple-element.66), channel_id=1, source_target_pairs={{0,4},{4,8},{8,12},{12,16},{16,20},{20,24},{24,28},{28,32},{32,36}... | collective-permute-start | bytes 9224 | tf_op jit(solution)/shard_map/ppermute | solution.py:26
  277.2 4.3 %collective-permute-start.29 = (f32[6,18,1]{2,1,0:T(8,128)S(1)}, f32[6,18,1]{2,1,0:T(8,128)S(1)}, u32[]{:S(2)}, u32[]{:S(2)}) collective-permute-start(f32[6,18,1]{2,1,0:T(8,128)S(1)} %get-tuple-element.57), channel_id=1, source_target_pairs={{1,0},{2,1},{3,2},{5,4},{6,5},{7,6},{9,8},{10,9},{11,10},{13,12},{... | collective-permute-start | bytes 1304 | tf_op jit(solution)/shard_map/ppermute | solution.py:27
  279.1 5.7 %collective-permute-start.28 = (f32[6,18,1]{2,1,0:T(8,128)S(1)}, f32[6,18,1]{2,1,0:T(8,128)S(1)}, u32[]{:S(2)}, u32[]{:S(2)}) collective-permute-start(f32[6,18,1]{2,1,0:T(8,128)S(1)} %get-tuple-element.56), channel_id=1, source_target_pairs={{0,1},{1,2},{2,3},{4,5},{5,6},{6,7},{8,9},{9,10},{10,11},{12,13},{... | collective-permute-start | bytes 1304 | tf_op jit(solution)/shard_map/ppermute | solution.py:26
  285.1 3.3 collective-permute-start.31
  287.0 5.5 %collective-permute-start.30 = (f32[1,16,128]{2,1,0:T(8,128)S(1)}, f32[1,16,128]{2,1,0:T(8,128)S(1)}, u32[]{:S(2)}, u32[]{:S(2)}) collective-permute-start(f32[1,16,128]{2,1,0:T(8,128)S(1)} %get-tuple-element.72), channel_id=1, source_target_pairs={{0,64},{64,128},{128,192},{1,65},{65,129},{129,193},{2,66},{66,130... | collective-permute-start | bytes 24584 | tf_op jit(solution)/shard_map/ppermute | solution.py:26
  292.6 5.8 %collective-permute-start.33 = (f32[6,1,128]{2,1,0:T(1,128)S(1)}, f32[6,1,128]{2,1,0:T(1,128)S(1)}, u32[]{:S(2)}, u32[]{:S(2)}) collective-permute-start(f32[6,1,128]{2,1,0:T(1,128)S(1)} %get-tuple-element.65), channel_id=1, source_target_pairs={{4,0},{8,4},{12,8},{16,12},{20,16},{24,20},{28,24},{32,28},{36,32}... | collective-permute-start | bytes 9224 | tf_op jit(solution)/shard_map/ppermute | solution.py:27
  294.5 9.1 %collective-permute-start.32 = (f32[6,1,128]{2,1,0:T(1,128)S(1)}, f32[6,1,128]{2,1,0:T(1,128)S(1)}, u32[]{:S(2)}, u32[]{:S(2)}) collective-permute-start(f32[6,1,128]{2,1,0:T(1,128)S(1)} %get-tuple-element.64), channel_id=1, source_target_pairs={{0,4},{4,8},{8,12},{12,16},{16,20},{20,24},{24,28},{28,32},{32,36}... | collective-permute-start | bytes 9224 | tf_op jit(solution)/shard_map/ppermute | solution.py:26
  303.7 4.3 %collective-permute-start.35 = (f32[6,18,1]{2,1,0:T(8,128)S(1)}, f32[6,18,1]{2,1,0:T(8,128)S(1)}, u32[]{:S(2)}, u32[]{:S(2)}) collective-permute-start(f32[6,18,1]{2,1,0:T(8,128)S(1)} %get-tuple-element.55), channel_id=1, source_target_pairs={{1,0},{2,1},{3,2},{5,4},{6,5},{7,6},{9,8},{10,9},{11,10},{13,12},{... | collective-permute-start | bytes 1304 | tf_op jit(solution)/shard_map/ppermute | solution.py:27
  305.6 5.7 %collective-permute-start.34 = (f32[6,18,1]{2,1,0:T(8,128)S(1)}, f32[6,18,1]{2,1,0:T(8,128)S(1)}, u32[]{:S(2)}, u32[]{:S(2)}) collective-permute-start(f32[6,18,1]{2,1,0:T(8,128)S(1)} %get-tuple-element.54), channel_id=1, source_target_pairs={{0,1},{1,2},{2,3},{4,5},{5,6},{6,7},{8,9},{9,10},{10,11},{12,13},{... | collective-permute-start | bytes 1304 | tf_op jit(solution)/shard_map/ppermute | solution.py:26
  311.6 3.3 collective-permute-start.37
  313.5 5.5 %collective-permute-start.36 = (f32[1,16,128]{2,1,0:T(8,128)S(1)}, f32[1,16,128]{2,1,0:T(8,128)S(1)}, u32[]{:S(2)}, u32[]{:S(2)}) collective-permute-start(f32[1,16,128]{2,1,0:T(8,128)S(1)} %get-tuple-element.70), channel_id=1, source_target_pairs={{0,64},{64,128},{128,192},{1,65},{65,129},{129,193},{2,66},{66,130... | collective-permute-start | bytes 24584 | tf_op jit(solution)/shard_map/ppermute | solution.py:26
  319.1 5.8 %collective-permute-start.39 = (f32[6,1,128]{2,1,0:T(1,128)S(1)}, f32[6,1,128]{2,1,0:T(1,128)S(1)}, u32[]{:S(2)}, u32[]{:S(2)}) collective-permute-start(f32[6,1,128]{2,1,0:T(1,128)S(1)} %get-tuple-element.63), channel_id=1, source_target_pairs={{4,0},{8,4},{12,8},{16,12},{20,16},{24,20},{28,24},{32,28},{36,32}... | collective-permute-start | bytes 9224 | tf_op jit(solution)/shard_map/ppermute | solution.py:27
  321.0 9.1 %collective-permute-start.38 = (f32[6,1,128]{2,1,0:T(1,128)S(1)}, f32[6,1,128]{2,1,0:T(1,128)S(1)}, u32[]{:S(2)}, u32[]{:S(2)}) collective-permute-start(f32[6,1,128]{2,1,0:T(1,128)S(1)} %get-tuple-element.62), channel_id=1, source_target_pairs={{0,4},{4,8},{8,12},{12,16},{16,20},{20,24},{24,28},{28,32},{32,36}... | collective-permute-start | bytes 9224 | tf_op jit(solution)/shard_map/ppermute | solution.py:26
  330.2 5.2 %collective-permute-start.41 = (f32[6,18,1]{2,1,0:T(8,128)S(1)}, f32[6,18,1]{2,1,0:T(8,128)S(1)}, u32[]{:S(2)}, u32[]{:S(2)}) collective-permute-start(f32[6,18,1]{2,1,0:T(8,128)S(1)} %get-tuple-element.53), channel_id=1, source_target_pairs={{1,0},{2,1},{3,2},{5,4},{6,5},{7,6},{9,8},{10,9},{11,10},{13,12},{... | collective-permute-start | bytes 1304 | tf_op jit(solution)/shard_map/ppermute | solution.py:27
  332.1 5.7 %collective-permute-start.40 = (f32[6,18,1]{2,1,0:T(8,128)S(1)}, f32[6,18,1]{2,1,0:T(8,128)S(1)}, u32[]{:S(2)}, u32[]{:S(2)}) collective-permute-start(f32[6,18,1]{2,1,0:T(8,128)S(1)} %get-tuple-element.52), channel_id=1, source_target_pairs={{0,1},{1,2},{2,3},{4,5},{5,6},{6,7},{8,9},{9,10},{10,11},{12,13},{... | collective-permute-start | bytes 1304 | tf_op jit(solution)/shard_map/ppermute | solution.py:26
where the time goes:
time: 341 us; the launch traced here: 339 us
  starting transfers between devices  120 us (35%)
  local copies, waits for them, and re-layouts  105 us (31%)
  waiting for transfers between devices  56.8 us (17%)
  other arithmetic  54.7 us (16%)
    ppermute x21, starting transfers between devices, with_halo(): after = lax.ppermute(first, axis, down)  76.6 us
    another operation x4, local copies, waits for them, and re-layouts, on_device(): coarsened_volumes = restrict(jnp.stack([power, perf_cells]))  56.1 us
    ppermute x21, waiting for transfers between devices, with_halo(): before = lax.ppermute(last, axis, up)  53.8 us
    ppermute x21, starting transfers between devices, with_halo(): before = lax.ppermute(last, axis, up)  43.7 us
    slice x1, local copies, waits for them, and re-layouts, jacobi(): resid_imag = source[1] - apply_imag  36.4 us
    unnamed x3, other arithmetic  19.9 us
    another operation x4, other arithmetic, jacobi(): return jnp.stack([new_real, new_imag])  13.4 us
  transfers between devices with their start and end apart: 42, of which 16 were waited for; matrix products, arithmetic and copies ran while one was open for 36% of the time, Pallas kernels for 0%

commit v1 on v0

v1 whole, which is shorter than its diff:
```python
import jax
import jax.numpy as jnp
from jax import lax
from jax.experimental import pallas as pl
from jax.experimental.pallas import tpu as pltpu
from jax.sharding import PartitionSpec as P

F32 = jnp.float32
BF16 = jnp.bfloat16

RELAXATION = 0.8
DAMPING_SHIFT = 0.5
DIFFUSION = 0.15
HEATING = 0.25
LN_PREFACTOR = 226.78
ENERGY_BARRIER = 75535.0
CORE_WARMTH = 310.15

FX, CX, LX, TX, QX = 12, 10, 8, 12, 10
XB_CODE, XB_COARSE, XB_THERM, XB = 128, 160, 192, 256
YB_CODE, YB_COARSE, YB_THERM, YB = 192, 272, 336, 384
WIDE = 2 * FX * 48 + CX * 48
N_CODE = 2 * FX * 48
N_COARSE, N_THETA, N_PERF, NARROW = 0, 512, 800, 1056
GROUPS = 16
ZB = (WIDE + NARROW) // GROUPS


def vmem():
    return pl.BlockSpec(memory_space=pltpu.VMEM)


def smem():
    return pl.BlockSpec(memory_space=pltpu.SMEM)


def exchange(up, down, axis):
    n = lax.axis_size(axis)
    ahead = [(i, (i + 1) % n) for i in range(n)]
    back = [(j, i) for i, j in ahead]
    return lax.ppermute(up, axis, ahead), lax.ppermute(down, axis, back)


def exact_dot(values, weights):
    high = values.astype(BF16)
    rest = values - high.astype(F32)
    mid = rest.astype(BF16)
    low = (rest - mid.astype(F32)).astype(BF16)
    total = jnp.dot(high, weights, preferred_element_type=F32)
    total = total + jnp.dot(mid, weights, preferred_element_type=F32)
    return total + jnp.dot(low, weights, preferred_element_type=F32)


def iota(shape, dim):
    return lax.broadcasted_iota(jnp.int32, shape, dim)


def pick(codes, entries):
    value = jnp.where(codes == 0.0, entries[0], entries[1])
    value = jnp.where(codes == 2.0, entries[2], value)
    return jnp.where(codes == 3.0, entries[3], value)


def pack_x(wash, it, co, codes, theta, up, down, perf, pool):
    lane, col = iota((256, 128), 0), iota((256, 128), 1)
    pairs = jnp.where(lane // 2 == col, 1.0, 0.0).astype(BF16)
    entries = [wash[k] for k in range(4)]
    for i in range(4):
        both = pick(codes[2 * i].astype(F32), entries) + pick(codes[2 * i + 1].astype(F32), entries)
        for half in range(2):
            pool[half, i * 32 : i * 32 + 32, :] = both[:, half * 128 : half * 128 + 128]
    rows = jnp.concatenate([pool[h, pl.ds(0, 64, 2), :] + pool[h, pl.ds(1, 64, 2), :] for h in range(2)], axis=1)
    washed = exact_dot(rows, pairs) * 0.125
    for i in range(4):
        perf[i] = washed[i * 16 : i * 16 + 16]
    for ref, fine, coarse in ((up, 6, 2), (down, 0, 0)):
        for c in range(2):
            for k in range(2):
                ref[pl.ds((c * 2 + k) * 32, 32), :] = it[c, fine + k]
        ref[pl.ds(XB_CODE, 32), :] = codes[7 if fine else 0].astype(F32)
        for k in range(2):
            for c in range(2):
                ref[pl.ds(XB_COARSE + 16 * k, 16), pl.ds(128 * c, 128)] = co[c, coarse + k]
        for i in range(4):
            ref[pl.ds(XB_THERM + 16 * i, 16), pl.ds(0, 128)] = theta[i]
            ref[pl.ds(XB_THERM + 16 * i, 16), pl.ds(128, 128)] = washed[i * 16 : i * 16 + 16]


class Columns:
    def __init__(self, it, co, codes, theta, perf, before, after):
        self.it, self.co, self.codes, self.theta, self.perf = it, co, codes, theta, perf
        self.before, self.after = before, after

    def iterate(self, c, f, rows):
        at, n = rows
        if 2 <= f < 10:
            return self.it[c, f - 2, pl.ds(at, n), :]
        ref, k = (self.before, f) if f < 2 else (self.after, f - 10)
        return ref[pl.ds((c * 2 + k) * 32 + at, n), :]

    def code(self, f, rows):
        at, n = rows
        if 1 <= f < 9:
            return self.codes[f - 1, pl.ds(at, n), :].astype(F32)
        return (self.before if f < 1 else self.after)[pl.ds(XB_CODE + at, n), :]

    def coarse(self, c, f, rows):
        at, n = rows
        if 2 <= f < 6:
            return self.co[c, f - 2, pl.ds(at, n), :]
        ref, k = (self.before, f) if f < 2 else (self.after, f - 6)
        return ref[pl.ds(XB_COARSE + 16 * k + at, n), pl.ds(128 * c, 128)]

    def warm(self, f, rows):
        at, n = rows
        if 4 <= f < 8:
            return self.theta[f - 4, pl.ds(at, n), :]
        ref, k = (self.before, f) if f < 4 else (self.after, f - 8)
        return ref[pl.ds(XB_THERM + 16 * k + at, n), pl.ds(0, 128)]

    def wash(self, f, rows):
        at, n = rows
        if 3 <= f < 7:
            return self.perf[f - 3, pl.ds(at, n), :]
        ref, k = (self.before, f + 1) if f < 3 else (self.after, f - 7)
        return ref[pl.ds(XB_THERM + 16 * k + at, n), pl.ds(128, 128)]


def pack_y(it, co, codes, theta, perf, before, after, up, down):
    block = Columns(it, co, codes, theta, perf, before, after)
    for ref, last in ((up, True), (down, False)):
        fine, coarse, warm = ((24, 8), (8, 8), (12, 4)) if last else ((0, 8), (0, 8), (0, 4))
        for c in range(2):
            for f in range(FX):
                ref[pl.ds((c * FX + f) * 8, 8), :] = block.iterate(c, f, fine)
        for f in range(CX):
            ref[pl.ds(YB_CODE + f * 8, 8), :] = block.code(f, fine)
        for f in range(LX):
            for c in range(2):
                ref[pl.ds(YB_COARSE + f * 8, 8), pl.ds(128 * c, 128)] = block.coarse(c, f, coarse)
        for f in range(TX):
            ref[pl.ds(YB_THERM + f * 4, 4), pl.ds(0, 128)] = block.warm(f, warm)
            wash = block.wash(f - 1, warm) if 1 <= f < 11 else jnp.zeros((4, 128), F32)
            ref[pl.ds(YB_THERM + f * 4, 4), pl.ds(128, 128)] = wash


def rows_of(wide, narrow, start, count, half):
    parts = []
    if start < WIDE:
        n = min(count, WIDE - start)
        parts.append(wide[pl.ds(start, n), pl.ds(128 * half, 128)])
        start, count = start + n, count - n
    if count:
        parts.append(narrow[pl.ds(start - WIDE, count), :])
    return parts[0] if len(parts) == 1 else jnp.concatenate(parts, axis=0)


def pack_z(it, co, codes, theta, perf, before, after, below, above, wide, narrow, up, down):
    block = Columns(it, co, codes, theta, perf, before, after)
    for c in range(2):
        for f in range(FX):
            at, k = (c * FX + f) * 48, (c * FX + f) * 8
            wide[pl.ds(at, 32), :] = block.iterate(c, f, (0, 32))
            wide[pl.ds(at + 32, 8), :] = above[pl.ds(k, 8), :]
            wide[pl.ds(at + 40, 8), :] = below[pl.ds(k, 8), :]
    for f in range(CX):
        at, k = N_CODE + f * 48, YB_CODE + f * 8
        wide[pl.ds(at, 32), :] = block.code(f, (0, 32))
        wide[pl.ds(at + 32, 8), :] = above[pl.ds(k, 8), :]
        wide[pl.ds(at + 40, 8), :] = below[pl.ds(k, 8), :]
    row = iota((8, 128), 0)
    for c in range(2):
        for f in range(LX):
            at, k, half = N_COARSE + (c * LX + f) * 32, YB_COARSE + f * 8, pl.ds(128 * c, 128)
            over, under = above[pl.ds(k, 8), half], below[pl.ds(k, 8), half]
            narrow[pl.ds(at, 16), :] = block.coarse(c, f, (0, 16))
            narrow[pl.ds(at + 16, 8), :] = jnp.where(row < 4, over, under)
            far = jnp.where(row == 1, jnp.broadcast_to(over[4:5], (8, 128)), 0.0)
            narrow[pl.ds(at + 24, 8), :] = jnp.where(row == 0, jnp.broadcast_to(under[3:4], (8, 128)), far)
    for f in range(TX):
        at, k = N_THETA + f * 24, YB_THERM + f * 4
        narrow[pl.ds(at, 16), :] = block.warm(f, (0, 16))
        narrow[pl.ds(at + 16, 4), :] = above[pl.ds(k, 4), pl.ds(0, 128)]
        narrow[pl.ds(at + 20, 4), :] = below[pl.ds(k, 4), pl.ds(0, 128)]
    for f in range(QX):
        at, k = N_PERF + f * 24, YB_THERM + (f + 1) * 4
        narrow[pl.ds(at, 16), :] = block.wash(f, (0, 16))
        narrow[pl.ds(at + 16, 4), :] = above[pl.ds(k, 4), pl.ds(128, 128)]
        narrow[pl.ds(at + 20, 4), :] = below[pl.ds(k, 4), pl.ds(128, 128)]
    narrow[pl.ds(N_PERF + QX * 24, NARROW - N_PERF - QX * 24), :] = jnp.zeros((NARROW - N_PERF - QX * 24, 128), F32)
    lane = iota((ZB, 128), 1) // 8
    for ref, half, shift in ((up, 1, 8), (down, 0, 0)):
        packed = None
        for g in range(GROUPS):
            part = rows_of(wide, narrow, g * ZB, ZB, half)
            turn = (8 * g + shift) % 128
            part = pltpu.roll(part, turn, 1) if turn else part
            packed = part if packed is None else jnp.where(lane == g, part, packed)
        ref[...] = packed


def sources(coord, loc_s, exc_s, loc, field, spread, gather):
    field[...] = jnp.zeros(field.shape, F32)
    first = loc[0:1, :] - coord[0] * 8
    second = loc[1:2, :] - coord[1] * 32
    third = loc[2:3, :] - coord[2] * 256
    near = (first >= -1) & (first < 9) & (second >= -7) & (second < 39) & (third >= -7) & (third < 263)
    order = iota((1, 1024), 1)
    lane = iota((1, 384), 1)

    def place(state):
        e, keys = state
        x = loc_s[0, e] - coord[0] * 8 + 1
        y = loc_s[1, e] - coord[1] * 32
        z = loc_s[2, e] - coord[2] * 256
        y = jnp.where(y < 0, y + 48, y)
        z = jnp.where(z < 0, z + 384, z)
        for c in range(2):
            field[c, x, pl.ds(y, 1), :] += jnp.where(lane == z, exc_s[c, e], 0.0)
        keys = jnp.where(order == e, 1024, keys)
        return jnp.min(keys), keys

    keys = jnp.where(near, order, 1024)
    lax.while_loop(lambda state: state[0] < 1024, place, (jnp.min(keys), keys))

    k, f = iota((256, 384), 0), iota((256, 384), 1)
    cell = jnp.where(f < 320, f, f - 384)
    centre = cell >> 1
    beside = centre + jnp.where((cell & 1) == 1, 1, -1)
    weight = jnp.where(k == (centre & 255), 0.75, jnp.where(k == (beside & 255), 0.25, 0.0))
    spread[...] = weight.astype(BF16)
    f, k = iota((384, 256), 0), iota((384, 256), 1)
    cell = jnp.where(f < 320, f, f - 384)
    gather[...] = jnp.where(k == ((cell >> 1) & 255), 1.0, 0.0).astype(BF16)


def smooth(coord, wave_t, damp_t, wide, narrow, left, right, source, spread, gather,
           out, power, up, down, tiles, halo, grown, fine, first, second, gain_r, gain_i, pool):
    lane = iota((ZB, 128), 1)
    for g in range(GROUPS):
        turn = (128 - 8 * g) % 128
        after = pltpu.roll(right[...], turn, 1) if turn else right[...]
        turn = (120 - 8 * g) % 128
        before = pltpu.roll(left[...], turn, 1) if turn else left[...]
        halo[pl.ds(g * ZB, ZB), :] = jnp.where(lane < 8, after, jnp.where(lane >= 120, before, 0.0))
    tiles[...] = halo[pl.ds(WIDE + N_THETA, NARROW - N_THETA), :]

    def flag(test):
        return jnp.where(test, 1.0, 0.0)

    x_before, x_after = flag(coord[0] > 0), flag(coord[0] < 3)
    y_before, y_after = flag(coord[1] > 0), flag(coord[1] < 15)
    z_before, z_after = flag(coord[2] > 0), flag(coord[2] < 3)

    row, col = iota((32, 256), 0), iota((32, 256), 1)
    y_ok = jnp.where(row < 16, 1.0, jnp.where((row < 20) | (row == 25), y_after, y_before))
    z_ok = jnp.where(col < 128, 1.0, jnp.where(col < 192, z_after, z_before))
    inside = y_ok * z_ok
    row = iota((24, 256), 0)
    for c in range(2):
        for f in range(LX):
            at = N_COARSE + (c * LX + f) * 32
            cells = jnp.concatenate([narrow[pl.ds(at, 32), :], halo[pl.ds(WIDE + at, 32), :]], axis=1)
            x_ok = x_before if f < 2 else x_after if f >= 6 else None
            cells = cells * (inside if x_ok is None else inside * x_ok)
            centre = cells[0:24]
            lower = jnp.where(row == 20, jnp.broadcast_to(cells[24:25], (24, 256)), pltpu.roll(centre, 1, 0))
            upper = jnp.where(row == 19, jnp.broadcast_to(cells[25:26], (24, 256)), pltpu.roll(centre, 23, 0))
            even = 0.75 * centre + 0.25 * lower
            odd = 0.75 * centre + 0.25 * upper
            for half in range(2):
                to = (c * LX + f) * 48
                grown[half, pl.ds(to, 24, 2), :] = even[:, half * 128 : half * 128 + 128]
                grown[half, pl.ds(to + 1, 24, 2), :] = odd[:, half * 128 : half * 128 + 128]
    fine[...] = exact_dot(jnp.concatenate([grown[0], grown[1]], axis=1), spread[...])

    row, col = iota((48, 384), 0), iota((48, 384), 1)
    y_ok = jnp.where(row < 32, 1.0, jnp.where(row < 40, y_after, y_before))
    z_ok = jnp.where(col < 256, 1.0, jnp.where(col < 320, z_after, z_before))
    inside = y_ok * z_ok
    for c in range(2):
        for f in range(FX):
            at = (c * FX + f) * 48
            start = jnp.concatenate([wide[pl.ds(at, 48), :], halo[pl.ds(at, 48), :]], axis=1)
            near = c * LX + f // 2 + 1
            far = near + (1 if f % 2 else -1)
            grow = 0.75 * fine[pl.ds(near * 48, 48), :] + 0.25 * fine[pl.ds(far * 48, 48), :]
            x_ok = x_before if f < 2 else x_after if f >= 10 else None
            first[c, f] = (start + grow) * (inside if x_ok is None else inside * x_ok)

    gains_r, gains_i, damps = [], [], []
    for t in range(4):
        speed = jnp.full((8, 128), wave_t[t], F32)
        damp = jnp.full((8, 128), damp_t[t], F32)
        wave = 1.0 / (speed * speed)
        diag_r = 6.0 - wave
        diag_i = DAMPING_SHIFT * wave + damp
        modulus = diag_r * diag_r + diag_i * diag_i
        gains_r.append((RELAXATION * diag_r / modulus)[0:1, 0:1])
        gains_i.append((RELAXATION * diag_i / modulus)[0:1, 0:1])
        damps.append(damp_t[t])

    def step(cells, at, drive_r, drive_i, g_r, g_i):
        sums = []
        for c, drive in ((0, drive_r), (1, drive_i)):
            mid = cells[c, at]
            total = cells[c, at - 1] + cells[c, at + 1] + drive
            total = total + pltpu.roll(mid, 1, 0) + pltpu.roll(mid, 47, 0)
            sums.append((mid, total + pltpu.roll(mid, 1, 1) + pltpu.roll(mid, 383, 1)))
        (mid_r, sum_r), (mid_i, sum_i) = sums
        keep = 1.0 - RELAXATION
        return keep * mid_r + (g_r * sum_r + g_i * sum_i), keep * mid_i + (g_r * sum_i - g_i * sum_r)

    def classes(f):
        at = N_CODE + f * 48
        return jnp.concatenate([wide[pl.ds(at, 48), :], halo[pl.ds(at, 48), :]], axis=1)

    for f in range(CX):
        codes = classes(f)
        x_ok = x_before if f < 1 else x_after if f >= 9 else None
        ok = inside if x_ok is None else inside * x_ok
        g_r = pick(codes, gains_r) * ok
        g_i = pick(codes, gains_i) * ok
        gain_r[f], gain_i[f] = g_r, g_i
        second[0, f], second[1, f] = step(first, f + 1, source[0, f], source[1, f], g_r, g_i)

    for i in range(4):
        heat = None
        for f in (2 * i, 2 * i + 1):
            new_r, new_i = step(second, f + 1, source[0, f + 1], source[1, f + 1], gain_r[f + 1], gain_i[f + 1])
            out[0, f] = new_r[0:32, 0:256]
            out[1, f] = new_i[0:32, 0:256]
            layer = pick(classes(f + 1), damps) * (new_r * new_r + new_i * new_i)
            heat = layer if heat is None else heat + layer
        for third in range(3):
            pool[third, pl.ds(i * 48, 48), :] = heat[:, third * 128 : third * 128 + 128]
    sums = jnp.concatenate([pool[t, pl.ds(0, 96, 2), :] + pool[t, pl.ds(1, 96, 2), :] for t in range(3)], axis=1)
    sums = exact_dot(sums, gather[...]) * 0.125
    for i in range(4):
        power[i] = sums[i * 24 : i * 24 + 24]
        if i >= 1:
            up[i - 1] = sums[i * 24 : i * 24 + 24]
        if i < 3:
            down[i] = sums[i * 24 : i * 24 + 24]


def bioheat(coord, narrow, tiles, power, before, after, injury, warm_out, dose_out, now, later):
    def flag(test):
        return jnp.where(test, 1.0, 0.0)

    x_before, x_after = flag(coord[0] > 0), flag(coord[0] < 3)
    row, col = iota((24, 256), 0), iota((24, 256), 1)
    y_ok = jnp.where(row < 16, 1.0, jnp.where(row < 20, flag(coord[1] < 15), flag(coord[1] > 0)))
    z_ok = jnp.where(col < 128, 1.0, jnp.where(col < 192, flag(coord[2] < 3), flag(coord[2] > 0)))
    inside = y_ok * z_ok
    edge = [inside * (x_before if f < 4 else x_after) if not 4 <= f < 8 else inside for f in range(TX)]

    def extended(base, f):
        at = base + f * 24
        return jnp.concatenate([narrow[pl.ds(at, 24), :], tiles[pl.ds(at - N_THETA, 24), :]], axis=1)

    for f in range(TX):
        now[f] = extended(N_THETA, f) * edge[f]
    dose = [injury[i] for i in range(4)]
    state, other = now, later
    for turn in range(4):
        for f in range(1 + turn, TX - 1 - turn):
            mid = state[f]
            beside = state[f - 1] + state[f + 1]
            beside = beside + pltpu.roll(mid, 1, 0) + pltpu.roll(mid, 23, 0)
            beside = beside + pltpu.roll(mid, 1, 1) + pltpu.roll(mid, 255, 1)
            heat = power[f - 4] if 4 <= f < 8 else before[f - 1] if f < 4 else after[f - 8]
            wash = extended(N_PERF, f - 1)
            new = mid + DIFFUSION * (beside - 6.0 * mid) - wash * mid + HEATING * heat
            other[f] = new * edge[f]
            if 4 <= f < 8:
                own = new[0:16, 0:128]
                dose[f - 4] = dose[f - 4] + jnp.exp(LN_PREFACTOR - ENERGY_BARRIER / (CORE_WARMTH + own))
                if turn == 3:
                    warm_out[f - 4] = own
        state, other = other, state
    for i in range(4):
        dose_out[i] = jnp.log(dose[i])


def shaped(*shape, dtype=F32):
    return jax.ShapeDtypeStruct(shape, dtype)


def call(kernel, name, in_specs, outs, scratch=(), cost=2000):
    return pl.pallas_call(
        kernel,
        name=name,
        out_shape=tuple(outs),
        in_specs=in_specs,
        out_specs=tuple(vmem() for _ in outs),
        scratch_shapes=list(scratch),
        cost_estimate=pl.CostEstimate(flops=cost * 1000, bytes_accessed=cost * 1000, transcendentals=0),
        compiler_params=pltpu.CompilerParams(vmem_limit_bytes=24 * 1024 * 1024),
    )


def on_device(
    acoustic_iterate,
    coarse_update,
    class_codes_volume,
    element_location,
    element_excitation,
    class_wavespeed,
    class_damping,
    washout_fraction,
    thermal_excess,
    injury_integral,
):
    it, co, codes, theta = acoustic_iterate, coarse_update, class_codes_volume, thermal_excess
    coord = jnp.stack([lax.axis_index("gx"), lax.axis_index("gy"), lax.axis_index("gz")]).astype(jnp.int32)
    loc = element_location.T

    up, down, perf = call(
        pack_x, "pack_x", [smem()] + [vmem()] * 4,
        [shaped(XB, 256), shaped(XB, 256), shaped(4, 16, 128)],
        [pltpu.VMEM((2, 128, 128), F32)],
    )(washout_fraction, it, co, codes, theta)
    before, after = exchange(up, down, "gx")

    field, spread, gather = call(
        sources, "sources", [smem(), smem(), smem(), vmem()],
        [shaped(2, CX, 48, 384), shaped(256, 384, dtype=BF16), shaped(384, 256, dtype=BF16)], cost=8000,
    )(coord, loc, element_excitation, loc)

    up, down = call(pack_y, "pack_y", [vmem()] * 7, [shaped(YB, 256), shaped(YB, 256)])(
        it, co, codes, theta, perf, before, after
    )
    below, above = exchange(up, down, "gy")

    wide, narrow, up, down = call(
        pack_z, "pack_z", [vmem()] * 9,
        [shaped(WIDE, 256), shaped(NARROW, 128), shaped(ZB, 128), shaped(ZB, 128)],
    )(it, co, codes, theta, perf, before, after, below, above)
    left, right = exchange(up, down, "gz")

    pressure, power, up, down, tiles = call(
        smooth, "smooth", [smem()] * 3 + [vmem()] * 7,
        [
            shaped(2, 8, 32, 256),
            shaped(4, 24, 256),
            shaped(3, 24, 256),
            shaped(3, 24, 256),
            shaped(NARROW - N_THETA, 128),
        ],
        [
            pltpu.VMEM((WIDE + NARROW, 128), F32),
            pltpu.VMEM((2, 2 * LX * 48, 128), F32),
            pltpu.VMEM((2 * LX * 48, 384), F32),
            pltpu.VMEM((2, FX, 48, 384), F32),
            pltpu.VMEM((2, CX, 48, 384), F32),
            pltpu.VMEM((CX, 48, 384), F32),
            pltpu.VMEM((CX, 48, 384), F32),
            pltpu.VMEM((3, 192, 128), F32),
        ],
    )(coord, class_wavespeed, class_damping, wide, narrow, left, right, field, spread, gather)
    before, after = exchange(up, down, "gx")

    warmth, dose = call(
        bioheat, "bioheat", [smem()] + [vmem()] * 6,
        [shaped(4, 16, 128), shaped(4, 16, 128)],
        [pltpu.VMEM((TX, 24, 256), F32), pltpu.VMEM((TX, 24, 256), F32)],
    )(coord, narrow, tiles, power, before, after, injury_integral)
    return pressure, warmth, dose


def solution(mesh):
    placed = (
        P(None, "gx", "gy", "gz"),
        P(None, "gx", "gy", "gz"),
        P("gx", "gy", "gz"),
        P(),
        P(),
        P(),
        P(),
        P(),
        P("gx", "gy", "gz"),
        P("gx", "gy", "gz"),
    )
    return jax.shard_map(
        on_device,
        mesh=mesh,
        in_specs=placed,
        out_specs=(P(None, "gx", "gy", "gz"), P("gx", "gy", "gz"), P("gx", "gy", "gz")),
        check_vma=False,
    )
```

time: 341 us -> 54.8 us (0.16)
  the two profiles are of different devices: /device:TPU:30 before, /device:TPU:6 now
where the time goes in v1:
time: 54.8 us; the launch traced here: 54.5 us
  waiting for transfers between devices  20 us (36%)
  starting transfers between devices  14.4 us (26%)
  Pallas kernels  11.4 us (21%)
  local copies, waits for them, and re-layouts  7.86 us (14%)
  between operations  0.76 us (1%)
    ppermute x8, waiting for transfers between devices, exchange(): return (lax.ppermute(up, axis, ahead), lax.ppermute(down, axis, back))  20 us
    ppermute x8, starting transfers between devices, exchange(): return (lax.ppermute(up, axis, ahead), lax.ppermute(down, axis, back))  14.4 us
    unnamed x36, local copies, waits for them, and re-layouts  7.86 us
    pallas_call x1, Pallas kernels, on_device(): call(smooth, 'smooth', [smem()] * 3 + [vmem()] * 7, [shaped(2, 8, 32, 256...  5.15 us
    pallas_call x1, Pallas kernels, on_device(): call(sources, 'sources', [smem(), smem(), smem(), vmem()], [shaped(2, CX,...  2.92 us
    pallas_call x1, Pallas kernels, on_device(): call(bioheat, 'bioheat', [smem()] + [vmem()] * 6, [shaped(4, 16, 128), sh...  1.67 us
  transfers between devices with their start and end apart: 8, of which 5 were waited for; matrix products, arithmetic and copies ran while one was open for 0% of the time, Pallas kernels for 5%

profile of v1, /device:TPU:6, one launch (start us, length us, event | category | flops | bytes accessed | tf_op | source)
XLA Modules:
  0.0 54.5 jit_solution(13280714009258641508)
XLA Ops:
  0.6 0.0 copy-start
  0.6 1.0 %copy-done = f32[2,8,32,256]{3,2,1,0:T(8,128)S(1)} copy-done((f32[2,8,32,256]{3,2,1,0:T(8,128)S(1)}, f32[2,8,32,256]{3,2,1,0:T(8,128)}, u32[]{:S(2)}) %copy-start) | copy-done | bytes 524312
  1.7 0.0 copy-start.3
  1.7 0.9 %copy-done.3 = s32[8,32,256]{2,1,0:T(8,128)S(1)} copy-done((s32[8,32,256]{2,1,0:T(8,128)S(1)}, s32[8,32,256]{2,1,0:T(8,128)}, u32[]{:S(2)}) %copy-start.3) | copy-done | bytes 262168
  2.6 0.0 copy-start.6
  2.6 0.8 %copy-done.6 = f32[2,4,16,128]{3,2,1,0:T(8,128)S(1)} copy-done((f32[2,4,16,128]{3,2,1,0:T(8,128)S(1)}, f32[2,4,16,128]{3,2,1,0:T(8,128)}, u32[]{:S(2)}) %copy-start.6) | copy-done | bytes 65560
  3.5 0.0 copy-start.9
  3.5 0.8 %copy-done.9 = f32[4,16,128]{2,1,0:T(8,128)S(1)} copy-done((f32[4,16,128]{2,1,0:T(8,128)S(1)}, f32[4,16,128]{2,1,0:T(8,128)}, u32[]{:S(2)}) %copy-start.9) | copy-done | bytes 32792
  4.2 0.0 copy-start.15
  4.2 0.7 %copy-done.15 = f32[4]{0:T(128)S(1)} copy-done((f32[4]{0:T(128)S(1)}, f32[4]{0:T(128)}, u32[]{:S(2)}) %copy-start.15) | copy-done | bytes 40
  4.9 0.0 copy-start.2
  4.9 0.8 %pack_x.1 = (f32[256,256]{1,0:T(8,128)S(1)}, f32[256,256]{1,0:T(8,128)S(1)}, f32[4,16,128]{2,1,0:T(8,128)S(1)}) custom-call(f32[4]{0:T(128)S(1)} %copy-done.15, f32[2,8,32,256]{3,2,1,0:T(8,128)S(1)} %copy-done, f32[2,4,16,128]{3,2,1,0:T(8,128)S(1)} %copy-done.6, s32[8,32,256]{2,1,0:T(8,128)S(1)} %copy-done.3, f32[4,16,128]{2,1,0:T(8,128)S(1)} %copy-done.9), custom_call_target="tpu_custom_call" | custom-call | flops 2000000 | bytes 2000000 | tf_op jit(solution)/shard_map/pack_x/pallas_call | solution.py:419
  5.7 2.3 %collective-permute-start = (f32[256,256]{1,0:T(8,128)S(1)}, f32[256,256]{1,0:T(8,128)S(1)}, u32[]{:S(2)}, u32[]{:S(2)}) collective-permute-start(f32[256,256]{1,0:T(8,128)S(1)} %get-tuple-element.23), channel_id=1, source_target_pairs={{0,64},{64,128},{128,192},{192,0},{1,65},{65,129},{129,193},{193,1... | collective-permute-start | bytes 786440 | tf_op jit(solution)/shard_map/ppermute | solution.py:41
  8.0 0.0 collective-permute-start.1
  8.0 5.8 %collective-permute-done.before = f32[256,256]{1,0:T(8,128)S(1)} collective-permute-done((f32[256,256]{1,0:T(8,128)S(1)}, f32[256,256]{1,0:T(8,128)S(1)}, u32[]{:S(2)}, u32[]{:S(2)}) %collective-permute-start) | collective-permute-done | bytes 262176 | tf_op jit(solution)/shard_map/ppermute | solution.py:41
  13.8 1.8 %collective-permute-done.1.after = f32[256,256]{1,0:T(8,128)S(1)} collective-permute-done((f32[256,256]{1,0:T(8,128)S(1)}, f32[256,256]{1,0:T(8,128)S(1)}, u32[]{:S(2)}, u32[]{:S(2)}) %collective-permute-start.1) | collective-permute-done | bytes 262176 | tf_op jit(solution)/shard_map/ppermute | solution.py:41
  15.6 1.0 %copy-done.1 = f32[2,8,32,256]{3,2,1,0:T(8,128)S(1)} copy-done((f32[2,8,32,256]{3,2,1,0:T(8,128)S(1)}, f32[2,8,32,256]{3,2,1,0:T(8,128)}, u32[]{:S(2)}) %copy-start.1) | copy-done | bytes 524312
  16.6 0.9 %copy-done.4 = s32[8,32,256]{2,1,0:T(8,128)S(1)} copy-done((s32[8,32,256]{2,1,0:T(8,128)S(1)}, s32[8,32,256]{2,1,0:T(8,128)}, u32[]{:S(2)}) %copy-start.4) | copy-done | bytes 262168
  17.5 0.8 %copy-done.7 = f32[2,4,16,128]{3,2,1,0:T(8,128)S(1)} copy-done((f32[2,4,16,128]{3,2,1,0:T(8,128)S(1)}, f32[2,4,16,128]{3,2,1,0:T(8,128)}, u32[]{:S(2)}) %copy-start.7) | copy-done | bytes 65560
  18.4 0.8 %copy-done.10 = f32[4,16,128]{2,1,0:T(8,128)S(1)} copy-done((f32[4,16,128]{2,1,0:T(8,128)S(1)}, f32[4,16,128]{2,1,0:T(8,128)}, u32[]{:S(2)}) %copy-start.10) | copy-done | bytes 32792
  19.2 0.1 pack_y.1
  19.2 1.7 %collective-permute-start.2 = (f32[384,256]{1,0:T(8,128)S(1)}, f32[384,256]{1,0:T(8,128)S(1)}, u32[]{:S(2)}, u32[]{:S(2)}) collective-permute-start(f32[384,256]{1,0:T(8,128)S(1)} %get-tuple-element.25), channel_id=1, source_target_pairs={{0,4},{4,8},{8,12},{12,16},{16,20},{20,24},{24,28},{28,32},{32,36}... | collective-permute-start | bytes 1179656 | tf_op jit(solution)/shard_map/ppermute | solution.py:41
  20.9 6.7 %collective-permute-start.3 = (f32[384,256]{1,0:T(8,128)S(1)}, f32[384,256]{1,0:T(8,128)S(1)}, u32[]{:S(2)}, u32[]{:S(2)}) collective-permute-start(f32[384,256]{1,0:T(8,128)S(1)} %get-tuple-element.26), channel_id=1, source_target_pairs={{4,0},{8,4},{12,8},{16,12},{20,16},{24,20},{28,24},{32,28},{36,32}... | collective-permute-start | bytes 1179656 | tf_op jit(solution)/shard_map/ppermute | solution.py:41
  27.5 7.8 %collective-permute-done.2.below = f32[384,256]{1,0:T(8,128)S(1)} collective-permute-done((f32[384,256]{1,0:T(8,128)S(1)}, f32[384,256]{1,0:T(8,128)S(1)}, u32[]{:S(2)}, u32[]{:S(2)}) %collective-permute-start.2) | collective-permute-done | bytes 393248 | tf_op jit(solution)/shard_map/ppermute | solution.py:41
  35.4 0.0 collective-permute-done.3.above
  35.4 0.0 copy-done.2
  35.4 0.0 copy-done.5
  35.4 0.0 copy-done.8
  35.4 0.0 copy-done.11
  35.4 0.8 %pack_z.1 = (f32[1632,256]{1,0:T(8,128)S(1)}, f32[1056,128]{1,0:T(8,128)S(1)}, f32[168,128]{1,0:T(8,128)S(1)}, f32[168,128]{1,0:T(8,128)S(1)}) custom-call(f32[2,8,32,256]{3,2,1,0:T(8,128)S(1)} %copy-done.2, f32[2,4,16,128]{3,2,1,0:T(8,128)S(1)} %copy-done.8, s32[8,32,256]{2,1,0:T(8,128)S(1)} %copy-done.5, f32[4,16,128]{2,1,0:T(8,128)S(1)} %copy-done.11, ...), custom_call_target="tpu_custom_call" | custom-call | flops 2000000 | bytes 2000000 | tf_op jit(solution)/shard_map/pack_z/pallas_call | solution.py:436
  36.2 0.1 collective-permute-start.4
  36.3 1.7 %collective-permute-start.5 = (f32[168,128]{1,0:T(8,128)S(1)}, f32[168,128]{1,0:T(8,128)S(1)}, u32[]{:S(2)}, u32[]{:S(2)}) collective-permute-start(f32[168,128]{1,0:T(8,128)S(1)} %get-tuple-element.30), channel_id=1, source_target_pairs={{1,0},{2,1},{3,2},{0,3},{5,4},{6,5},{7,6},{4,7},{9,8},{10,9},{11,1... | collective-permute-start | bytes 258056 | tf_op jit(solution)/shard_map/ppermute | solution.py:41
  38.0 0.1 pad_add_fusion.coord
  38.1 0.0 copy-done.12
  38.1 0.0 copy-done.14
  38.1 2.9 %sources.1 = (f32[2,10,48,384]{3,2,1,0:T(8,128)S(1)}, bf16[256,384]{1,0:T(8,128)(2,1)S(1)}, bf16[384,256]{1,0:T(8,128)(2,1)S(1)}) custom-call(s32[3]{0:T(128)S(1)} %pad_add_fusion.coord, s32[3,1024]{1,0:T(4,128)S(1)} %bitcast.4, f32[2,1024]{1,0:T(2,128)S(1)} %copy-done.14, s32[3,1024]{1,0:T(4,128)S(1)} %bitcast.5), custom_call_target="tpu_custom_call" | custom-call | flops 8000000 | bytes 8000000 | tf_op jit(solution)/shard_map/sources/pallas_call | solution.py:426
  41.0 0.0 collective-permute-done.4.left
  41.0 0.0 collective-permute-done.5.right
  41.1 0.0 copy-done.16
  41.1 0.0 copy-done.17
  41.1 0.0 copy-start.13
  41.1 5.2 %smooth.1 = (f32[2,8,32,256]{3,2,1,0:T(8,128)}, f32[4,24,256]{2,1,0:T(8,128)S(1)}, f32[3,24,256]{2,1,0:T(8,128)S(1)}, f32[3,24,256]{2,1,0:T(8,128)S(1)}, f32[544,128]{1,0:T(8,128)S(1)}) custom-call(s32[3]{0:T(128)S(1)} %pad_add_fusion.coord, f32[4]{0:T(128)S(1)} %copy-done.16, f32[4]{0:T(128)S(1)} %copy-done.17, f32[1632,256]{1,0:T(8,128)S(1)} %get-tuple-element.27.wide, ...), custom_call_target="tpu_custom_call" | custom-call | flops 2000000 | bytes 2000000 | tf_op jit(solution)/shard_map/smooth/pallas_call | solution.py:442
  46.2 1.0 %collective-permute-start.6 = (f32[3,24,256]{2,1,0:T(8,128)S(1)}, f32[3,24,256]{2,1,0:T(8,128)S(1)}, u32[]{:S(2)}, u32[]{:S(2)}) collective-permute-start(f32[3,24,256]{2,1,0:T(8,128)S(1)} %get-tuple-element.37), channel_id=1, source_target_pairs={{0,64},{64,128},{128,192},{192,0},{1,65},{65,129},{129,193},{193,1... | collective-permute-start | bytes 221192 | tf_op jit(solution)/shard_map/ppermute | solution.py:41
  47.3 1.0 %collective-permute-start.7 = (f32[3,24,256]{2,1,0:T(8,128)S(1)}, f32[3,24,256]{2,1,0:T(8,128)S(1)}, u32[]{:S(2)}, u32[]{:S(2)}) collective-permute-start(f32[3,24,256]{2,1,0:T(8,128)S(1)} %get-tuple-element.38), channel_id=1, source_target_pairs={{64,0},{128,64},{192,128},{0,192},{65,1},{129,65},{193,129},{1,193... | collective-permute-start | bytes 221192 | tf_op jit(solution)/shard_map/ppermute | solution.py:41
  48.3 2.3 %collective-permute-done.6.before = f32[3,24,256]{2,1,0:T(8,128)S(1)} collective-permute-done((f32[3,24,256]{2,1,0:T(8,128)S(1)}, f32[3,24,256]{2,1,0:T(8,128)S(1)}, u32[]{:S(2)}, u32[]{:S(2)}) %collective-permute-start.6) | collective-permute-done | bytes 73760 | tf_op jit(solution)/shard_map/ppermute | solution.py:41
  50.6 2.2 %collective-permute-done.7.after = f32[3,24,256]{2,1,0:T(8,128)S(1)} collective-permute-done((f32[3,24,256]{2,1,0:T(8,128)S(1)}, f32[3,24,256]{2,1,0:T(8,128)S(1)}, u32[]{:S(2)}, u32[]{:S(2)}) %collective-permute-start.7) | collective-permute-done | bytes 73760 | tf_op jit(solution)/shard_map/ppermute | solution.py:41
  52.8 0.0 copy-done.13
  52.8 1.7 %bioheat.1 = (f32[4,16,128]{2,1,0:T(8,128)}, f32[4,16,128]{2,1,0:T(8,128)}) custom-call(s32[3]{0:T(128)S(1)} %pad_add_fusion.coord, f32[1056,128]{1,0:T(8,128)S(1)} %get-tuple-element.28.narrow, f32[544,128]{1,0:T(8,128)S(1)} %get-tuple-element.35.tiles, f32[4,24,256]{2,1,0:T(8,128)S(1)} %get-tuple-element.36.power, ...), custom_call_target="tpu_custom_call" | custom-call | flops 2000000 | bytes 2000000 | tf_op jit(solution)/shard_map/bioheat/pallas_call | solution.py:464
  (11 shorter events, 0.0 us)
Async XLA Ops:
  0.6 1.0 %copy-start = (f32[2,8,32,256]{3,2,1,0:T(8,128)S(1)}, f32[2,8,32,256]{3,2,1,0:T(8,128)}, u32[]{:S(2)}) copy-start(f32[2,8,32,256]{3,2,1,0:T(8,128)} %it.5) | copy-start | bytes 1572868
  1.7 0.9 %copy-start.3 = (s32[8,32,256]{2,1,0:T(8,128)S(1)}, s32[8,32,256]{2,1,0:T(8,128)}, u32[]{:S(2)}) copy-start(s32[8,32,256]{2,1,0:T(8,128)} %codes.5) | copy-start | bytes 786436
  2.6 0.8 %copy-start.6 = (f32[2,4,16,128]{3,2,1,0:T(8,128)S(1)}, f32[2,4,16,128]{3,2,1,0:T(8,128)}, u32[]{:S(2)}) copy-start(f32[2,4,16,128]{3,2,1,0:T(8,128)} %co.5) | copy-start | bytes 196612
  3.5 0.8 %copy-start.9 = (f32[4,16,128]{2,1,0:T(8,128)S(1)}, f32[4,16,128]{2,1,0:T(8,128)}, u32[]{:S(2)}) copy-start(f32[4,16,128]{2,1,0:T(8,128)} %theta.5) | copy-start | bytes 98308
  4.2 0.7 %copy-start.15 = (f32[4]{0:T(128)S(1)}, f32[4]{0:T(128)}, u32[]{:S(2)}) copy-start(f32[4]{0:T(128)} %wash.1) | copy-start | bytes 52
  4.9 30.5 %copy-start.2 = (f32[2,8,32,256]{3,2,1,0:T(8,128)S(1)}, f32[2,8,32,256]{3,2,1,0:T(8,128)}, u32[]{:S(2)}) copy-start(f32[2,8,32,256]{3,2,1,0:T(8,128)} %it.5) | copy-start | bytes 1572868
  4.9 30.5 %copy-start.5 = (s32[8,32,256]{2,1,0:T(8,128)S(1)}, s32[8,32,256]{2,1,0:T(8,128)}, u32[]{:S(2)}) copy-start(s32[8,32,256]{2,1,0:T(8,128)} %codes.5) | copy-start | bytes 786436
  4.9 30.5 %copy-start.8 = (f32[2,4,16,128]{3,2,1,0:T(8,128)S(1)}, f32[2,4,16,128]{3,2,1,0:T(8,128)}, u32[]{:S(2)}) copy-start(f32[2,4,16,128]{3,2,1,0:T(8,128)} %co.5) | copy-start | bytes 196612
  4.9 30.5 %copy-start.11 = (f32[4,16,128]{2,1,0:T(8,128)S(1)}, f32[4,16,128]{2,1,0:T(8,128)}, u32[]{:S(2)}) copy-start(f32[4,16,128]{2,1,0:T(8,128)} %theta.5) | copy-start | bytes 98308
  5.7 8.1 %collective-permute-start = (f32[256,256]{1,0:T(8,128)S(1)}, f32[256,256]{1,0:T(8,128)S(1)}, u32[]{:S(2)}, u32[]{:S(2)}) collective-permute-start(f32[256,256]{1,0:T(8,128)S(1)} %get-tuple-element.23), channel_id=1, source_target_pairs={{0,64},{64,128},{128,192},{192,0},{1,65},{65,129},{129,193},{193,1... | collective-permute-start | bytes 786440 | tf_op jit(solution)/shard_map/ppermute | solution.py:41
  8.0 7.6 %collective-permute-start.1 = (f32[256,256]{1,0:T(8,128)S(1)}, f32[256,256]{1,0:T(8,128)S(1)}, u32[]{:S(2)}, u32[]{:S(2)}) collective-permute-start(f32[256,256]{1,0:T(8,128)S(1)} %get-tuple-element.24), channel_id=1, source_target_pairs={{64,0},{128,64},{192,128},{0,192},{65,1},{129,65},{193,129},{1,193... | collective-permute-start | bytes 786440 | tf_op jit(solution)/shard_map/ppermute | solution.py:41
  15.6 1.0 %copy-start.1 = (f32[2,8,32,256]{3,2,1,0:T(8,128)S(1)}, f32[2,8,32,256]{3,2,1,0:T(8,128)}, u32[]{:S(2)}) copy-start(f32[2,8,32,256]{3,2,1,0:T(8,128)} %it.5) | copy-start | bytes 1572868
  16.6 0.9 %copy-start.4 = (s32[8,32,256]{2,1,0:T(8,128)S(1)}, s32[8,32,256]{2,1,0:T(8,128)}, u32[]{:S(2)}) copy-start(s32[8,32,256]{2,1,0:T(8,128)} %codes.5) | copy-start | bytes 786436
  17.5 0.8 %copy-start.7 = (f32[2,4,16,128]{3,2,1,0:T(8,128)S(1)}, f32[2,4,16,128]{3,2,1,0:T(8,128)}, u32[]{:S(2)}) copy-start(f32[2,4,16,128]{3,2,1,0:T(8,128)} %co.5) | copy-start | bytes 196612
  18.4 0.8 %copy-start.10 = (f32[4,16,128]{2,1,0:T(8,128)S(1)}, f32[4,16,128]{2,1,0:T(8,128)}, u32[]{:S(2)}) copy-start(f32[4,16,128]{2,1,0:T(8,128)} %theta.5) | copy-start | bytes 98308
  19.1 19.0 %copy-start.12 = (s32[1024,3]{0,1:T(4,128)S(1)}, s32[1024,3]{0,1:T(4,128)}, u32[]{:S(2)}) copy-start(s32[1024,3]{0,1:T(4,128)} %param.13) | copy-start | bytes 36868
  19.1 19.0 %copy-start.14 = (f32[2,1024]{1,0:T(2,128)S(1)}, f32[2,1024]{1,0:T(2,128)}, u32[]{:S(2)}) copy-start(f32[2,1024]{1,0:T(2,128)} %exc_s.1) | copy-start | bytes 24580
  19.1 21.9 %copy-start.16 = (f32[4]{0:T(128)S(1)}, f32[4]{0:T(128)}, u32[]{:S(2)}) copy-start(f32[4]{0:T(128)} %wave_t.1) | copy-start | bytes 52
  19.1 21.9 %copy-start.17 = (f32[4]{0:T(128)S(1)}, f32[4]{0:T(128)}, u32[]{:S(2)}) copy-start(f32[4]{0:T(128)} %damp_t.1) | copy-start | bytes 52
  19.2 16.1 %collective-permute-start.2 = (f32[384,256]{1,0:T(8,128)S(1)}, f32[384,256]{1,0:T(8,128)S(1)}, u32[]{:S(2)}, u32[]{:S(2)}) collective-permute-start(f32[384,256]{1,0:T(8,128)S(1)} %get-tuple-element.25), channel_id=1, source_target_pairs={{0,4},{4,8},{8,12},{12,16},{16,20},{20,24},{24,28},{28,32},{32,36}... | collective-permute-start | bytes 1179656 | tf_op jit(solution)/shard_map/ppermute | solution.py:41
  20.9 14.5 %collective-permute-start.3 = (f32[384,256]{1,0:T(8,128)S(1)}, f32[384,256]{1,0:T(8,128)S(1)}, u32[]{:S(2)}, u32[]{:S(2)}) collective-permute-start(f32[384,256]{1,0:T(8,128)S(1)} %get-tuple-element.26), channel_id=1, source_target_pairs={{4,0},{8,4},{12,8},{16,12},{20,16},{24,20},{28,24},{32,28},{36,32}... | collective-permute-start | bytes 1179656 | tf_op jit(solution)/shard_map/ppermute | solution.py:41
  36.2 4.8 %collective-permute-start.4 = (f32[168,128]{1,0:T(8,128)S(1)}, f32[168,128]{1,0:T(8,128)S(1)}, u32[]{:S(2)}, u32[]{:S(2)}) collective-permute-start(f32[168,128]{1,0:T(8,128)S(1)} %get-tuple-element.29), channel_id=1, source_target_pairs={{0,1},{1,2},{2,3},{3,0},{4,5},{5,6},{6,7},{7,4},{8,9},{9,10},{10,1... | collective-permute-start | bytes 258056 | tf_op jit(solution)/shard_map/ppermute | solution.py:41
  36.3 4.8 %collective-permute-start.5 = (f32[168,128]{1,0:T(8,128)S(1)}, f32[168,128]{1,0:T(8,128)S(1)}, u32[]{:S(2)}, u32[]{:S(2)}) collective-permute-start(f32[168,128]{1,0:T(8,128)S(1)} %get-tuple-element.30), channel_id=1, source_target_pairs={{1,0},{2,1},{3,2},{0,3},{5,4},{6,5},{7,6},{4,7},{9,8},{10,9},{11,1... | collective-permute-start | bytes 258056 | tf_op jit(solution)/shard_map/ppermute | solution.py:41
  41.1 11.7 %copy-start.13 = (f32[4,16,128]{2,1,0:T(8,128)S(1)}, f32[4,16,128]{2,1,0:T(8,128)}, u32[]{:S(2)}) copy-start(f32[4,16,128]{2,1,0:T(8,128)} %injury.1) | copy-start | bytes 98308
  46.2 4.4 %collective-permute-start.6 = (f32[3,24,256]{2,1,0:T(8,128)S(1)}, f32[3,24,256]{2,1,0:T(8,128)S(1)}, u32[]{:S(2)}, u32[]{:S(2)}) collective-permute-start(f32[3,24,256]{2,1,0:T(8,128)S(1)} %get-tuple-element.37), channel_id=1, source_target_pairs={{0,64},{64,128},{128,192},{192,0},{1,65},{65,129},{129,193},{193,1... | collective-permute-start | bytes 221192 | tf_op jit(solution)/shard_map/ppermute | solution.py:41
  47.3 5.6 %collective-permute-start.7 = (f32[3,24,256]{2,1,0:T(8,128)S(1)}, f32[3,24,256]{2,1,0:T(8,128)S(1)}, u32[]{:S(2)}, u32[]{:S(2)}) collective-permute-start(f32[3,24,256]{2,1,0:T(8,128)S(1)} %get-tuple-element.38), channel_id=1, source_target_pairs={{64,0},{128,64},{192,128},{0,192},{65,1},{129,65},{193,129},{1,193... | collective-permute-start | bytes 221192 | tf_op jit(solution)/shard_map/ppermute | solution.py:41

commit v2 on v1

--- a/solution.py
+++ b/solution.py
@@ -30,6 +30,10 @@
     return pl.BlockSpec(memory_space=pltpu.VMEM)
 
 
+def hbm():
+    return pl.BlockSpec(memory_space=pltpu.HBM)
+
+
 def smem():
     return pl.BlockSpec(memory_space=pltpu.SMEM)
 
@@ -61,9 +65,19 @@
     return jnp.where(codes == 3.0, entries[3], value)
 
 
-def pack_x(wash, it, co, codes, theta, up, down, perf, pool):
+def pack_x(wash_h, it_h, co_h, codes_h, theta_h, up, down, perf, it, co, codes, theta, pool, wash, sems):
+    loads = [
+        pltpu.make_async_copy(src, dst, sems.at[k])
+        for k, (src, dst) in enumerate(
+            ((codes_h, codes), (it_h, it), (wash_h, wash), (co_h, co), (theta_h, theta))
+        )
+    ]
+    for load in loads:
+        load.start()
     lane, col = iota((256, 128), 0), iota((256, 128), 1)
     pairs = jnp.where(lane // 2 == col, 1.0, 0.0).astype(BF16)
+    for load in loads:
+        load.wait()
     entries = [wash[k] for k in range(4)]
     for i in range(4):
         both = pick(codes[2 * i].astype(F32), entries) + pick(codes[2 * i + 1].astype(F32), entries)
@@ -126,7 +140,7 @@
         return ref[pl.ds(XB_THERM + 16 * k + at, n), pl.ds(128, 128)]
 
 
-def pack_y(it, co, codes, theta, perf, before, after, up, down):
+def pack_y(it, co, codes, theta, perf, before, after, after_this, up, down):
     block = Columns(it, co, codes, theta, perf, before, after)
     for ref, last in ((up, True), (down, False)):
         fine, coarse, warm = ((24, 8), (8, 8), (12, 4)) if last else ((0, 8), (0, 8), (0, 4))
@@ -199,7 +213,7 @@
         ref[...] = packed
 
 
-def sources(coord, loc_s, exc_s, loc, field, spread, gather):
+def sources(coord, loc_s, exc_s, loc, after_this, field, spread, gather):
     field[...] = jnp.zeros(field.shape, F32)
     first = loc[0:1, :] - coord[0] * 8
     second = loc[1:2, :] - coord[1] * 32
@@ -344,7 +358,10 @@
             down[i] = sums[i * 24 : i * 24 + 24]
 
 
-def bioheat(coord, narrow, tiles, power, before, after, injury, warm_out, dose_out, now, later):
+def bioheat(coord, narrow, tiles, power, before, after, injury, wave, warm_out, dose_out, wave_out, now, later, sem):
+    store = pltpu.make_async_copy(wave, wave_out, sem)
+    store.start()
+
     def flag(test):
         return jnp.where(test, 1.0, 0.0)
 
@@ -381,19 +398,20 @@
         state, other = other, state
     for i in range(4):
         dose_out[i] = jnp.log(dose[i])
+    store.wait()
 
 
 def shaped(*shape, dtype=F32):
     return jax.ShapeDtypeStruct(shape, dtype)
 
 
-def call(kernel, name, in_specs, outs, scratch=(), cost=2000):
+def call(kernel, name, in_specs, outs, scratch=(), out_specs=None, cost=2000):
     return pl.pallas_call(
         kernel,
         name=name,
         out_shape=tuple(outs),
         in_specs=in_specs,
-        out_specs=tuple(vmem() for _ in outs),
+        out_specs=tuple(out_specs or [vmem() for _ in outs]),
         scratch_shapes=list(scratch),
         cost_estimate=pl.CostEstimate(flops=cost * 1000, bytes_accessed=cost * 1000, transcendentals=0),
         compiler_params=pltpu.CompilerParams(vmem_limit_bytes=24 * 1024 * 1024),
@@ -416,20 +434,28 @@
     coord = jnp.stack([lax.axis_index("gx"), lax.axis_index("gy"), lax.axis_index("gz")]).astype(jnp.int32)
     loc = element_location.T
 
-    up, down, perf = call(
-        pack_x, "pack_x", [smem()] + [vmem()] * 4,
-        [shaped(XB, 256), shaped(XB, 256), shaped(4, 16, 128)],
-        [pltpu.VMEM((2, 128, 128), F32)],
-    )(washout_fraction, it, co, codes, theta)
+    up, down, perf, it, co, codes, theta = call(
+        pack_x, "pack_x", [hbm()] * 5,
+        [
+            shaped(XB, 256),
+            shaped(XB, 256),
+            shaped(4, 16, 128),
+            shaped(2, 8, 32, 256),
+            shaped(2, 4, 16, 128),
+            shaped(8, 32, 256, dtype=jnp.int32),
+            shaped(4, 16, 128),
+        ],
+        [pltpu.VMEM((2, 128, 128), F32), pltpu.SMEM((4,), F32), pltpu.SemaphoreType.DMA((5,))],
+    )(*[pltpu.with_memory_space_constraint(a, pltpu.HBM) for a in (washout_fraction, it, co, codes, theta)])
     before, after = exchange(up, down, "gx")
 
     field, spread, gather = call(
-        sources, "sources", [smem(), smem(), smem(), vmem()],
+        sources, "sources", [smem(), smem(), smem(), vmem(), vmem()],
         [shaped(2, CX, 48, 384), shaped(256, 384, dtype=BF16), shaped(384, 256, dtype=BF16)], cost=8000,
-    )(coord, loc, element_excitation, loc)
-
-    up, down = call(pack_y, "pack_y", [vmem()] * 7, [shaped(YB, 256), shaped(YB, 256)])(
-        it, co, codes, theta, perf, before, after
+    )(coord, loc, element_excitation, loc, perf)
+
+    up, down = call(pack_y, "pack_y", [vmem()] * 8, [shaped(YB, 256), shaped(YB, 256)])(
+        it, co, codes, theta, perf, before, after, gather
     )
     below, above = exchange(up, down, "gy")
 
@@ -461,11 +487,12 @@
     )(coord, class_wavespeed, class_damping, wide, narrow, left, right, field, spread, gather)
     before, after = exchange(up, down, "gx")
 
-    warmth, dose = call(
-        bioheat, "bioheat", [smem()] + [vmem()] * 6,
-        [shaped(4, 16, 128), shaped(4, 16, 128)],
-        [pltpu.VMEM((TX, 24, 256), F32), pltpu.VMEM((TX, 24, 256), F32)],
-    )(coord, narrow, tiles, power, before, after, injury_integral)
+    warmth, dose, pressure = call(
+        bioheat, "bioheat", [smem()] + [vmem()] * 7,
+        [shaped(4, 16, 128), shaped(4, 16, 128), shaped(2, 8, 32, 256)],
+        [pltpu.VMEM((TX, 24, 256), F32), pltpu.VMEM((TX, 24, 256), F32), pltpu.SemaphoreType.DMA],
+        [vmem(), vmem(), hbm()],
+    )(coord, narrow, tiles, power, before, after, injury_integral, pressure)
     return pressure, warmth, dose
 
 

time: 54.8 us -> 47 us (0.86)
  the two profiles are of different devices: /device:TPU:6 before, /device:TPU:1 now
where the time goes in v2:
time: 47 us; the launch traced here: 46.7 us
  starting transfers between devices  17.8 us (38%)
  waiting for transfers between devices  15.5 us (33%)
  Pallas kernels  11.3 us (24%)
  local copies, waits for them, and re-layouts  1.43 us (3%)
  between operations  0.69 us (1%)
    ppermute x8, starting transfers between devices, exchange(): return (lax.ppermute(up, axis, ahead), lax.ppermute(down, axis, back))  17.8 us
    ppermute x8, waiting for transfers between devices, exchange(): return (lax.ppermute(up, axis, ahead), lax.ppermute(down, axis, back))  15.5 us
    pallas_call x1, Pallas kernels, on_device(): call(smooth, 'smooth', [smem()] * 3 + [vmem()] * 7, [shaped(2, 8, 32, 256...  4.5 us
    pallas_call x1, Pallas kernels, on_device(): call(sources, 'sources', [smem(), smem(), smem(), vmem(), vmem()], [shape...  2.51 us
    pallas_call x1, Pallas kernels, on_device(): call(bioheat, 'bioheat', [smem()] + [vmem()] * 7, [shaped(4, 16, 128), sh...  1.97 us
    pallas_call x1, Pallas kernels, on_device(): call(pack_x, 'pack_x', [hbm()] * 5, [shaped(XB, 256), shaped(XB, 256), sh...  1.43 us
    unnamed x10, local copies, waits for them, and re-layouts  1.43 us
  transfers between devices with their start and end apart: 8, of which 5 were waited for; matrix products, arithmetic and copies ran while one was open for 0% of the time, Pallas kernels for 5%

profile of v2, /device:TPU:1, one launch (start us, length us, event | category | flops | bytes accessed | tf_op | source)
XLA Modules:
  0.0 46.7 jit_solution(16866232181969023286)
XLA Ops:
  0.6 1.4 %pack_x.1 = (f32[256,256]{1,0:T(8,128)S(1)}, f32[256,256]{1,0:T(8,128)S(1)}, f32[4,16,128]{2,1,0:T(8,128)S(1)}, f32[2,8,32,256]{3,2,1,0:T(8,128)S(1)}, f32[2,4,1...) custom-call(f32[4]{0:T(128)} %wash_h.1, f32[2,8,32,256]{3,2,1,0:T(8,128)} %it_h.1, ...), custom_call_target="tpu_custom_call" | custom-call | flops 2000000 | bytes 2000000 | tf_op jit(solution)/shard_map/pack_x/pallas_call | solution.py:437
  2.1 2.1 %collective-permute-start = (f32[256,256]{1,0:T(8,128)S(1)}, f32[256,256]{1,0:T(8,128)S(1)}, u32[]{:S(2)}, u32[]{:S(2)}) collective-permute-start(f32[256,256]{1,0:T(8,128)S(1)} %get-tuple-element.32), channel_id=1, source_target_pairs={{0,64},{64,128},{128,192},{192,0},{1,65},{65,129},{129,193},{193,1... | collective-permute-start | bytes 786440 | tf_op jit(solution)/shard_map/ppermute | solution.py:45
  4.2 1.4 %collective-permute-start.1 = (f32[256,256]{1,0:T(8,128)S(1)}, f32[256,256]{1,0:T(8,128)S(1)}, u32[]{:S(2)}, u32[]{:S(2)}) collective-permute-start(f32[256,256]{1,0:T(8,128)S(1)} %get-tuple-element.33), channel_id=1, source_target_pairs={{64,0},{128,64},{192,128},{0,192},{65,1},{129,65},{193,129},{1,193... | collective-permute-start | bytes 786440 | tf_op jit(solution)/shard_map/ppermute | solution.py:45
  5.5 0.1 pad_add_fusion.coord
  5.6 0.0 copy-start
  5.6 0.7 %copy-done = s32[1024,3]{0,1:T(4,128)S(1)} copy-done((s32[1024,3]{0,1:T(4,128)S(1)}, s32[1024,3]{0,1:T(4,128)}, u32[]{:S(2)}) %copy-start) | copy-done | bytes 12312
  6.3 0.0 copy-start.2
  6.3 0.7 %copy-done.2 = f32[2,1024]{1,0:T(2,128)S(1)} copy-done((f32[2,1024]{1,0:T(2,128)S(1)}, f32[2,1024]{1,0:T(2,128)}, u32[]{:S(2)}) %copy-start.2) | copy-done | bytes 8216
  7.0 2.5 %sources.1 = (f32[2,10,48,384]{3,2,1,0:T(8,128)S(1)}, bf16[256,384]{1,0:T(8,128)(2,1)S(1)}, bf16[384,256]{1,0:T(8,128)(2,1)S(1)}) custom-call(s32[3]{0:T(128)S(1)} %pad_add_fusion.coord, s32[3,1024]{1,0:T(4,128)S(1)} %bitcast.4, f32[2,1024]{1,0:T(2,128)S(1)} %copy-done.2, s32[3,1024]{1,0:T(4,128)S(1)} %bitcast.5, ...), custom_call_target="tpu_custom_call" | custom-call | flops 8000000 | bytes 8000000 | tf_op jit(solution)/shard_map/sources/pallas_call | solution.py:452
  9.6 0.0 collective-permute-done.before
  9.6 1.1 %collective-permute-done.1.after = f32[256,256]{1,0:T(8,128)S(1)} collective-permute-done((f32[256,256]{1,0:T(8,128)S(1)}, f32[256,256]{1,0:T(8,128)S(1)}, u32[]{:S(2)}, u32[]{:S(2)}) %collective-permute-start.1) | collective-permute-done | bytes 262176 | tf_op jit(solution)/shard_map/ppermute | solution.py:45
  10.7 0.0 copy-start.3
  10.7 0.0 copy-start.4
  10.7 0.1 pack_y.1
  10.8 2.4 %collective-permute-start.2 = (f32[384,256]{1,0:T(8,128)S(1)}, f32[384,256]{1,0:T(8,128)S(1)}, u32[]{:S(2)}, u32[]{:S(2)}) collective-permute-start(f32[384,256]{1,0:T(8,128)S(1)} %get-tuple-element.35), channel_id=1, source_target_pairs={{0,4},{4,8},{8,12},{12,16},{16,20},{20,24},{24,28},{28,32},{32,36}... | collective-permute-start | bytes 1179656 | tf_op jit(solution)/shard_map/ppermute | solution.py:45
  13.2 6.7 %collective-permute-start.3 = (f32[384,256]{1,0:T(8,128)S(1)}, f32[384,256]{1,0:T(8,128)S(1)}, u32[]{:S(2)}, u32[]{:S(2)}) collective-permute-start(f32[384,256]{1,0:T(8,128)S(1)} %get-tuple-element.36), channel_id=1, source_target_pairs={{4,0},{8,4},{12,8},{16,12},{20,16},{24,20},{28,24},{32,28},{36,32}... | collective-permute-start | bytes 1179656 | tf_op jit(solution)/shard_map/ppermute | solution.py:45
  19.8 7.8 %collective-permute-done.2.below = f32[384,256]{1,0:T(8,128)S(1)} collective-permute-done((f32[384,256]{1,0:T(8,128)S(1)}, f32[384,256]{1,0:T(8,128)S(1)}, u32[]{:S(2)}, u32[]{:S(2)}) %collective-permute-start.2) | collective-permute-done | bytes 393248 | tf_op jit(solution)/shard_map/ppermute | solution.py:45
  27.6 0.0 collective-permute-done.3.above
  27.6 0.8 %pack_z.1 = (f32[1632,256]{1,0:T(8,128)S(1)}, f32[1056,128]{1,0:T(8,128)S(1)}, f32[168,128]{1,0:T(8,128)S(1)}, f32[168,128]{1,0:T(8,128)S(1)}) custom-call(f32[2,8,32,256]{3,2,1,0:T(8,128)S(1)} %get-tuple-element.27.it, f32[2,4,16,128]{3,2,1,0:T(8,128)S(1)} %get-tuple-element.28.co, s32[8,32,256]{2,1,0:T(8,128)S(1)} %get-tuple-element.29.codes, ...), custom_call_target="tpu_custom_call" | custom-call | flops 2000000 | bytes 2000000 | tf_op jit(solution)/shard_map/pack_z/pallas_call | solution.py:462
  28.4 2.5 %collective-permute-start.4 = (f32[168,128]{1,0:T(8,128)S(1)}, f32[168,128]{1,0:T(8,128)S(1)}, u32[]{:S(2)}, u32[]{:S(2)}) collective-permute-start(f32[168,128]{1,0:T(8,128)S(1)} %get-tuple-element.39), channel_id=1, source_target_pairs={{0,1},{1,2},{2,3},{3,0},{4,5},{5,6},{6,7},{7,4},{8,9},{9,10},{10,1... | collective-permute-start | bytes 258056 | tf_op jit(solution)/shard_map/ppermute | solution.py:45
  30.9 0.0 collective-permute-start.5
  31.0 1.5 %collective-permute-done.4.left = f32[168,128]{1,0:T(8,128)S(1)} collective-permute-done((f32[168,128]{1,0:T(8,128)S(1)}, f32[168,128]{1,0:T(8,128)S(1)}, u32[]{:S(2)}, u32[]{:S(2)}) %collective-permute-start.4) | collective-permute-done | bytes 86048 | tf_op jit(solution)/shard_map/ppermute | solution.py:45
  32.5 2.4 %collective-permute-done.5.right = f32[168,128]{1,0:T(8,128)S(1)} collective-permute-done((f32[168,128]{1,0:T(8,128)S(1)}, f32[168,128]{1,0:T(8,128)S(1)}, u32[]{:S(2)}, u32[]{:S(2)}) %collective-permute-start.5) | collective-permute-done | bytes 86048 | tf_op jit(solution)/shard_map/ppermute | solution.py:45
  34.9 0.0 copy-done.3
  34.9 0.0 copy-done.4
  34.9 0.0 copy-start.1
  34.9 4.5 %smooth.1 = (f32[2,8,32,256]{3,2,1,0:T(8,128)S(1)}, f32[4,24,256]{2,1,0:T(8,128)S(1)}, f32[3,24,256]{2,1,0:T(8,128)S(1)}, f32[3,24,256]{2,1,0:T(8,128)S(1)}, f32[544,128]{1,0:T(8,128)S(1)}) custom-call(s32[3]{0:T(128)S(1)} %pad_add_fusion.coord, f32[4]{0:T(128)S(1)} %copy-done.3, f32[4]{0:T(128)S(1)} %copy-done.4, f32[1632,256]{1,0:T(8,128)S(1)} %get-tuple-element.38.wide, ...), custom_call_target="tpu_custom_call" | custom-call | flops 2000000 | bytes 2000000 | tf_op jit(solution)/shard_map/smooth/pallas_call | solution.py:468
  39.4 1.0 %collective-permute-start.6 = (f32[3,24,256]{2,1,0:T(8,128)S(1)}, f32[3,24,256]{2,1,0:T(8,128)S(1)}, u32[]{:S(2)}, u32[]{:S(2)}) collective-permute-start(f32[3,24,256]{2,1,0:T(8,128)S(1)} %get-tuple-element.45), channel_id=1, source_target_pairs={{0,64},{64,128},{128,192},{192,0},{1,65},{65,129},{129,193},{193,1... | collective-permute-start | bytes 221192 | tf_op jit(solution)/shard_map/ppermute | solution.py:45
  40.3 1.8 %collective-permute-start.7 = (f32[3,24,256]{2,1,0:T(8,128)S(1)}, f32[3,24,256]{2,1,0:T(8,128)S(1)}, u32[]{:S(2)}, u32[]{:S(2)}) collective-permute-start(f32[3,24,256]{2,1,0:T(8,128)S(1)} %get-tuple-element.46), channel_id=1, source_target_pairs={{64,0},{128,64},{192,128},{0,192},{65,1},{129,65},{193,129},{1,193... | collective-permute-start | bytes 221192 | tf_op jit(solution)/shard_map/ppermute | solution.py:45
  42.1 2.6 %collective-permute-done.6.before = f32[3,24,256]{2,1,0:T(8,128)S(1)} collective-permute-done((f32[3,24,256]{2,1,0:T(8,128)S(1)}, f32[3,24,256]{2,1,0:T(8,128)S(1)}, u32[]{:S(2)}, u32[]{:S(2)}) %collective-permute-start.6) | collective-permute-done | bytes 73760 | tf_op jit(solution)/shard_map/ppermute | solution.py:45
  44.8 0.0 collective-permute-done.7.after
  44.8 0.0 copy-done.1
  44.8 2.0 %bioheat.1 = (f32[4,16,128]{2,1,0:T(8,128)}, f32[4,16,128]{2,1,0:T(8,128)}, f32[2,8,32,256]{3,2,1,0:T(8,128)}) custom-call(s32[3]{0:T(128)S(1)} %pad_add_fusion.coord, f32[1056,128]{1,0:T(8,128)S(1)} %get-tuple-element.37.narrow, f32[544,128]{1,0:T(8,128)S(1)} %get-tuple-element.43.tiles, f32[4,24,256]{2,1,0:T(8,128)S(1)} %get-tuple-element.44.power, ...), custom_call_target="tpu_custom_call" | custom-call | flops 2000000 | bytes 2000000 | tf_op jit(solution)/shard_map/bioheat/pallas_call | solution.py:490
Async XLA Ops:
  2.1 7.5 %collective-permute-start = (f32[256,256]{1,0:T(8,128)S(1)}, f32[256,256]{1,0:T(8,128)S(1)}, u32[]{:S(2)}, u32[]{:S(2)}) collective-permute-start(f32[256,256]{1,0:T(8,128)S(1)} %get-tuple-element.32), channel_id=1, source_target_pairs={{0,64},{64,128},{128,192},{192,0},{1,65},{65,129},{129,193},{193,1... | collective-permute-start | bytes 786440 | tf_op jit(solution)/shard_map/ppermute | solution.py:45
  4.2 6.5 %collective-permute-start.1 = (f32[256,256]{1,0:T(8,128)S(1)}, f32[256,256]{1,0:T(8,128)S(1)}, u32[]{:S(2)}, u32[]{:S(2)}) collective-permute-start(f32[256,256]{1,0:T(8,128)S(1)} %get-tuple-element.33), channel_id=1, source_target_pairs={{64,0},{128,64},{192,128},{0,192},{65,1},{129,65},{193,129},{1,193... | collective-permute-start | bytes 786440 | tf_op jit(solution)/shard_map/ppermute | solution.py:45
  5.6 0.7 %copy-start = (s32[1024,3]{0,1:T(4,128)S(1)}, s32[1024,3]{0,1:T(4,128)}, u32[]{:S(2)}) copy-start(s32[1024,3]{0,1:T(4,128)} %param.13) | copy-start | bytes 36868
  6.3 0.7 %copy-start.2 = (f32[2,1024]{1,0:T(2,128)S(1)}, f32[2,1024]{1,0:T(2,128)}, u32[]{:S(2)}) copy-start(f32[2,1024]{1,0:T(2,128)} %exc_s.1) | copy-start | bytes 24580
  10.7 24.2 %copy-start.3 = (f32[4]{0:T(128)S(1)}, f32[4]{0:T(128)}, u32[]{:S(2)}) copy-start(f32[4]{0:T(128)} %wave_t.1) | copy-start | bytes 52
  10.7 24.2 %copy-start.4 = (f32[4]{0:T(128)S(1)}, f32[4]{0:T(128)}, u32[]{:S(2)}) copy-start(f32[4]{0:T(128)} %damp_t.1) | copy-start | bytes 52
  10.8 16.8 %collective-permute-start.2 = (f32[384,256]{1,0:T(8,128)S(1)}, f32[384,256]{1,0:T(8,128)S(1)}, u32[]{:S(2)}, u32[]{:S(2)}) collective-permute-start(f32[384,256]{1,0:T(8,128)S(1)} %get-tuple-element.35), channel_id=1, source_target_pairs={{0,4},{4,8},{8,12},{12,16},{16,20},{20,24},{24,28},{28,32},{32,36}... | collective-permute-start | bytes 1179656 | tf_op jit(solution)/shard_map/ppermute | solution.py:45
  13.2 14.5 %collective-permute-start.3 = (f32[384,256]{1,0:T(8,128)S(1)}, f32[384,256]{1,0:T(8,128)S(1)}, u32[]{:S(2)}, u32[]{:S(2)}) collective-permute-start(f32[384,256]{1,0:T(8,128)S(1)} %get-tuple-element.36), channel_id=1, source_target_pairs={{4,0},{8,4},{12,8},{16,12},{20,16},{24,20},{28,24},{32,28},{36,32}... | collective-permute-start | bytes 1179656 | tf_op jit(solution)/shard_map/ppermute | solution.py:45
  28.4 4.1 %collective-permute-start.4 = (f32[168,128]{1,0:T(8,128)S(1)}, f32[168,128]{1,0:T(8,128)S(1)}, u32[]{:S(2)}, u32[]{:S(2)}) collective-permute-start(f32[168,128]{1,0:T(8,128)S(1)} %get-tuple-element.39), channel_id=1, source_target_pairs={{0,1},{1,2},{2,3},{3,0},{4,5},{5,6},{6,7},{7,4},{8,9},{9,10},{10,1... | collective-permute-start | bytes 258056 | tf_op jit(solution)/shard_map/ppermute | solution.py:45
  30.9 3.9 %collective-permute-start.5 = (f32[168,128]{1,0:T(8,128)S(1)}, f32[168,128]{1,0:T(8,128)S(1)}, u32[]{:S(2)}, u32[]{:S(2)}) collective-permute-start(f32[168,128]{1,0:T(8,128)S(1)} %get-tuple-element.40), channel_id=1, source_target_pairs={{1,0},{2,1},{3,2},{0,3},{5,4},{6,5},{7,6},{4,7},{9,8},{10,9},{11,1... | collective-permute-start | bytes 258056 | tf_op jit(solution)/shard_map/ppermute | solution.py:45
  34.9 9.9 %copy-start.1 = (f32[4,16,128]{2,1,0:T(8,128)S(1)}, f32[4,16,128]{2,1,0:T(8,128)}, u32[]{:S(2)}) copy-start(f32[4,16,128]{2,1,0:T(8,128)} %injury.1) | copy-start | bytes 98308
  39.4 5.4 %collective-permute-start.6 = (f32[3,24,256]{2,1,0:T(8,128)S(1)}, f32[3,24,256]{2,1,0:T(8,128)S(1)}, u32[]{:S(2)}, u32[]{:S(2)}) collective-permute-start(f32[3,24,256]{2,1,0:T(8,128)S(1)} %get-tuple-element.45), channel_id=1, source_target_pairs={{0,64},{64,128},{128,192},{192,0},{1,65},{65,129},{129,193},{193,1... | collective-permute-start | bytes 221192 | tf_op jit(solution)/shard_map/ppermute | solution.py:45
  40.3 4.4 %collective-permute-start.7 = (f32[3,24,256]{2,1,0:T(8,128)S(1)}, f32[3,24,256]{2,1,0:T(8,128)S(1)}, u32[]{:S(2)}, u32[]{:S(2)}) collective-permute-start(f32[3,24,256]{2,1,0:T(8,128)S(1)} %get-tuple-element.46), channel_id=1, source_target_pairs={{64,0},{128,64},{192,128},{0,192},{65,1},{129,65},{193,129},{1,193... | collective-permute-start | bytes 221192 | tf_op jit(solution)/shard_map/ppermute | solution.py:45

commit v3 on v2

--- a/solution.py
+++ b/solution.py
@@ -18,12 +18,14 @@
 
 FX, CX, LX, TX, QX = 12, 10, 8, 12, 10
 XB_CODE, XB_COARSE, XB_THERM, XB = 128, 160, 192, 256
-YB_CODE, YB_COARSE, YB_THERM, YB = 192, 272, 336, 384
+OWN = (128, 192, 224, 240)
+FAR = (64, 80, 112, 144)
 WIDE = 2 * FX * 48 + CX * 48
 N_CODE = 2 * FX * 48
 N_COARSE, N_THETA, N_PERF, NARROW = 0, 512, 800, 1056
 GROUPS = 16
 ZB = (WIDE + NARROW) // GROUPS
+AXES = ("gx", "gy", "gz")
 
 
 def vmem():
@@ -38,11 +40,55 @@
     return pl.BlockSpec(memory_space=pltpu.SMEM)
 
 
-def exchange(up, down, axis):
-    n = lax.axis_size(axis)
-    ahead = [(i, (i + 1) % n) for i in range(n)]
-    back = [(j, i) for i, j in ahead]
-    return lax.ppermute(up, axis, ahead), lax.ppermute(down, axis, back)
+def swaps(sizes, axis, odd):
+    count, targets = 1, []
+    for n in sizes:
+        count *= n
+    for i in range(count):
+        place, rest = [], i
+        for n in reversed(sizes):
+            place.insert(0, rest % n)
+            rest //= n
+        partner = list(place)
+        partner[axis] = ((place[axis] + 1) ^ 1) - 1 if odd else place[axis] ^ 1
+        if not 0 <= partner[axis] < sizes[axis]:
+            other = 2 if axis != 2 else 0
+            partner = list(place)
+            partner[other] = place[other] ^ 1
+        j = 0
+        for n, at in zip(sizes, partner):
+            j = j * n + at
+        targets.append((i, j))
+    return targets
+
+
+def exchange(pair, axis):
+    sizes = [lax.axis_size(name) for name in AXES]
+    return [lax.ppermute(buffer, AXES, swaps(sizes, axis, bool(k))) for k, buffer in enumerate(pair)]
+
+
+def is_even(axis):
+    return lax.axis_index(AXES[axis]) % 2 == 0
+
+
+class Sender:
+    def __init__(self, first, second, axis):
+        self.first, self.second, self.even = first, second, is_even(axis)
+
+    def put(self, rows, lanes, up, down):
+        self.first[rows, lanes] = jnp.where(self.even, up, down)
+        self.second[rows, lanes] = jnp.where(self.even, down, up)
+
+
+class Receiver:
+    def __init__(self, first, second, axis):
+        self.first, self.second, self.even = first, second, is_even(axis)
+
+    def before(self, *at):
+        return jnp.where(self.even, self.second[at], self.first[at])
+
+    def after(self, *at):
+        return jnp.where(self.even, self.first[at], self.second[at])
 
 
 def exact_dot(values, weights):
@@ -65,7 +111,7 @@
     return jnp.where(codes == 3.0, entries[3], value)
 
 
-def pack_x(wash_h, it_h, co_h, codes_h, theta_h, up, down, perf, it, co, codes, theta, pool, wash, sems):
+def pack_x(wash_h, it_h, co_h, codes_h, theta_h, x_one, x_two, y_one, y_two, perf, it, co, codes, theta, pool, wash, sems):
     loads = [
         pltpu.make_async_copy(src, dst, sems.at[k])
         for k, (src, dst) in enumerate(
@@ -87,75 +133,83 @@
     washed = exact_dot(rows, pairs) * 0.125
     for i in range(4):
         perf[i] = washed[i * 16 : i * 16 + 16]
-    for ref, fine, coarse in ((up, 6, 2), (down, 0, 0)):
+    to, every = Sender(x_one, x_two, 0), pl.ds(0, 256)
+    for c in range(2):
+        for k in range(2):
+            to.put(pl.ds((c * 2 + k) * 32, 32), every, it[c, 6 + k], it[c, k])
+    to.put(pl.ds(XB_CODE, 32), every, codes[7].astype(F32), codes[0].astype(F32))
+    for k in range(2):
         for c in range(2):
-            for k in range(2):
-                ref[pl.ds((c * 2 + k) * 32, 32), :] = it[c, fine + k]
-        ref[pl.ds(XB_CODE, 32), :] = codes[7 if fine else 0].astype(F32)
-        for k in range(2):
-            for c in range(2):
-                ref[pl.ds(XB_COARSE + 16 * k, 16), pl.ds(128 * c, 128)] = co[c, coarse + k]
-        for i in range(4):
-            ref[pl.ds(XB_THERM + 16 * i, 16), pl.ds(0, 128)] = theta[i]
-            ref[pl.ds(XB_THERM + 16 * i, 16), pl.ds(128, 128)] = washed[i * 16 : i * 16 + 16]
+            to.put(pl.ds(XB_COARSE + 16 * k, 16), pl.ds(128 * c, 128), co[c, 2 + k], co[c, k])
+    for i in range(4):
+        for k, value in enumerate((theta[i], washed[i * 16 : i * 16 + 16])):
+            to.put(pl.ds(XB_THERM + 16 * i, 16), pl.ds(128 * k, 128), value, value)
+    block = Columns(it, co, codes, theta, perf, None)
+    block.send_y(Sender(y_one, y_two, 1), OWN, range(2, 10), range(1, 9), range(2, 6), range(4, 8))
 
 
 class Columns:
-    def __init__(self, it, co, codes, theta, perf, before, after):
-        self.it, self.co, self.codes, self.theta, self.perf = it, co, codes, theta, perf
-        self.before, self.after = before, after
-
-    def iterate(self, c, f, rows):
-        at, n = rows
+    def __init__(self, it, co, codes, theta, perf, beside):
+        self.it, self.co, self.codes, self.theta, self.perf, self.beside = it, co, codes, theta, perf, beside
+
+    def iterate(self, c, f, at, n):
         if 2 <= f < 10:
             return self.it[c, f - 2, pl.ds(at, n), :]
-        ref, k = (self.before, f) if f < 2 else (self.after, f - 10)
-        return ref[pl.ds((c * 2 + k) * 32 + at, n), :]
-
-    def code(self, f, rows):
-        at, n = rows
+        side, k = (self.beside.before, f) if f < 2 else (self.beside.after, f - 10)
+        return side(pl.ds((c * 2 + k) * 32 + at, n), pl.ds(0, 256))
+
+    def code(self, f, at, n):
         if 1 <= f < 9:
             return self.codes[f - 1, pl.ds(at, n), :].astype(F32)
-        return (self.before if f < 1 else self.after)[pl.ds(XB_CODE + at, n), :]
-
-    def coarse(self, c, f, rows):
-        at, n = rows
+        side = self.beside.before if f < 1 else self.beside.after
+        return side(pl.ds(XB_CODE + at, n), pl.ds(0, 256))
+
+    def coarse(self, c, f, at, n):
         if 2 <= f < 6:
             return self.co[c, f - 2, pl.ds(at, n), :]
-        ref, k = (self.before, f) if f < 2 else (self.after, f - 6)
-        return ref[pl.ds(XB_COARSE + 16 * k + at, n), pl.ds(128 * c, 128)]
-
-    def warm(self, f, rows):
-        at, n = rows
+        side, k = (self.beside.before, f) if f < 2 else (self.beside.after, f - 6)
+        return side(pl.ds(XB_COARSE + 16 * k + at, n), pl.ds(128 * c, 128))
+
+    def warm(self, f, at, n):
         if 4 <= f < 8:
             return self.theta[f - 4, pl.ds(at, n), :]
-        ref, k = (self.before, f) if f < 4 else (self.after, f - 8)
-        return ref[pl.ds(XB_THERM + 16 * k + at, n), pl.ds(0, 128)]
-
-    def wash(self, f, rows):
-        at, n = rows
+        side, k = (self.beside.before, f) if f < 4 else (self.beside.after, f - 8)
+        return side(pl.ds(XB_THERM + 16 * k + at, n), pl.ds(0, 128))
+
+    def wash(self, f, at, n):
         if 3 <= f < 7:
             return self.perf[f - 3, pl.ds(at, n), :]
-        ref, k = (self.before, f + 1) if f < 3 else (self.after, f - 7)
-        return ref[pl.ds(XB_THERM + 16 * k + at, n), pl.ds(128, 128)]
-
-
-def pack_y(it, co, codes, theta, perf, before, after, after_this, up, down):
-    block = Columns(it, co, codes, theta, perf, before, after)
-    for ref, last in ((up, True), (down, False)):
-        fine, coarse, warm = ((24, 8), (8, 8), (12, 4)) if last else ((0, 8), (0, 8), (0, 4))
+        side, k = (self.beside.before, f + 1) if f < 3 else (self.beside.after, f - 7)
+        return side(pl.ds(XB_THERM + 16 * k + at, n), pl.ds(128, 128))
+
+    def send_y(self, to, start, iterates, codes, coarses, thermals):
+        every = pl.ds(0, 256)
         for c in range(2):
-            for f in range(FX):
-                ref[pl.ds((c * FX + f) * 8, 8), :] = block.iterate(c, f, fine)
-        for f in range(CX):
-            ref[pl.ds(YB_CODE + f * 8, 8), :] = block.code(f, fine)
-        for f in range(LX):
+            for k, f in enumerate(iterates):
+                rows = pl.ds((c * len(iterates) + k) * 8, 8)
+                to.put(rows, every, self.iterate(c, f, 24, 8), self.iterate(c, f, 0, 8))
+        for k, f in enumerate(codes):
+            to.put(pl.ds(start[0] + k * 8, 8), every, self.code(f, 24, 8), self.code(f, 0, 8))
+        for k, f in enumerate(coarses):
             for c in range(2):
-                ref[pl.ds(YB_COARSE + f * 8, 8), pl.ds(128 * c, 128)] = block.coarse(c, f, coarse)
-        for f in range(TX):
-            ref[pl.ds(YB_THERM + f * 4, 4), pl.ds(0, 128)] = block.warm(f, warm)
-            wash = block.wash(f - 1, warm) if 1 <= f < 11 else jnp.zeros((4, 128), F32)
-            ref[pl.ds(YB_THERM + f * 4, 4), pl.ds(128, 128)] = wash
+                rows = pl.ds(start[1] + k * 8, 8)
+                to.put(rows, pl.ds(128 * c, 128), self.coarse(c, f, 8, 8), self.coarse(c, f, 0, 8))
+        for k, f in enumerate(thermals):
+            rows = pl.ds(start[2] + k * 4, 4)
+            to.put(rows, pl.ds(0, 128), self.warm(f, 12, 4), self.warm(f, 0, 4))
+            if 1 <= f < 11:
+                to.put(rows, pl.ds(128, 128), self.wash(f - 1, 12, 4), self.wash(f - 1, 0, 4))
+            else:
+                to.put(rows, pl.ds(128, 128), jnp.zeros((4, 128), F32), jnp.zeros((4, 128), F32))
+
+
+FAR_LAYERS = ((0, 1, 10, 11), (0, 9), (0, 1, 6, 7), (0, 1, 2, 3, 8, 9, 10, 11))
+OWN_LAYERS = (tuple(range(2, 10)), tuple(range(1, 9)), tuple(range(2, 6)), tuple(range(4, 8)))
+
+
+def pack_y(it, co, codes, theta, perf, x_one, x_two, one, two):
+    block = Columns(it, co, codes, theta, perf, Receiver(x_one, x_two, 0))
+    block.send_y(Sender(one, two, 1), FAR, *FAR_LAYERS)
 
 
 def rows_of(wide, narrow, start, count, half):
@@ -169,52 +223,67 @@
     return parts[0] if len(parts) == 1 else jnp.concatenate(parts, axis=0)
 
 
-def pack_z(it, co, codes, theta, perf, before, after, below, above, wide, narrow, up, down):
-    block = Columns(it, co, codes, theta, perf, before, after)
+def pack_z(it, co, codes, theta, perf, x_one, x_two, own_one, own_two, far_one, far_two, after_this, wide, narrow, one, two):
+    block = Columns(it, co, codes, theta, perf, Receiver(x_one, x_two, 0))
+    own, far = Receiver(own_one, own_two, 1), Receiver(far_one, far_two, 1)
+
+    def beside(kind, f, height, lanes, part=0):
+        at, layers, start = (own, OWN_LAYERS[kind], OWN) if f in OWN_LAYERS[kind] else (far, FAR_LAYERS[kind], FAR)
+        row = (start[kind - 1] if kind else part * len(layers) * height) + layers.index(f) * height
+        return at.after(pl.ds(row, height), lanes), at.before(pl.ds(row, height), lanes)
+
+    every = pl.ds(0, 256)
     for c in range(2):
         for f in range(FX):
-            at, k = (c * FX + f) * 48, (c * FX + f) * 8
-            wide[pl.ds(at, 32), :] = block.iterate(c, f, (0, 32))
-            wide[pl.ds(at + 32, 8), :] = above[pl.ds(k, 8), :]
-            wide[pl.ds(at + 40, 8), :] = below[pl.ds(k, 8), :]
+            at = (c * FX + f) * 48
+            wide[pl.ds(at, 32), :] = block.iterate(c, f, 0, 32)
+            wide[pl.ds(at + 32, 8), :], wide[pl.ds(at + 40, 8), :] = beside(0, f, 8, every, c)
     for f in range(CX):
-        at, k = N_CODE + f * 48, YB_CODE + f * 8
-        wide[pl.ds(at, 32), :] = block.code(f, (0, 32))
-        wide[pl.ds(at + 32, 8), :] = above[pl.ds(k, 8), :]
-        wide[pl.ds(at + 40, 8), :] = below[pl.ds(k, 8), :]
+        at = N_CODE + f * 48
+        wide[pl.ds(at, 32), :] = block.code(f, 0, 32)
+        wide[pl.ds(at + 32, 8), :], wide[pl.ds(at + 40, 8), :] = beside(1, f, 8, every)
     row = iota((8, 128), 0)
     for c in range(2):
         for f in range(LX):
-            at, k, half = N_COARSE + (c * LX + f) * 32, YB_COARSE + f * 8, pl.ds(128 * c, 128)
-            over, under = above[pl.ds(k, 8), half], below[pl.ds(k, 8), half]
-            narrow[pl.ds(at, 16), :] = block.coarse(c, f, (0, 16))
+            at = N_COARSE + (c * LX + f) * 32
+            over, under = beside(2, f, 8, pl.ds(128 * c, 128))
+            narrow[pl.ds(at, 16), :] = block.coarse(c, f, 0, 16)
             narrow[pl.ds(at + 16, 8), :] = jnp.where(row < 4, over, under)
-            far = jnp.where(row == 1, jnp.broadcast_to(over[4:5], (8, 128)), 0.0)
-            narrow[pl.ds(at + 24, 8), :] = jnp.where(row == 0, jnp.broadcast_to(under[3:4], (8, 128)), far)
+            last = jnp.where(row == 1, jnp.broadcast_to(over[4:5], (8, 128)), 0.0)
+            narrow[pl.ds(at + 24, 8), :] = jnp.where(row == 0, jnp.broadcast_to(under[3:4], (8, 128)), last)
     for f in range(TX):
-        at, k = N_THETA + f * 24, YB_THERM + f * 4
-        narrow[pl.ds(at, 16), :] = block.warm(f, (0, 16))
-        narrow[pl.ds(at + 16, 4), :] = above[pl.ds(k, 4), pl.ds(0, 128)]
-        narrow[pl.ds(at + 20, 4), :] = below[pl.ds(k, 4), pl.ds(0, 128)]
+        at = N_THETA + f * 24
+        narrow[pl.ds(at, 16), :] = block.warm(f, 0, 16)
+        narrow[pl.ds(at + 16, 4), :], narrow[pl.ds(at + 20, 4), :] = beside(3, f, 4, pl.ds(0, 128))
     for f in range(QX):
-        at, k = N_PERF + f * 24, YB_THERM + (f + 1) * 4
-        narrow[pl.ds(at, 16), :] = block.wash(f, (0, 16))
-        narrow[pl.ds(at + 16, 4), :] = above[pl.ds(k, 4), pl.ds(128, 128)]
-        narrow[pl.ds(at + 20, 4), :] = below[pl.ds(k, 4), pl.ds(128, 128)]
+        at = N_PERF + f * 24
+        narrow[pl.ds(at, 16), :] = block.wash(f, 0, 16)
+        narrow[pl.ds(at + 16, 4), :], narrow[pl.ds(at + 20, 4), :] = beside(3, f + 1, 4, pl.ds(128, 128))
     narrow[pl.ds(N_PERF + QX * 24, NARROW - N_PERF - QX * 24), :] = jnp.zeros((NARROW - N_PERF - QX * 24, 128), F32)
     lane = iota((ZB, 128), 1) // 8
-    for ref, half, shift in ((up, 1, 8), (down, 0, 0)):
+    ends = []
+    for half, shift in ((1, 8), (0, 0)):
         packed = None
         for g in range(GROUPS):
             part = rows_of(wide, narrow, g * ZB, ZB, half)
             turn = (8 * g + shift) % 128
             part = pltpu.roll(part, turn, 1) if turn else part
             packed = part if packed is None else jnp.where(lane == g, part, packed)
-        ref[...] = packed
-
-
-def sources(coord, loc_s, exc_s, loc, after_this, field, spread, gather):
+        ends.append(packed)
+    Sender(one, two, 2).put(pl.ds(0, ZB), pl.ds(0, 128), *ends)
+
+
+def sources(loc_h, exc_h, after_this, field, spread, gather, loc_s, exc_s, loc, sems):
+    loads = [
+        pltpu.make_async_copy(src, dst, sems.at[k])
+        for k, (src, dst) in enumerate(((loc_h, loc), (loc_h, loc_s), (exc_h, exc_s)))
+    ]
+    for load in loads:
+        load.start()
     field[...] = jnp.zeros(field.shape, F32)
+    coord = [lax.axis_index(name) for name in AXES]
+    for load in loads:
+        load.wait()
     first = loc[0:1, :] - coord[0] * 8
     second = loc[1:2, :] - coord[1] * 32
     third = loc[2:3, :] - coord[2] * 256
@@ -248,14 +317,17 @@
     gather[...] = jnp.where(k == ((cell >> 1) & 255), 1.0, 0.0).astype(BF16)
 
 
-def smooth(coord, wave_t, damp_t, wide, narrow, left, right, source, spread, gather,
-           out, power, up, down, tiles, halo, grown, fine, first, second, gain_r, gain_i, pool):
+def smooth(wave_t, damp_t, wide, narrow, z_one, z_two, source, spread, gather,
+           out, power, one, two, tiles, halo, grown, fine, first, second, gain_r, gain_i, pool):
+    coord = [lax.axis_index(name) for name in AXES]
     lane = iota((ZB, 128), 1)
+    came = Receiver(z_one, z_two, 2)
+    right, left = came.after(pl.ds(0, ZB), pl.ds(0, 128)), came.before(pl.ds(0, ZB), pl.ds(0, 128))
     for g in range(GROUPS):
         turn = (128 - 8 * g) % 128
-        after = pltpu.roll(right[...], turn, 1) if turn else right[...]
+        after = pltpu.roll(right, turn, 1) if turn else right
         turn = (120 - 8 * g) % 128
-        before = pltpu.roll(left[...], turn, 1) if turn else left[...]
+        before = pltpu.roll(left, turn, 1) if turn else left
         halo[pl.ds(g * ZB, ZB), :] = jnp.where(lane < 8, after, jnp.where(lane >= 120, before, 0.0))
     tiles[...] = halo[pl.ds(WIDE + N_THETA, NARROW - N_THETA), :]
 
@@ -352,15 +424,16 @@
     sums = exact_dot(sums, gather[...]) * 0.125
     for i in range(4):
         power[i] = sums[i * 24 : i * 24 + 24]
-        if i >= 1:
-            up[i - 1] = sums[i * 24 : i * 24 + 24]
-        if i < 3:
-            down[i] = sums[i * 24 : i * 24 + 24]
-
-
-def bioheat(coord, narrow, tiles, power, before, after, injury, wave, warm_out, dose_out, wave_out, now, later, sem):
+    Sender(one, two, 0).put(pl.ds(0, 72), pl.ds(0, 256), sums[24:96], sums[0:72])
+
+
+def bioheat(narrow, tiles, power, x_one, x_two, injury, wave, warm_out, dose_out, wave_out, now, later, sem):
     store = pltpu.make_async_copy(wave, wave_out, sem)
     store.start()
+    coord = [lax.axis_index(name) for name in AXES]
+    came = Receiver(x_one, x_two, 0)
+    layer = [(pl.ds(24 * k, 24), pl.ds(0, 256)) for k in range(3)]
+    heats = [None] + [came.before(*at) for at in layer] + [power[i] for i in range(4)] + [came.after(*at) for at in layer]
 
     def flag(test):
         return jnp.where(test, 1.0, 0.0)
@@ -386,7 +459,7 @@
             beside = state[f - 1] + state[f + 1]
             beside = beside + pltpu.roll(mid, 1, 0) + pltpu.roll(mid, 23, 0)
             beside = beside + pltpu.roll(mid, 1, 1) + pltpu.roll(mid, 255, 1)
-            heat = power[f - 4] if 4 <= f < 8 else before[f - 1] if f < 4 else after[f - 8]
+            heat = heats[f]
             wash = extended(N_PERF, f - 1)
             new = mid + DIFFUSION * (beside - 6.0 * mid) - wash * mid + HEATING * heat
             other[f] = new * edge[f]
@@ -430,15 +503,16 @@
     thermal_excess,
     injury_integral,
 ):
-    it, co, codes, theta = acoustic_iterate, coarse_update, class_codes_volume, thermal_excess
-    coord = jnp.stack([lax.axis_index("gx"), lax.axis_index("gy"), lax.axis_index("gz")]).astype(jnp.int32)
-    loc = element_location.T
-
-    up, down, perf, it, co, codes, theta = call(
+    def in_hbm(*arrays):
+        return [pltpu.with_memory_space_constraint(array, pltpu.HBM) for array in arrays]
+
+    *sent, perf, it, co, codes, theta = call(
         pack_x, "pack_x", [hbm()] * 5,
         [
             shaped(XB, 256),
             shaped(XB, 256),
+            shaped(OWN[3], 256),
+            shaped(OWN[3], 256),
             shaped(4, 16, 128),
             shaped(2, 8, 32, 256),
             shaped(2, 4, 16, 128),
@@ -446,32 +520,38 @@
             shaped(4, 16, 128),
         ],
         [pltpu.VMEM((2, 128, 128), F32), pltpu.SMEM((4,), F32), pltpu.SemaphoreType.DMA((5,))],
-    )(*[pltpu.with_memory_space_constraint(a, pltpu.HBM) for a in (washout_fraction, it, co, codes, theta)])
-    before, after = exchange(up, down, "gx")
-
+    )(*in_hbm(washout_fraction, acoustic_iterate, coarse_update, class_codes_volume, thermal_excess))
+    own = (it, co, codes, theta, perf)
+    x_came = exchange(sent[:2], 0)
+    y_came = exchange(sent[2:], 1)
+
+    sent = call(pack_y, "pack_y", [vmem()] * 7, [shaped(FAR[3], 256)] * 2)(*own, *x_came)
     field, spread, gather = call(
-        sources, "sources", [smem(), smem(), smem(), vmem(), vmem()],
-        [shaped(2, CX, 48, 384), shaped(256, 384, dtype=BF16), shaped(384, 256, dtype=BF16)], cost=8000,
-    )(coord, loc, element_excitation, loc, perf)
-
-    up, down = call(pack_y, "pack_y", [vmem()] * 8, [shaped(YB, 256), shaped(YB, 256)])(
-        it, co, codes, theta, perf, before, after, gather
-    )
-    below, above = exchange(up, down, "gy")
-
-    wide, narrow, up, down = call(
-        pack_z, "pack_z", [vmem()] * 9,
+        sources, "sources", [hbm(), hbm(), vmem()],
+        [shaped(2, CX, 48, 384), shaped(256, 384, dtype=BF16), shaped(384, 256, dtype=BF16)],
+        [
+            pltpu.SMEM((3, 1024), jnp.int32),
+            pltpu.SMEM((2, 1024), F32),
+            pltpu.VMEM((3, 1024), jnp.int32),
+            pltpu.SemaphoreType.DMA((3,)),
+        ],
+        cost=8000,
+    )(*in_hbm(element_location.T, element_excitation), sent[0])
+    far_came = exchange(sent, 1)
+
+    wide, narrow, *sent = call(
+        pack_z, "pack_z", [vmem()] * 12,
         [shaped(WIDE, 256), shaped(NARROW, 128), shaped(ZB, 128), shaped(ZB, 128)],
-    )(it, co, codes, theta, perf, before, after, below, above)
-    left, right = exchange(up, down, "gz")
-
-    pressure, power, up, down, tiles = call(
-        smooth, "smooth", [smem()] * 3 + [vmem()] * 7,
+    )(*own, *x_came, *y_came, *far_came, gather)
+    z_came = exchange(sent, 2)
+
+    pressure, power, *sent, tiles = call(
+        smooth, "smooth", [smem()] * 2 + [vmem()] * 7,
         [
             shaped(2, 8, 32, 256),
             shaped(4, 24, 256),
-            shaped(3, 24, 256),
-            shaped(3, 24, 256),
+            shaped(72, 256),
+            shaped(72, 256),
             shaped(NARROW - N_THETA, 128),
         ],
         [
@@ -484,15 +564,15 @@
             pltpu.VMEM((CX, 48, 384), F32),
             pltpu.VMEM((3, 192, 128), F32),
         ],
-    )(coord, class_wavespeed, class_damping, wide, narrow, left, right, field, spread, gather)
-    before, after = exchange(up, down, "gx")
+    )(class_wavespeed, class_damping, wide, narrow, *z_came, field, spread, gather)
+    x_came = exchange(sent, 0)
 
     warmth, dose, pressure = call(
-        bioheat, "bioheat", [smem()] + [vmem()] * 7,
+        bioheat, "bioheat", [vmem()] * 7,
         [shaped(4, 16, 128), shaped(4, 16, 128), shaped(2, 8, 32, 256)],
         [pltpu.VMEM((TX, 24, 256), F32), pltpu.VMEM((TX, 24, 256), F32), pltpu.SemaphoreType.DMA],
         [vmem(), vmem(), hbm()],
-    )(coord, narrow, tiles, power, before, after, injury_integral, pressure)
+    )(narrow, tiles, power, *x_came, injury_integral, pressure)
     return pressure, warmth, dose
 
 

time: 47 us -> 38.5 us (0.82)
  the two profiles are of different devices: /device:TPU:1 before, /device:TPU:20 now
where the time goes in v3:
time: 38.5 us; the launch traced here: 38 us
  starting transfers between devices  14.6 us (38%)
  waiting for transfers between devices  11.9 us (31%)
  Pallas kernels  10.8 us (28%)
  between operations  0.71 us (2%)
    ppermute x10, starting transfers between devices, exchange(): lax.ppermute(buffer, AXES, swaps(sizes, axis, bool(k)))  14.6 us
    ppermute x10, waiting for transfers between devices, exchange(): lax.ppermute(buffer, AXES, swaps(sizes, axis, bool(k)))  11.9 us
    pallas_call x1, Pallas kernels, on_device(): call(smooth, 'smooth', [smem()] * 2 + [vmem()] * 7, [shaped(2, 8, 32, 256...  4.36 us
    pallas_call x1, Pallas kernels, on_device(): call(sources, 'sources', [hbm(), hbm(), vmem()], [shaped(2, CX, 48, 384),...  2.79 us
    pallas_call x1, Pallas kernels, on_device(): call(bioheat, 'bioheat', [vmem()] * 7, [shaped(4, 16, 128), shaped(4, 16,...  1.43 us
    pallas_call x1, Pallas kernels, on_device(): call(pack_x, 'pack_x', [hbm()] * 5, [shaped(XB, 256), shaped(XB, 256), sh...  1.42 us
  transfers between devices with their start and end apart: 10, of which 8 were waited for; matrix products, arithmetic and copies ran while one was open for 0% of the time, Pallas kernels for 7%

profile of v3, /device:TPU:20, one launch (start us, length us, event | category | flops | bytes accessed | tf_op | source)
XLA Modules:
  0.0 38.0 jit_solution(18069068989249270150)
XLA Ops:
  0.6 1.4 %pack_x.1 = (f32[256,256]{1,0:T(8,128)S(1)}, f32[256,256]{1,0:T(8,128)S(1)}, f32[240,256]{1,0:T(8,128)S(1)}, f32[240,256]{1,0:T(8,128)S(1)}, f32[4,16,128]{2,1,0...) custom-call(f32[4]{0:T(128)} %wash_h.1, ...), custom_call_target="tpu_custom_call" | custom-call | flops 2000000 | bytes 2000000 | tf_op jit(solution)/shard_map/pack_x/pallas_call | solution.py:509
  2.1 1.3 %collective-permute-start = (f32[256,256]{1,0:T(8,128)S(1)}, f32[256,256]{1,0:T(8,128)S(1)}, u32[]{:S(2)}, u32[]{:S(2)}) collective-permute-start(f32[256,256]{1,0:T(8,128)S(1)} %get-tuple-element.34), channel_id=1, source_target_pairs={{0,64},{1,65},{2,66},{3,67},{4,68},{5,69},{6,70},{7,71},{8,72},{9,... | collective-permute-start | bytes 786440 | tf_op jit(solution)/shard_map/ppermute | solution.py:67
  3.3 0.0 collective-permute-start.1
  3.4 1.9 %collective-permute-start.2 = (f32[240,256]{1,0:T(8,128)S(1)}, f32[240,256]{1,0:T(8,128)S(1)}, u32[]{:S(2)}, u32[]{:S(2)}) collective-permute-start(f32[240,256]{1,0:T(8,128)S(1)} %get-tuple-element.36), channel_id=1, source_target_pairs={{0,4},{1,5},{2,6},{3,7},{4,0},{5,1},{6,2},{7,3},{8,12},{9,13},{10,... | collective-permute-start | bytes 737288 | tf_op jit(solution)/shard_map/ppermute | solution.py:67
  5.3 4.7 %collective-permute-start.3 = (f32[240,256]{1,0:T(8,128)S(1)}, f32[240,256]{1,0:T(8,128)S(1)}, u32[]{:S(2)}, u32[]{:S(2)}) collective-permute-start(f32[240,256]{1,0:T(8,128)S(1)} %get-tuple-element.37), channel_id=1, source_target_pairs={{0,1},{1,0},{2,3},{3,2},{4,8},{5,9},{6,10},{7,11},{8,4},{9,5},{10,... | collective-permute-start | bytes 737288 | tf_op jit(solution)/shard_map/ppermute | solution.py:67
  10.0 0.2 collective-permute-done.x_one
  10.2 0.9 %collective-permute-done.1.x_two = f32[256,256]{1,0:T(8,128)S(1)} collective-permute-done((f32[256,256]{1,0:T(8,128)S(1)}, f32[256,256]{1,0:T(8,128)S(1)}, u32[]{:S(2)}, u32[]{:S(2)}) %collective-permute-start.1) | collective-permute-done | bytes 262176 | tf_op jit(solution)/shard_map/ppermute | solution.py:67
  11.1 0.0 copy-start.1
  11.1 0.0 copy-start.2
  11.2 5.7 %collective-permute-start.5 = (f32[144,256]{1,0:T(8,128)S(1)}, f32[144,256]{1,0:T(8,128)S(1)}, u32[]{:S(2)}, u32[]{:S(2)}) collective-permute-start(f32[144,256]{1,0:T(8,128)S(1)} %get-tuple-element.39), channel_id=1, source_target_pairs={{0,1},{1,0},{2,3},{3,2},{4,8},{5,9},{6,10},{7,11},{8,4},{9,5},{10,... | collective-permute-start | bytes 442376 | tf_op jit(solution)/shard_map/ppermute | solution.py:67
  16.9 0.0 collective-permute-start.4
  16.9 2.8 %sources.1 = (f32[2,10,48,384]{3,2,1,0:T(8,128)S(1)}, bf16[256,384]{1,0:T(8,128)(2,1)S(1)}, bf16[384,256]{1,0:T(8,128)(2,1)S(1)}) custom-call(s32[3,1024]{1,0:T(4,128)} %bitcast.1, f32[2,1024]{1,0:T(2,128)} %exc_h.1, f32[144,256]{1,0:T(8,128)S(1)} %get-tuple-element.38.after_this), custom_call_target="tpu_custom_call" | custom-call | flops 8000000 | bytes 8000000 | tf_op jit(solution)/shard_map/sources/pallas_call | solution.py:529
  19.7 0.0 collective-permute-done.2.own_one
  19.7 0.0 collective-permute-done.3.own_two
  19.7 0.3 collective-permute-done.5.far_two
  20.0 2.0 %collective-permute-done.4.far_one = f32[144,256]{1,0:T(8,128)S(1)} collective-permute-done((f32[144,256]{1,0:T(8,128)S(1)}, f32[144,256]{1,0:T(8,128)S(1)}, u32[]{:S(2)}, u32[]{:S(2)}) %collective-permute-start.4) | collective-permute-done | bytes 147488 | tf_op jit(solution)/shard_map/ppermute | solution.py:67
  22.0 0.8 %pack_z.1 = (f32[1632,256]{1,0:T(8,128)S(1)}, f32[1056,128]{1,0:T(8,128)S(1)}, f32[168,128]{1,0:T(8,128)S(1)}, f32[168,128]{1,0:T(8,128)S(1)}) custom-call(f32[2,8,32,256]{3,2,1,0:T(8,128)S(1)} %get-tuple-element.29.it, f32[2,4,16,128]{3,2,1,0:T(8,128)S(1)} %get-tuple-element.30.co, s32[8,32,256]{2,1,0:T(8,128)S(1)} %get-tuple-element.31.codes, ...), custom_call_target="tpu_custom_call" | custom-call | flops 2000000 | bytes 2000000 | tf_op jit(solution)/shard_map/pack_z/pallas_call | solution.py:542
  22.8 0.1 collective-permute-start.6
  22.9 0.4 collective-permute-start.7
  23.3 0.9 %collective-permute-done.6.z_one = f32[168,128]{1,0:T(8,128)S(1)} collective-permute-done((f32[168,128]{1,0:T(8,128)S(1)}, f32[168,128]{1,0:T(8,128)S(1)}, u32[]{:S(2)}, u32[]{:S(2)}) %collective-permute-start.6) | collective-permute-done | bytes 86048 | tf_op jit(solution)/shard_map/ppermute | solution.py:67
  24.2 3.3 %collective-permute-done.7.z_two = f32[168,128]{1,0:T(8,128)S(1)} collective-permute-done((f32[168,128]{1,0:T(8,128)S(1)}, f32[168,128]{1,0:T(8,128)S(1)}, u32[]{:S(2)}, u32[]{:S(2)}) %collective-permute-start.7) | collective-permute-done | bytes 86048 | tf_op jit(solution)/shard_map/ppermute | solution.py:67
  27.5 0.0 copy-done.1
  27.5 0.0 copy-done.2
  27.5 0.0 copy-start
  27.5 4.4 %smooth.1 = (f32[2,8,32,256]{3,2,1,0:T(8,128)S(1)}, f32[4,24,256]{2,1,0:T(8,128)S(1)}, f32[72,256]{1,0:T(8,128)S(1)}, f32[72,256]{1,0:T(8,128)S(1)}, f32[544,128]{1,0:T(8,128)S(1)}) custom-call(f32[4]{0:T(128)S(1)} %copy-done.1, f32[4]{0:T(128)S(1)} %copy-done.2, f32[1632,256]{1,0:T(8,128)S(1)} %get-tuple-element.42.wide, ...), custom_call_target="tpu_custom_call" | custom-call | flops 2000000 | bytes 2000000 | tf_op jit(solution)/shard_map/smooth/pallas_call | solution.py:548
  31.8 0.4 collective-permute-start.8
  32.2 0.1 collective-permute-start.9
  32.3 4.0 %collective-permute-done.8.x_one = f32[72,256]{1,0:T(8,128)S(1)} collective-permute-done((f32[72,256]{1,0:T(8,128)S(1)}, f32[72,256]{1,0:T(8,128)S(1)}, u32[]{:S(2)}, u32[]{:S(2)}) %collective-permute-start.8) | collective-permute-done | bytes 73760 | tf_op jit(solution)/shard_map/ppermute | solution.py:67
  36.3 0.3 collective-permute-done.9.x_two
  36.6 0.0 copy-done
  36.6 1.4 %bioheat.1 = (f32[4,16,128]{2,1,0:T(8,128)}, f32[4,16,128]{2,1,0:T(8,128)}, f32[2,8,32,256]{3,2,1,0:T(8,128)}) custom-call(f32[1056,128]{1,0:T(8,128)S(1)} %get-tuple-element.41.narrow, f32[544,128]{1,0:T(8,128)S(1)} %get-tuple-element.47.tiles, f32[4,24,256]{2,1,0:T(8,128)S(1)} %get-tuple-element.48.power, f32[72,256]{1,0:T(8,128)S(1)} %collective-permute-done.8.x_one, ...), custom_call_target="tpu_custom_call" | custom-call | flops 2000000 | bytes 2000000 | tf_op jit(solution)/shard_map/bioheat/pallas_call | solution.py:570
  (1 shorter events, 0.0 us)
Async XLA Ops:
  2.1 8.1 %collective-permute-start = (f32[256,256]{1,0:T(8,128)S(1)}, f32[256,256]{1,0:T(8,128)S(1)}, u32[]{:S(2)}, u32[]{:S(2)}) collective-permute-start(f32[256,256]{1,0:T(8,128)S(1)} %get-tuple-element.34), channel_id=1, source_target_pairs={{0,64},{1,65},{2,66},{3,67},{4,68},{5,69},{6,70},{7,71},{8,72},{9,... | collective-permute-start | bytes 786440 | tf_op jit(solution)/shard_map/ppermute | solution.py:67
  3.3 7.8 %collective-permute-start.1 = (f32[256,256]{1,0:T(8,128)S(1)}, f32[256,256]{1,0:T(8,128)S(1)}, u32[]{:S(2)}, u32[]{:S(2)}) collective-permute-start(f32[256,256]{1,0:T(8,128)S(1)} %get-tuple-element.35), channel_id=1, source_target_pairs={{0,1},{1,0},{2,3},{3,2},{4,5},{5,4},{6,7},{7,6},{8,9},{9,8},{10,11... | collective-permute-start | bytes 786440 | tf_op jit(solution)/shard_map/ppermute | solution.py:67
  3.4 16.3 %collective-permute-start.2 = (f32[240,256]{1,0:T(8,128)S(1)}, f32[240,256]{1,0:T(8,128)S(1)}, u32[]{:S(2)}, u32[]{:S(2)}) collective-permute-start(f32[240,256]{1,0:T(8,128)S(1)} %get-tuple-element.36), channel_id=1, source_target_pairs={{0,4},{1,5},{2,6},{3,7},{4,0},{5,1},{6,2},{7,3},{8,12},{9,13},{10,... | collective-permute-start | bytes 737288 | tf_op jit(solution)/shard_map/ppermute | solution.py:67
  5.3 14.4 %collective-permute-start.3 = (f32[240,256]{1,0:T(8,128)S(1)}, f32[240,256]{1,0:T(8,128)S(1)}, u32[]{:S(2)}, u32[]{:S(2)}) collective-permute-start(f32[240,256]{1,0:T(8,128)S(1)} %get-tuple-element.37), channel_id=1, source_target_pairs={{0,1},{1,0},{2,3},{3,2},{4,8},{5,9},{6,10},{7,11},{8,4},{9,5},{10,... | collective-permute-start | bytes 737288 | tf_op jit(solution)/shard_map/ppermute | solution.py:67
  11.1 16.4 %copy-start.1 = (f32[4]{0:T(128)S(1)}, f32[4]{0:T(128)}, u32[]{:S(2)}) copy-start(f32[4]{0:T(128)} %wave_t.1) | copy-start | bytes 52
  11.1 16.4 %copy-start.2 = (f32[4]{0:T(128)S(1)}, f32[4]{0:T(128)}, u32[]{:S(2)}) copy-start(f32[4]{0:T(128)} %damp_t.1) | copy-start | bytes 52
  11.2 8.8 %collective-permute-start.5 = (f32[144,256]{1,0:T(8,128)S(1)}, f32[144,256]{1,0:T(8,128)S(1)}, u32[]{:S(2)}, u32[]{:S(2)}) collective-permute-start(f32[144,256]{1,0:T(8,128)S(1)} %get-tuple-element.39), channel_id=1, source_target_pairs={{0,1},{1,0},{2,3},{3,2},{4,8},{5,9},{6,10},{7,11},{8,4},{9,5},{10,... | collective-permute-start | bytes 442376 | tf_op jit(solution)/shard_map/ppermute | solution.py:67
  16.9 5.1 %collective-permute-start.4 = (f32[144,256]{1,0:T(8,128)S(1)}, f32[144,256]{1,0:T(8,128)S(1)}, u32[]{:S(2)}, u32[]{:S(2)}) collective-permute-start(f32[144,256]{1,0:T(8,128)S(1)} %get-tuple-element.38.after_this), channel_id=1, source_target_pairs={{0,4},{1,5},{2,6},{3,7},{4,0},{5,1},{6,2},{7,3},{8,12},{9,13},{10,... | collective-permute-start | bytes 442376 | tf_op jit(solution)/shard_map/ppermute | solution.py:67
  22.8 1.4 %collective-permute-start.6 = (f32[168,128]{1,0:T(8,128)S(1)}, f32[168,128]{1,0:T(8,128)S(1)}, u32[]{:S(2)}, u32[]{:S(2)}) collective-permute-start(f32[168,128]{1,0:T(8,128)S(1)} %get-tuple-element.43), channel_id=1, source_target_pairs={{0,1},{1,0},{2,3},{3,2},{4,5},{5,4},{6,7},{7,6},{8,9},{9,8},{10,11... | collective-permute-start | bytes 258056 | tf_op jit(solution)/shard_map/ppermute | solution.py:67
  22.9 4.6 %collective-permute-start.7 = (f32[168,128]{1,0:T(8,128)S(1)}, f32[168,128]{1,0:T(8,128)S(1)}, u32[]{:S(2)}, u32[]{:S(2)}) collective-permute-start(f32[168,128]{1,0:T(8,128)S(1)} %get-tuple-element.44), channel_id=1, source_target_pairs={{0,64},{1,2},{2,1},{3,67},{4,68},{5,6},{6,5},{7,71},{8,72},{9,10},... | collective-permute-start | bytes 258056 | tf_op jit(solution)/shard_map/ppermute | solution.py:67
  27.5 9.1 %copy-start = (f32[4,16,128]{2,1,0:T(8,128)S(1)}, f32[4,16,128]{2,1,0:T(8,128)}, u32[]{:S(2)}) copy-start(f32[4,16,128]{2,1,0:T(8,128)} %injury.1) | copy-start | bytes 98308
  31.8 4.4 %collective-permute-start.8 = (f32[72,256]{1,0:T(8,128)S(1)}, f32[72,256]{1,0:T(8,128)S(1)}, u32[]{:S(2)}, u32[]{:S(2)}) collective-permute-start(f32[72,256]{1,0:T(8,128)S(1)} %get-tuple-element.49), channel_id=1, source_target_pairs={{0,64},{1,65},{2,66},{3,67},{4,68},{5,69},{6,70},{7,71},{8,72},{9,... | collective-permute-start | bytes 221192 | tf_op jit(solution)/shard_map/ppermute | solution.py:67
  32.2 4.4 %collective-permute-start.9 = (f32[72,256]{1,0:T(8,128)S(1)}, f32[72,256]{1,0:T(8,128)S(1)}, u32[]{:S(2)}, u32[]{:S(2)}) collective-permute-start(f32[72,256]{1,0:T(8,128)S(1)} %get-tuple-element.50), channel_id=1, source_target_pairs={{0,1},{1,0},{2,3},{3,2},{4,5},{5,4},{6,7},{7,6},{8,9},{9,8},{10,11... | collective-permute-start | bytes 221192 | tf_op jit(solution)/shard_map/ppermute | solution.py:67

commit v4 on v3

v4 whole, which is shorter than its diff:
```python
import jax
import jax.numpy as jnp
from jax import lax
from jax.experimental import pallas as pl
from jax.experimental.pallas import tpu as pltpu
from jax.sharding import PartitionSpec as P

F32 = jnp.float32
BF16 = jnp.bfloat16

RELAXATION = 0.8
DAMPING_SHIFT = 0.5
DIFFUSION = 0.15
HEATING = 0.25
LN_PREFACTOR = 226.78
ENERGY_BARRIER = 75535.0
CORE_WARMTH = 310.15

FX, CX, LX, TX, QX = 12, 10, 8, 12, 10
XB_CODE, XB_COARSE, XB_THERM, XB = 128, 160, 192, 256
YB_CODE, YB_COARSE, YB_THERM, YB = 128, 192, 212, 232
KB_CODE, KB_COARSE, KB_THERM, KB = 64, 80, 100, 128
WIDE = 2 * FX * 48 + CX * 48
N_CODE = 2 * FX * 48
N_COARSE, N_THETA, N_PERF, NARROW = 0, 512, 800, 1056
GROUPS = 16
ZB = (WIDE + NARROW) // GROUPS
AXES = ("gx", "gy", "gz")


def vmem():
    return pl.BlockSpec(memory_space=pltpu.VMEM)


def hbm():
    return pl.BlockSpec(memory_space=pltpu.HBM)


def smem():
    return pl.BlockSpec(memory_space=pltpu.SMEM)


def swaps(sizes, axis, odd):
    count, targets = 1, []
    for n in sizes:
        count *= n
    for i in range(count):
        place, rest = [], i
        for n in reversed(sizes):
            place.insert(0, rest % n)
            rest //= n
        partner = list(place)
        partner[axis] = ((place[axis] + 1) ^ 1) - 1 if odd else place[axis] ^ 1
        if not 0 <= partner[axis] < sizes[axis]:
            other = 2 if axis != 2 else 0
            partner = list(place)
            partner[other] = place[other] ^ 1
        j = 0
        for n, at in zip(sizes, partner):
            j = j * n + at
        targets.append((i, j))
    return targets


def exchange(pair, axis):
    sizes = [lax.axis_size(name) for name in AXES]
    return [lax.ppermute(buffer, AXES, swaps(sizes, axis, (axis == 1) != (k == 1))) for k, buffer in enumerate(pair)]


def is_even(axis):
    return lax.axis_index(AXES[axis]) % 2 == (1 if axis == 1 else 0)


class Sender:
    def __init__(self, first, second, axis):
        self.first, self.second, self.even = first, second, is_even(axis)

    def put(self, rows, lanes, up, down):
        self.first[rows, lanes] = jnp.where(self.even, up, down)
        self.second[rows, lanes] = jnp.where(self.even, down, up)


class Receiver:
    def __init__(self, first, second, axis):
        self.first, self.second, self.even = first, second, is_even(axis)

    def before(self, *at):
        return jnp.where(self.even, self.second[at], self.first[at])

    def after(self, *at):
        return jnp.where(self.even, self.first[at], self.second[at])


def exact_dot(values, weights):
    high = values.astype(BF16)
    rest = values - high.astype(F32)
    mid = rest.astype(BF16)
    low = (rest - mid.astype(F32)).astype(BF16)
    total = jnp.dot(high, weights, preferred_element_type=F32)
    total = total + jnp.dot(mid, weights, preferred_element_type=F32)
    return total + jnp.dot(low, weights, preferred_element_type=F32)


def iota(shape, dim):
    return lax.broadcasted_iota(jnp.int32, shape, dim)


def pick(codes, entries):
    value = jnp.where(codes == 0.0, entries[0], entries[1])
    value = jnp.where(codes == 2.0, entries[2], value)
    return jnp.where(codes == 3.0, entries[3], value)


def pack_x(wash_h, it_h, co_h, codes_h, theta_h, x_one, x_two, y_one, y_two, perf, it, co, codes, theta, pool, wash, sems):
    loads = [
        pltpu.make_async_copy(src, dst, sems.at[k])
        for k, (src, dst) in enumerate(
            ((codes_h, codes), (it_h, it), (wash_h, wash), (co_h, co), (theta_h, theta))
        )
    ]
    for load in loads:
        load.start()
    lane, col = iota((256, 128), 0), iota((256, 128), 1)
    pairs = jnp.where(lane // 2 == col, 1.0, 0.0).astype(BF16)
    for load in loads:
        load.wait()
    entries = [wash[k] for k in range(4)]
    for i in range(4):
        both = pick(codes[2 * i].astype(F32), entries) + pick(codes[2 * i + 1].astype(F32), entries)
        for half in range(2):
            pool[half, i * 32 : i * 32 + 32, :] = both[:, half * 128 : half * 128 + 128]
    rows = jnp.concatenate([pool[h, pl.ds(0, 64, 2), :] + pool[h, pl.ds(1, 64, 2), :] for h in range(2)], axis=1)
    washed = exact_dot(rows, pairs) * 0.125
    for i in range(4):
        perf[i] = washed[i * 16 : i * 16 + 16]
    to, every = Sender(x_one, x_two, 0), pl.ds(0, 256)
    for c in range(2):
        for k in range(2):
            to.put(pl.ds((c * 2 + k) * 32, 32), every, it[c, 6 + k], it[c, k])
    to.put(pl.ds(XB_CODE, 32), every, codes[7].astype(F32), codes[0].astype(F32))
    for k in range(2):
        for c in range(2):
            to.put(pl.ds(XB_COARSE + 16 * k, 16), pl.ds(128 * c, 128), co[c, 2 + k], co[c, k])
    for i in range(4):
        for k, value in enumerate((theta[i], washed[i * 16 : i * 16 + 16])):
            to.put(pl.ds(XB_THERM + 16 * i, 16), pl.ds(128 * k, 128), value, value)
    to = Sender(y_one, y_two, 1)
    for c in range(2):
        for k in range(8):
            to.put(pl.ds((c * 8 + k) * 8, 8), every, it[c, k, 24:32, :], it[c, k, 0:8, :])
    for k in range(8):
        to.put(pl.ds(YB_CODE + k * 8, 8), every, codes[k, 24:32, :].astype(F32), codes[k, 0:8, :].astype(F32))
    for k in range(4):
        for c in range(2):
            to.put(pl.ds(YB_COARSE + k * 5, 5), pl.ds(128 * c, 128), co[c, k, 11:16, :], co[c, k, 0:5, :])
        for c, field in enumerate((theta, perf)):
            to.put(pl.ds(YB_THERM + k * 4, 4), pl.ds(128 * c, 128), field[k, 12:16, :], field[k, 0:4, :])


class Columns:
    def __init__(self, it, co, codes, theta, perf, beside):
        self.it, self.co, self.codes, self.theta, self.perf, self.beside = it, co, codes, theta, perf, beside

    def iterate(self, c, f, at, n):
        if 2 <= f < 10:
            return self.it[c, f - 2, pl.ds(at, n), :]
        side, k = (self.beside.before, f) if f < 2 else (self.beside.after, f - 10)
        return side(pl.ds((c * 2 + k) * 32 + at, n), pl.ds(0, 256))

    def code(self, f, at, n):
        if 1 <= f < 9:
            return self.codes[f - 1, pl.ds(at, n), :].astype(F32)
        side = self.beside.before if f < 1 else self.beside.after
        return side(pl.ds(XB_CODE + at, n), pl.ds(0, 256))

    def coarse(self, c, f, at, n):
        if 2 <= f < 6:
            return self.co[c, f - 2, pl.ds(at, n), :]
        side, k = (self.beside.before, f) if f < 2 else (self.beside.after, f - 6)
        return side(pl.ds(XB_COARSE + 16 * k + at, n), pl.ds(128 * c, 128))

    def warm(self, f, at, n):
        if 4 <= f < 8:
            return self.theta[f - 4, pl.ds(at, n), :]
        side, k = (self.beside.before, f) if f < 4 else (self.beside.after, f - 8)
        return side(pl.ds(XB_THERM + 16 * k + at, n), pl.ds(0, 128))

    def wash(self, f, at, n):
        if 3 <= f < 7:
            return self.perf[f - 3, pl.ds(at, n), :]
        side, k = (self.beside.before, f + 1) if f < 3 else (self.beside.after, f - 7)
        return side(pl.ds(XB_THERM + 16 * k + at, n), pl.ds(128, 128))


def pack_corner(y_one, y_two, after_this, one, two):
    came, to = Receiver(y_one, y_two, 1), Sender(one, two, 0)

    def put(at, n, lanes, up, down):
        for k, side in enumerate((came.after, came.before)):
            to.put(pl.ds(at + k * n, n), lanes, side(pl.ds(up, n), lanes), side(pl.ds(down, n), lanes))

    every = pl.ds(0, 256)
    for c in range(2):
        for k in range(2):
            put((c * 2 + k) * 16, 8, every, (c * 8 + 6 + k) * 8, (c * 8 + k) * 8)
    put(KB_CODE, 8, every, YB_CODE + 56, YB_CODE)
    for k in range(2):
        put(KB_COARSE + k * 10, 5, every, YB_COARSE + (2 + k) * 5, YB_COARSE + k * 5)
    for k in range(3):
        put(KB_THERM + k * 8, 4, every, YB_THERM + (1 + k) * 4, YB_THERM + k * 4)


def rows_of(wide, narrow, start, count, half):
    parts = []
    if start < WIDE:
        n = min(count, WIDE - start)
        parts.append(wide[pl.ds(start, n), pl.ds(128 * half, 128)])
        start, count = start + n, count - n
    if count:
        parts.append(narrow[pl.ds(start - WIDE, count), :])
    return parts[0] if len(parts) == 1 else jnp.concatenate(parts, axis=0)


def pack_z(it, co, codes, theta, perf, x_one, x_two, y_one, y_two, k_one, k_two, wide, narrow, one, two):
    block = Columns(it, co, codes, theta, perf, Receiver(x_one, x_two, 0))
    rows, corners = Receiver(y_one, y_two, 1), Receiver(k_one, k_two, 0)

    def beside(f, first, count, height, own, corner, lanes, skip=0):
        k = f - first
        if 0 <= k < count:
            at = pl.ds(own + k * height, height)
            return rows.after(at, lanes), rows.before(at, lanes)
        side, k = (corners.before, f - skip) if k < 0 else (corners.after, k - count)
        return [side(pl.ds(corner + (2 * k + j) * height, height), lanes) for j in range(2)]

    every = pl.ds(0, 256)
    for c in range(2):
        for f in range(FX):
            at = (c * FX + f) * 48
            wide[pl.ds(at, 32), :] = block.iterate(c, f, 0, 32)
            wide[pl.ds(at + 32, 8), :], wide[pl.ds(at + 40, 8), :] = beside(f, 2, 8, 8, c * 64, c * 32, every)
    for f in range(CX):
        at = N_CODE + f * 48
        wide[pl.ds(at, 32), :] = block.code(f, 0, 32)
        wide[pl.ds(at + 32, 8), :], wide[pl.ds(at + 40, 8), :] = beside(f, 1, 8, 8, YB_CODE, KB_CODE, every)
    for c in range(2):
        for f in range(LX):
            at = N_COARSE + (c * LX + f) * 32
            over, under = beside(f, 2, 4, 5, YB_COARSE, KB_COARSE, pl.ds(128 * c, 128))
            narrow[pl.ds(at, 16), :] = block.coarse(c, f, 0, 16)
            narrow[pl.ds(at + 24, 8), :] = jnp.zeros((8, 128), F32)
            narrow[pl.ds(at + 16, 4), :] = over[0:4]
            narrow[pl.ds(at + 20, 4), :] = under[1:5]
            narrow[pl.ds(at + 24, 1), :] = under[0:1]
            narrow[pl.ds(at + 25, 1), :] = over[4:5]
    for f in range(TX):
        at = N_THETA + f * 24
        narrow[pl.ds(at, 16), :] = block.warm(f, 0, 16)
        if 0 < f < 11:
            over, under = beside(f, 4, 4, 4, YB_THERM, KB_THERM, pl.ds(0, 128), 1)
        else:
            over = under = jnp.zeros((4, 128), F32)
        narrow[pl.ds(at + 16, 4), :], narrow[pl.ds(at + 20, 4), :] = over, under
    for f in range(QX):
        at = N_PERF + f * 24
        narrow[pl.ds(at, 16), :] = block.wash(f, 0, 16)
        over, under = beside(f + 1, 4, 4, 4, YB_THERM, KB_THERM, pl.ds(128, 128), 1)
        narrow[pl.ds(at + 16, 4), :], narrow[pl.ds(at + 20, 4), :] = over, under
    narrow[pl.ds(N_PERF + QX * 24, NARROW - N_PERF - QX * 24), :] = jnp.zeros((NARROW - N_PERF - QX * 24, 128), F32)
    lane = iota((ZB, 128), 1) // 8
    ends = []
    for half, shift in ((1, 8), (0, 0)):
        packed = None
        for g in range(GROUPS):
            part = rows_of(wide, narrow, g * ZB, ZB, half)
            turn = (8 * g + shift) % 128
            part = pltpu.roll(part, turn, 1) if turn else part
            packed = part if packed is None else jnp.where(lane == g, part, packed)
        ends.append(packed)
    Sender(one, two, 2).put(pl.ds(0, ZB), pl.ds(0, 128), *ends)


def strip_cell(lane):
    return jnp.where(lane < 32, lane, jnp.where(lane < 96, lane + 192, lane - 128))


def sources(loc_h, exc_h, after_this, field, strip, spread, gather, spread_strip, gather_strip, loc_s, exc_s, loc, sems):
    loads = [
        pltpu.make_async_copy(src, dst, sems.at[k])
        for k, (src, dst) in enumerate(((loc_h, loc), (loc_h, loc_s), (exc_h, exc_s)))
    ]
    for load in loads:
        load.start()
    field[...] = jnp.zeros(field.shape, F32)
    strip[...] = jnp.zeros(strip.shape, F32)
    coord = [lax.axis_index(name) for name in AXES]
    for load in loads:
        load.wait()
    first = loc[0:1, :] - coord[0] * 8
    second = loc[1:2, :] - coord[1] * 32
    third = loc[2:3, :] - coord[2] * 256
    near = (first >= -1) & (first < 9) & (second >= -7) & (second < 39) & (third >= -7) & (third < 263)
    order = iota((1, 1024), 1)
    lane, cell = iota((1, 256), 1), strip_cell(iota((1, 128), 1))

    def place(state):
        e, keys = state
        x = loc_s[0, e] - coord[0] * 8 + 1
        y = loc_s[1, e] - coord[1] * 32
        z = loc_s[2, e] - coord[2] * 256
        y = jnp.where(y < 0, y + 48, y)
        for c in range(2):
            field[c, x, pl.ds(y, 1), :] += jnp.where(lane == z, exc_s[c, e], 0.0)
            strip[c, x, pl.ds(y, 1), :] += jnp.where(cell == z, exc_s[c, e], 0.0)
        keys = jnp.where(order == e, 1024, keys)
        return jnp.min(keys), keys

    keys = jnp.where(near, order, 1024)
    lax.while_loop(lambda state: state[0] < 1024, place, (jnp.min(keys), keys))

    def weights(cell, column, at):
        centre = cell >> 1
        beside = centre + jnp.where((cell & 1) == 1, 1, -1)
        weight = jnp.where(column == at(centre), 0.75, jnp.where(column == at(beside), 0.25, 0.0))
        return weight.astype(BF16)

    spread[...] = weights(iota((128, 256), 1), iota((128, 256), 0), lambda c: c)
    spread_strip[...] = weights(
        strip_cell(iota((256, 128), 1)),
        iota((256, 128), 0),
        lambda c: jnp.where(c < 0, c + 256, jnp.where(c < 128, c, c + 64)),
    )
    gather[...] = jnp.where(iota((256, 128), 1) == iota((256, 128), 0) >> 1, 1.0, 0.0).astype(BF16)
    centre = strip_cell(iota((128, 256), 0)) >> 1
    centre = jnp.where(centre < 0, centre + 256, centre)
    gather_strip[...] = jnp.where(iota((128, 256), 1) == centre, 1.0, 0.0).astype(BF16)


def flag(test):
    return jnp.where(test, 1.0, 0.0)


def x_flags():
    at = lax.axis_index("gx")
    return flag(at > 0), flag(at < 3)


def along_y(cells, row):
    lanes = cells.shape[1]
    centre = cells[0:24]
    lower = jnp.where(row == 20, jnp.broadcast_to(cells[24:25], (24, lanes)), pltpu.roll(centre, 1, 0))
    upper = jnp.where(row == 19, jnp.broadcast_to(cells[25:26], (24, lanes)), pltpu.roll(centre, 23, 0))
    return 0.75 * centre + 0.25 * lower, 0.75 * centre + 0.25 * upper


def coarse_rows(read, z_ok, grown):
    x_before, x_after = x_flags()
    at_y = lax.axis_index("gy")
    row = iota((32, 128), 0)
    y_ok = jnp.where(row < 16, 1.0, jnp.where((row < 20) | (row == 25), flag(at_y < 15), flag(at_y > 0)))
    inside = y_ok if z_ok is None else y_ok * z_ok
    row = iota((24, 128), 0)
    for c in range(2):
        for f in range(LX):
            x_ok = x_before if f < 2 else x_after if f >= 6 else None
            even, odd = along_y(read((c * LX + f) * 32) * (inside if x_ok is None else inside * x_ok), row)
            to = (c * LX + f) * 48
            grown[pl.ds(to, 24, 2), :] = even
            grown[pl.ds(to + 1, 24, 2), :] = odd


def relax(width, start, classes, z_ok, fine, drive, wave_t, damp_t, first, second, gain_r, gain_i, pool, emit):
    x_before, x_after = x_flags()
    at_y = lax.axis_index("gy")
    row = iota((48, width), 0)
    inside = jnp.where(row < 32, 1.0, jnp.where(row < 40, flag(at_y < 15), flag(at_y > 0)))
    if z_ok is not None:
        inside = inside * z_ok
    for c in range(2):
        for f in range(FX):
            near = c * LX + f // 2 + 1
            far = near + (1 if f % 2 else -1)
            grow = 0.75 * fine[pl.ds(near * 48, 48), :] + 0.25 * fine[pl.ds(far * 48, 48), :]
            x_ok = x_before if f < 2 else x_after if f >= 10 else None
            first[c, f] = (start((c * FX + f) * 48) + grow) * (inside if x_ok is None else inside * x_ok)

    gains_r, gains_i, damps = [], [], []
    for t in range(4):
        speed = jnp.full((8, 128), wave_t[t], F32)
        damp = jnp.full((8, 128), damp_t[t], F32)
        wave = 1.0 / (speed * speed)
        diag_r = 6.0 - wave
        diag_i = DAMPING_SHIFT * wave + damp
        modulus = diag_r * diag_r + diag_i * diag_i
        gains_r.append((RELAXATION * diag_r / modulus)[0:1, 0:1])
        gains_i.append((RELAXATION * diag_i / modulus)[0:1, 0:1])
        damps.append(damp_t[t])

    def step(cells, f, drive_f, g_r, g_i):
        sums = []
        for c in range(2):
            mid = cells[c, f]
            total = cells[c, f - 1] + cells[c, f + 1] + drive[c, drive_f]
            total = total + pltpu.roll(mid, 1, 0) + pltpu.roll(mid, 47, 0)
            sums.append((mid, total + pltpu.roll(mid, 1, 1) + pltpu.roll(mid, width - 1, 1)))
        (mid_r, sum_r), (mid_i, sum_i) = sums
        keep = 1.0 - RELAXATION
        return keep * mid_r + (g_r * sum_r + g_i * sum_i), keep * mid_i + (g_r * sum_i - g_i * sum_r)

    for f in range(CX):
        codes = classes(N_CODE + f * 48)
        x_ok = x_before if f < 1 else x_after if f >= 9 else None
        ok = inside if x_ok is None else inside * x_ok
        g_r = pick(codes, gains_r) * ok
        g_i = pick(codes, gains_i) * ok
        gain_r[f], gain_i[f] = g_r, g_i
        second[0, f], second[1, f] = step(first, f + 1, f, g_r, g_i)

    for i in range(4):
        heat = None
        for f in (2 * i, 2 * i + 1):
            new_r, new_i = step(second, f + 1, f + 1, gain_r[f + 1], gain_i[f + 1])
            emit(f, new_r, new_i)
            layer = pick(classes(N_CODE + (f + 1) * 48), damps) * (new_r * new_r + new_i * new_i)
            heat = layer if heat is None else heat + layer
        for tile in range(width // 128):
            pool[tile, pl.ds(i * 48, 48), :] = heat[:, tile * 128 : tile * 128 + 128]
    tiles = [pool[t, pl.ds(0, 96, 2), :] + pool[t, pl.ds(1, 96, 2), :] for t in range(width // 128)]
    return tiles[0] if len(tiles) == 1 else jnp.concatenate(tiles, axis=1)


def smooth_inner(wave_t, damp_t, wide, narrow, source, spread, gather, out, power, grown,
                 fine, first, second, gain_r, gain_i, pool):
    coarse_rows(lambda at: narrow[pl.ds(N_COARSE + at, 32), :], None, grown)
    fine[...] = exact_dot(grown[...], spread[...])

    def own(at):
        return wide[pl.ds(at, 48), :]

    def emit(f, new_r, new_i):
        out[0, f] = new_r[0:32]
        out[1, f] = new_i[0:32]

    sums = relax(256, own, own, None, fine, source, wave_t, damp_t, first, second, gain_r, gain_i, pool, emit)
    power[...] = exact_dot(sums, gather[...]) * 0.125


def smooth_ends(wave_t, damp_t, wide, z_one, z_two, source, spread, gather, inner, power_inner, grown,
                out, power, power_halo, one, two, tiles,
                halo, grown_halo, fine, first, second, gain_r, gain_i, pool):
    lane = iota((ZB, 128), 1)
    came, every = Receiver(z_one, z_two, 2), (pl.ds(0, ZB), pl.ds(0, 128))
    right, left = came.after(*every), came.before(*every)
    for g in range(GROUPS):
        turn = (192 - 8 * g) % 128
        after = pltpu.roll(right, turn, 1) if turn else right
        turn = (120 - 8 * g) % 128
        before = pltpu.roll(left, turn, 1) if turn else left
        halo[pl.ds(g * ZB, ZB), :] = jnp.where(lane < 96, after, before)
    beyond = halo[pl.ds(WIDE + N_THETA, NARROW - N_THETA), :]
    tiles[...] = jnp.where(iota(beyond.shape, 1) < 64, pltpu.roll(beyond, 64, 1), beyond)

    at_z = lax.axis_index("gz")
    after_ok, before_ok = flag(at_z < 3), flag(at_z > 0)
    z_ok = jnp.where(iota((32, 128), 1) < 96, after_ok, before_ok)
    coarse_rows(lambda at: halo[pl.ds(WIDE + N_COARSE + at, 32), :], z_ok, grown_halo)
    fine[...] = exact_dot(jnp.concatenate([grown[...], grown_halo[...]], axis=1), spread[...])

    lane = iota((48, 128), 1)

    def strip(at):
        ends = jnp.where(lane < 32, wide[pl.ds(at, 48), pl.ds(0, 128)], pltpu.roll(wide[pl.ds(at, 48), pl.ds(128, 128)], 64, 1))
        return jnp.where(lane < 64, ends, halo[pl.ds(at, 48), :])

    low, high = iota((32, 128), 1) < 8, iota((32, 128), 1) >= 120

    def emit(f, new_r, new_i):
        for c, new in enumerate((new_r[0:32], new_i[0:32])):
            out[c, f, :, pl.ds(0, 128)] = jnp.where(low, new, inner[c, f, :, pl.ds(0, 128)])
            out[c, f, :, pl.ds(128, 128)] = jnp.where(high, pltpu.roll(new, 64, 1), inner[c, f, :, pl.ds(128, 128)])

    z_ok = jnp.where(lane < 64, 1.0, jnp.where(lane < 96, after_ok, before_ok))
    live = jnp.where((lane < 72) | (lane >= 120), z_ok, 0.0)
    sums = relax(128, strip, strip, live, fine, source, wave_t, damp_t, first, second, gain_r, gain_i, pool, emit)
    sums = exact_dot(sums, gather[...]) * 0.125
    lane = iota((96, 128), 1)
    own = jnp.where((lane < 4) | (lane >= 124), sums[:, 0:128], power_inner[...])
    over = sums[:, 128:256]
    power[...], power_halo[...] = own, over

    def packed(first_layer):
        group, total = iota((24, 128), 1) // 16, None
        for k in range(3):
            at = (first_layer + k) * 24
            turned = pltpu.roll(over[at : at + 24], 16 * k + 8, 1)
            total = turned if total is None else jnp.where(group == k, turned, total)
        return total

    to, every = Sender(one, two, 0), pl.ds(0, 128)
    to.put(pl.ds(0, 72), every, own[24:96], own[0:72])
    to.put(pl.ds(72, 24), every, packed(1), packed(0))


def bioheat(narrow, tiles, power, power_halo, x_one, x_two, injury, wave, warm_out, dose_out, wave_out, now, later, sem):
    store = pltpu.make_async_copy(wave, wave_out, sem)
    store.start()
    coord = [lax.axis_index(name) for name in AXES]
    came = Receiver(x_one, x_two, 0)

    def sent(side, k):
        beyond = side(pl.ds(72, 24), pl.ds(0, 128))
        beyond = jnp.where(iota((24, 128), 1) // 16 == k, beyond, 0.0)
        return jnp.concatenate([side(pl.ds(24 * k, 24), pl.ds(0, 128)), pltpu.roll(beyond, 120 - 16 * k, 1)], axis=1)

    own = [jnp.concatenate([ref[pl.ds(24 * i, 24), :] for ref in (power, power_halo)], axis=1) for i in range(4)]
    heats = [None] + [sent(came.before, k) for k in range(3)] + own + [sent(came.after, k) for k in range(3)]

    x_before, x_after = flag(coord[0] > 0), flag(coord[0] < 3)
    row, col = iota((24, 256), 0), iota((24, 256), 1)
    y_ok = jnp.where(row < 16, 1.0, jnp.where(row < 20, flag(coord[1] < 15), flag(coord[1] > 0)))
    z_ok = jnp.where(col < 128, 1.0, jnp.where(col < 192, flag(coord[2] < 3), flag(coord[2] > 0)))
    inside = y_ok * z_ok
    edge = [inside * (x_before if f < 4 else x_after) if not 4 <= f < 8 else inside for f in range(TX)]

    def extended(base, f):
        at = base + f * 24
        return jnp.concatenate([narrow[pl.ds(at, 24), :], tiles[pl.ds(at - N_THETA, 24), :]], axis=1)

    for f in range(TX):
        now[f] = extended(N_THETA, f) * edge[f]
    dose = [injury[i] for i in range(4)]
    state, other = now, later
    for turn in range(4):
        for f in range(1 + turn, TX - 1 - turn):
            mid = state[f]
            beside = state[f - 1] + state[f + 1]
            beside = beside + pltpu.roll(mid, 1, 0) + pltpu.roll(mid, 23, 0)
            beside = beside + pltpu.roll(mid, 1, 1) + pltpu.roll(mid, 255, 1)
            heat = heats[f]
            wash = extended(N_PERF, f - 1)
            new = mid + DIFFUSION * (beside - 6.0 * mid) - wash * mid + HEATING * heat
            other[f] = new * edge[f]
            if 4 <= f < 8:
                own = new[0:16, 0:128]
                dose[f - 4] = dose[f - 4] + jnp.exp(LN_PREFACTOR - ENERGY_BARRIER / (CORE_WARMTH + own))
                if turn == 3:
                    warm_out[f - 4] = own
        state, other = other, state
    for i in range(4):
        dose_out[i] = jnp.log(dose[i])
    store.wait()


def shaped(*shape, dtype=F32):
    return jax.ShapeDtypeStruct(shape, dtype)


def call(kernel, name, in_specs, outs, scratch=(), out_specs=None, cost=2000):
    return pl.pallas_call(
        kernel,
        name=name,
        out_shape=tuple(outs),
        in_specs=in_specs,
        out_specs=tuple(out_specs or [vmem() for _ in outs]),
        scratch_shapes=list(scratch),
        cost_estimate=pl.CostEstimate(flops=cost * 1000, bytes_accessed=cost * 1000, transcendentals=0),
        compiler_params=pltpu.CompilerParams(vmem_limit_bytes=24 * 1024 * 1024),
    )


def on_device(
    acoustic_iterate,
    coarse_update,
    class_codes_volume,
    element_location,
    element_excitation,
    class_wavespeed,
    class_damping,
    washout_fraction,
    thermal_excess,
    injury_integral,
):
    def in_hbm(*arrays):
        return [pltpu.with_memory_space_constraint(array, pltpu.HBM) for array in arrays]

    *sent, perf, it, co, codes, theta = call(
        pack_x, "pack_x", [hbm()] * 5,
        [
            shaped(XB, 256),
            shaped(XB, 256),
            shaped(YB, 256),
            shaped(YB, 256),
            shaped(4, 16, 128),
            shaped(2, 8, 32, 256),
            shaped(2, 4, 16, 128),
            shaped(8, 32, 256, dtype=jnp.int32),
            shaped(4, 16, 128),
        ],
        [pltpu.VMEM((2, 128, 128), F32), pltpu.SMEM((4,), F32), pltpu.SemaphoreType.DMA((5,))],
    )(*in_hbm(washout_fraction, acoustic_iterate, coarse_update, class_codes_volume, thermal_excess))
    own = (it, co, codes, theta, perf)
    y_came = exchange(sent[2:], 1)
    x_came = exchange(sent[:2], 0)

    field, strip, *weights = call(
        sources, "sources", [hbm(), hbm(), vmem()],
        [
            shaped(2, CX, 48, 256),
            shaped(2, CX, 48, 128),
            shaped(128, 256, dtype=BF16),
            shaped(256, 128, dtype=BF16),
            shaped(256, 128, dtype=BF16),
            shaped(128, 256, dtype=BF16),
        ],
        [
            pltpu.SMEM((3, 1024), jnp.int32),
            pltpu.SMEM((2, 1024), F32),
            pltpu.VMEM((3, 1024), jnp.int32),
            pltpu.SemaphoreType.DMA((3,)),
        ],
        cost=8000,
    )(*in_hbm(element_location.T, element_excitation), perf)
    sent = call(pack_corner, "pack_corner", [vmem()] * 3, [shaped(KB, 256)] * 2)(*y_came, weights[0])
    corners = exchange(sent, 0)

    wide, narrow, *sent = call(
        pack_z, "pack_z", [vmem()] * 11,
        [shaped(WIDE, 256), shaped(NARROW, 128), shaped(ZB, 128), shaped(ZB, 128)],
    )(*own, *x_came, *y_came, *corners)
    z_came = exchange(sent, 2)

    def scratch(width):
        return [
            pltpu.VMEM((2 * LX * 48, width), F32),
            pltpu.VMEM((2, FX, 48, width), F32),
            pltpu.VMEM((2, CX, 48, width), F32),
            pltpu.VMEM((CX, 48, width), F32),
            pltpu.VMEM((CX, 48, width), F32),
            pltpu.VMEM((width // 128, 192, 128), F32),
        ]

    inner, power_inner, grown = call(
        smooth_inner, "smooth_inner", [smem()] * 2 + [vmem()] * 5,
        [shaped(2, 8, 32, 256), shaped(96, 128), shaped(2 * LX * 48, 128)],
        scratch(256),
    )(class_wavespeed, class_damping, wide, narrow, field, weights[0], weights[1])
    pressure, power, power_halo, *sent, tiles = call(
        smooth_ends, "smooth_ends", [smem()] * 2 + [vmem()] * 9,
        [
            shaped(2, 8, 32, 256),
            shaped(96, 128),
            shaped(96, 128),
            shaped(96, 128),
            shaped(96, 128),
            shaped(NARROW - N_THETA, 128),
        ],
        [pltpu.VMEM((WIDE + NARROW, 128), F32), pltpu.VMEM((2 * LX * 48, 128), F32)] + scratch(128),
    )(class_wavespeed, class_damping, wide, *z_came, strip, weights[2], weights[3], inner, power_inner, grown)
    x_came = exchange(sent, 0)

    warmth, dose, pressure = call(
        bioheat, "bioheat", [vmem()] * 8,
        [shaped(4, 16, 128), shaped(4, 16, 128), shaped(2, 8, 32, 256)],
        [pltpu.VMEM((TX, 24, 256), F32), pltpu.VMEM((TX, 24, 256), F32), pltpu.SemaphoreType.DMA],
        [vmem(), vmem(), hbm()],
    )(narrow, tiles, power, power_halo, *x_came, injury_integral, pressure)
    return pressure, warmth, dose


def solution(mesh):
    placed = (
        P(None, "gx", "gy", "gz"),
        P(None, "gx", "gy", "gz"),
        P("gx", "gy", "gz"),
        P(),
        P(),
        P(),
        P(),
        P(),
        P("gx", "gy", "gz"),
        P("gx", "gy", "gz"),
    )
    return jax.shard_map(
        on_device,
        mesh=mesh,
        in_specs=placed,
        out_specs=(P(None, "gx", "gy", "gz"), P("gx", "gy", "gz"), P("gx", "gy", "gz")),
        check_vma=False,
    )
```

time: 38.5 us -> 36.1 us (0.938)
  starting transfers between devices: 14.6 us -> 8.8 us
  Pallas kernels: 10.8 us -> 13 us
  waiting for transfers between devices: 11.9 us -> 13 us
    ppermute x10, starting transfers between devices: 14.6 us -> 8.8 us  [exchange(): lax.ppermute(buffer, AXES, swaps(sizes, axis, (axis == 1) != (k == 1)))]
    pallas_call x5 -> x6, Pallas kernels: 9.39 us -> 11.6 us  [the longest x1 3.81 us: on_device(): call(sources, 'sources', [hbm(), hbm(), vmem()], [shaped(2, CX, 48, 256),...]
    ppermute x10, waiting for transfers between devices: 11.9 us -> 13 us  [exchange(): lax.ppermute(buffer, AXES, swaps(sizes, axis, (axis == 1) != (k == 1)))]
  transfers between devices with their start and end apart: 10 -> 10, of which waited for: 8 -> 8; matrix products, arithmetic and copies ran while one was open for 0% -> 0% of each run, Pallas kernels for 7% -> 18%
where the time goes in v4:
time: 36.1 us; the launch traced here: 35.6 us
  Pallas kernels  13 us (36%)
  waiting for transfers between devices  13 us (36%)
  starting transfers between devices  8.8 us (24%)
  between operations  0.74 us (2%)
    ppermute x10, waiting for transfers between devices, exchange(): lax.ppermute(buffer, AXES, swaps(sizes, axis, (axis == 1) != (k == 1)))  13 us
    ppermute x10, starting transfers between devices, exchange(): lax.ppermute(buffer, AXES, swaps(sizes, axis, (axis == 1) != (k == 1)))  8.8 us
    pallas_call x1, Pallas kernels, on_device(): call(sources, 'sources', [hbm(), hbm(), vmem()], [shaped(2, CX, 48, 256),...  3.81 us
    pallas_call x1, Pallas kernels, on_device(): call(smooth_ends, 'smooth_ends', [smem()] * 2 + [vmem()] * 9, [shaped(2,...  2.78 us
    pallas_call x1, Pallas kernels, on_device(): call(smooth_inner, 'smooth_inner', [smem()] * 2 + [vmem()] * 5, [shaped(2...  2.71 us
    pallas_call x1, Pallas kernels, on_device(): call(bioheat, 'bioheat', [vmem()] * 8, [shaped(4, 16, 128), shaped(4, 16,...  1.44 us
    pallas_call x1, Pallas kernels, on_device(): call(pack_x, 'pack_x', [hbm()] * 5, [shaped(XB, 256), shaped(XB, 256), sh...  1.43 us
    pallas_call x1, Pallas kernels, on_device(): call(pack_z, 'pack_z', [vmem()] * 11, [shaped(WIDE, 256), shaped(NARROW,...  0.8 us
  transfers between devices with their start and end apart: 10, of which 8 were waited for; matrix products, arithmetic and copies ran while one was open for 0% of the time, Pallas kernels for 18%

profile of v4, /device:TPU:20, one launch (start us, length us, event | category | flops | bytes accessed | tf_op | source)
XLA Modules:
  0.0 35.6 jit_solution(16215715247427359309)
XLA Ops:
  0.6 0.0 copy-start.2
  0.6 0.0 copy-start.1
  0.7 1.4 %pack_x.1 = (f32[256,256]{1,0:T(8,128)S(1)}, f32[256,256]{1,0:T(8,128)S(1)}, f32[232,256]{1,0:T(8,128)S(1)}, f32[232,256]{1,0:T(8,128)S(1)}, f32[4,16,128]{2,1,0...) custom-call(f32[4]{0:T(128)} %wash_h.1, ...), custom_call_target="tpu_custom_call" | custom-call | flops 2000000 | bytes 2000000 | tf_op jit(solution)/shard_map/pack_x/pallas_call | solution.py:586
  2.1 5.7 %collective-permute-start.2 = (f32[232,256]{1,0:T(8,128)S(1)}, f32[232,256]{1,0:T(8,128)S(1)}, u32[]{:S(2)}, u32[]{:S(2)}) collective-permute-start(f32[232,256]{1,0:T(8,128)S(1)} %get-tuple-element.43), channel_id=1, source_target_pairs={{0,1},{1,0},{2,3},{3,2},{4,8},{5,9},{6,10},{7,11},{8,4},{9,5},{10,... | collective-permute-start | bytes 712712 | tf_op jit(solution)/shard_map/ppermute | solution.py:67
  7.8 0.0 collective-permute-start.3
  7.8 1.2 %collective-permute-start = (f32[256,256]{1,0:T(8,128)S(1)}, f32[256,256]{1,0:T(8,128)S(1)}, u32[]{:S(2)}, u32[]{:S(2)}) collective-permute-start(f32[256,256]{1,0:T(8,128)S(1)} %get-tuple-element.41), channel_id=1, source_target_pairs={{0,64},{1,65},{2,66},{3,67},{4,68},{5,69},{6,70},{7,71},{8,72},{9,... | collective-permute-start | bytes 786440 | tf_op jit(solution)/shard_map/ppermute | solution.py:67
  9.0 0.0 collective-permute-start.1
  9.0 3.8 %sources.1 = (f32[2,10,48,256]{3,2,1,0:T(8,128)S(1)}, f32[2,10,48,128]{3,2,1,0:T(8,128)S(1)}, bf16[128,256]{1,0:T(8,128)(2,1)S(1)}, bf16[256,128]{1,0:T(8,128)(2...) custom-call(s32[3,1024]{1,0:T(4,128)} %bitcast.1, f32[2,1024]{1,0:T(2,128)} %exc_h.1, ...), custom_call_target="tpu_custom_call" | custom-call | flops 8000000 | bytes 8000000 | tf_op jit(solution)/shard_map/sources/pallas_call | solution.py:605
  12.8 0.8 %collective-permute-done.2.y_one = f32[232,256]{1,0:T(8,128)S(1)} collective-permute-done((f32[232,256]{1,0:T(8,128)S(1)}, f32[232,256]{1,0:T(8,128)S(1)}, u32[]{:S(2)}, u32[]{:S(2)}) %collective-permute-start.2) | collective-permute-done | bytes 237600 | tf_op jit(solution)/shard_map/ppermute | solution.py:67
  13.6 1.5 %collective-permute-done.3.y_two = f32[232,256]{1,0:T(8,128)S(1)} collective-permute-done((f32[232,256]{1,0:T(8,128)S(1)}, f32[232,256]{1,0:T(8,128)S(1)}, u32[]{:S(2)}, u32[]{:S(2)}) %collective-permute-start.3) | collective-permute-done | bytes 237600 | tf_op jit(solution)/shard_map/ppermute | solution.py:67
  15.1 1.3 %collective-permute-start.4 = (f32[128,256]{1,0:T(8,128)S(1)}, f32[128,256]{1,0:T(8,128)S(1)}, u32[]{:S(2)}, u32[]{:S(2)}) collective-permute-start(f32[128,256]{1,0:T(8,128)S(1)} %get-tuple-element.46), channel_id=1, source_target_pairs={{0,64},{1,65},{2,66},{3,67},{4,68},{5,69},{6,70},{7,71},{8,72},{9,... | collective-permute-start | bytes 393224 | tf_op jit(solution)/shard_map/ppermute | solution.py:67
  16.4 0.0 collective-permute-start.5
  16.4 0.0 collective-permute-done.x_one
  16.4 0.1 collective-permute-done.1.x_two
  16.5 3.7 %collective-permute-done.4.k_one = f32[128,256]{1,0:T(8,128)S(1)} collective-permute-done((f32[128,256]{1,0:T(8,128)S(1)}, f32[128,256]{1,0:T(8,128)S(1)}, u32[]{:S(2)}, u32[]{:S(2)}) %collective-permute-start.4) | collective-permute-done | bytes 131104 | tf_op jit(solution)/shard_map/ppermute | solution.py:67
  20.1 1.2 %collective-permute-done.5.k_two = f32[128,256]{1,0:T(8,128)S(1)} collective-permute-done((f32[128,256]{1,0:T(8,128)S(1)}, f32[128,256]{1,0:T(8,128)S(1)}, u32[]{:S(2)}, u32[]{:S(2)}) %collective-permute-start.5) | collective-permute-done | bytes 131104 | tf_op jit(solution)/shard_map/ppermute | solution.py:67
  21.3 0.8 %pack_z.1 = (f32[1632,256]{1,0:T(8,128)S(1)}, f32[1056,128]{1,0:T(8,128)S(1)}, f32[168,128]{1,0:T(8,128)S(1)}, f32[168,128]{1,0:T(8,128)S(1)}) custom-call(f32[2,8,32,256]{3,2,1,0:T(8,128)S(1)} %get-tuple-element.36.it, f32[2,4,16,128]{3,2,1,0:T(8,128)S(1)} %get-tuple-element.37.co, s32[8,32,256]{2,1,0:T(8,128)S(1)} %get-tuple-element.38.codes, ...), custom_call_target="tpu_custom_call" | custom-call | flops 2000000 | bytes 2000000 | tf_op jit(solution)/shard_map/pack_z/pallas_call | solution.py:626
  22.1 0.1 collective-permute-start.6
  22.2 0.1 collective-permute-start.7
  22.4 0.0 copy-done.2
  22.4 0.0 copy-done.1
  22.4 2.7 %smooth_inner.1 = (f32[2,8,32,256]{3,2,1,0:T(8,128)S(1)}, f32[96,128]{1,0:T(8,128)S(1)}, f32[768,128]{1,0:T(8,128)S(1)}) custom-call(f32[4]{0:T(128)S(1)} %copy-done.1, f32[4]{0:T(128)S(1)} %copy-done.2, f32[1632,256]{1,0:T(8,128)S(1)} %get-tuple-element.49.wide, f32[1056,128]{1,0:T(8,128)S(1)} %get-tuple-element.48.narrow, ...), custom_call_target="tpu_custom_call" | custom-call | flops 2000000 | bytes 2000000 | tf_op jit(solution)/shard_map/smooth_inner/pallas_call | solution.py:642
  25.1 0.0 collective-permute-done.6.z_one
  25.1 1.7 %collective-permute-done.7.z_two = f32[168,128]{1,0:T(8,128)S(1)} collective-permute-done((f32[168,128]{1,0:T(8,128)S(1)}, f32[168,128]{1,0:T(8,128)S(1)}, u32[]{:S(2)}, u32[]{:S(2)}) %collective-permute-start.7) | collective-permute-done | bytes 86048 | tf_op jit(solution)/shard_map/ppermute | solution.py:67
  26.8 0.0 copy-start
  26.8 2.8 %smooth_ends.1 = (f32[2,8,32,256]{3,2,1,0:T(8,128)S(1)}, f32[96,128]{1,0:T(8,128)S(1)}, f32[96,128]{1,0:T(8,128)S(1)}, f32[96,128]{1,0:T(8,128)S(1)}, f32[96,128]{1,0:T(8,128)S(1)}, /*index=5*/f32[544,128]{1,0:T(8,128)S(1)}) custom-call(f32[4]{0:T(128)S(1)} %copy-done.1, f32[4]{0:T(128)S(1)} %copy-done.2, f32[1632,256]{1,0:T(8,128)S(1)} %get-tuple-element.49.wide, ...), custom_call_target="tpu_custom_call" | custom-call | flops 2000000 | bytes 2000000 | tf_op jit(solution)/shard_map/smooth_ends/pallas_call | solution.py:647
  29.6 0.4 %collective-permute-start.8 = (f32[96,128]{1,0:T(8,128)S(1)}, f32[96,128]{1,0:T(8,128)S(1)}, u32[]{:S(2)}, u32[]{:S(2)}) collective-permute-start(f32[96,128]{1,0:T(8,128)S(1)} %get-tuple-element.63), channel_id=1, source_target_pairs={{0,64},{1,65},{2,66},{3,67},{4,68},{5,69},{6,70},{7,71},{8,72},{9,... | collective-permute-start | bytes 147464 | tf_op jit(solution)/shard_map/ppermute | solution.py:67
  30.0 0.0 collective-permute-start.9
  30.0 3.9 %collective-permute-done.8.x_one = f32[96,128]{1,0:T(8,128)S(1)} collective-permute-done((f32[96,128]{1,0:T(8,128)S(1)}, f32[96,128]{1,0:T(8,128)S(1)}, u32[]{:S(2)}, u32[]{:S(2)}) %collective-permute-start.8) | collective-permute-done | bytes 49184 | tf_op jit(solution)/shard_map/ppermute | solution.py:67
  33.9 0.2 collective-permute-done.9.x_two
  34.1 0.0 copy-done
  34.1 1.4 %bioheat.1 = (f32[4,16,128]{2,1,0:T(8,128)}, f32[4,16,128]{2,1,0:T(8,128)}, f32[2,8,32,256]{3,2,1,0:T(8,128)}) custom-call(f32[1056,128]{1,0:T(8,128)S(1)} %get-tuple-element.48.narrow, f32[544,128]{1,0:T(8,128)S(1)} %get-tuple-element.60.tiles, f32[96,128]{1,0:T(8,128)S(1)} %get-tuple-element.61.power, f32[96,128]{1,0:T(8,128)S(1)} %get-tuple-element.62.power_halo, ...), custom_call_target="tpu_custom_call" | custom-call | flops 2000000 | bytes 2000000 | tf_op jit(solution)/shard_map/bioheat/pallas_call | solution.py:661
  (1 shorter events, 0.0 us)
Async XLA Ops:
  0.6 21.7 %copy-start.2 = (f32[4]{0:T(128)S(1)}, f32[4]{0:T(128)}, u32[]{:S(2)}) copy-start(f32[4]{0:T(128)} %damp_t.3) | copy-start | bytes 52
  0.6 21.7 %copy-start.1 = (f32[4]{0:T(128)S(1)}, f32[4]{0:T(128)}, u32[]{:S(2)}) copy-start(f32[4]{0:T(128)} %wave_t.3) | copy-start | bytes 52
  2.1 11.5 %collective-permute-start.2 = (f32[232,256]{1,0:T(8,128)S(1)}, f32[232,256]{1,0:T(8,128)S(1)}, u32[]{:S(2)}, u32[]{:S(2)}) collective-permute-start(f32[232,256]{1,0:T(8,128)S(1)} %get-tuple-element.43), channel_id=1, source_target_pairs={{0,1},{1,0},{2,3},{3,2},{4,8},{5,9},{6,10},{7,11},{8,4},{9,5},{10,... | collective-permute-start | bytes 712712 | tf_op jit(solution)/shard_map/ppermute | solution.py:67
  7.8 7.2 %collective-permute-start.3 = (f32[232,256]{1,0:T(8,128)S(1)}, f32[232,256]{1,0:T(8,128)S(1)}, u32[]{:S(2)}, u32[]{:S(2)}) collective-permute-start(f32[232,256]{1,0:T(8,128)S(1)} %get-tuple-element.44), channel_id=1, source_target_pairs={{0,4},{1,5},{2,6},{3,7},{4,0},{5,1},{6,2},{7,3},{8,12},{9,13},{10,... | collective-permute-start | bytes 712712 | tf_op jit(solution)/shard_map/ppermute | solution.py:67
  7.8 8.6 %collective-permute-start = (f32[256,256]{1,0:T(8,128)S(1)}, f32[256,256]{1,0:T(8,128)S(1)}, u32[]{:S(2)}, u32[]{:S(2)}) collective-permute-start(f32[256,256]{1,0:T(8,128)S(1)} %get-tuple-element.41), channel_id=1, source_target_pairs={{0,64},{1,65},{2,66},{3,67},{4,68},{5,69},{6,70},{7,71},{8,72},{9,... | collective-permute-start | bytes 786440 | tf_op jit(solution)/shard_map/ppermute | solution.py:67
  9.0 7.5 %collective-permute-start.1 = (f32[256,256]{1,0:T(8,128)S(1)}, f32[256,256]{1,0:T(8,128)S(1)}, u32[]{:S(2)}, u32[]{:S(2)}) collective-permute-start(f32[256,256]{1,0:T(8,128)S(1)} %get-tuple-element.42), channel_id=1, source_target_pairs={{0,1},{1,0},{2,3},{3,2},{4,5},{5,4},{6,7},{7,6},{8,9},{9,8},{10,11... | collective-permute-start | bytes 786440 | tf_op jit(solution)/shard_map/ppermute | solution.py:67
  15.1 5.1 %collective-permute-start.4 = (f32[128,256]{1,0:T(8,128)S(1)}, f32[128,256]{1,0:T(8,128)S(1)}, u32[]{:S(2)}, u32[]{:S(2)}) collective-permute-start(f32[128,256]{1,0:T(8,128)S(1)} %get-tuple-element.46), channel_id=1, source_target_pairs={{0,64},{1,65},{2,66},{3,67},{4,68},{5,69},{6,70},{7,71},{8,72},{9,... | collective-permute-start | bytes 393224 | tf_op jit(solution)/shard_map/ppermute | solution.py:67
  16.4 5.0 %collective-permute-start.5 = (f32[128,256]{1,0:T(8,128)S(1)}, f32[128,256]{1,0:T(8,128)S(1)}, u32[]{:S(2)}, u32[]{:S(2)}) collective-permute-start(f32[128,256]{1,0:T(8,128)S(1)} %get-tuple-element.47), channel_id=1, source_target_pairs={{0,1},{1,0},{2,3},{3,2},{4,5},{5,4},{6,7},{7,6},{8,9},{9,8},{10,11... | collective-permute-start | bytes 393224 | tf_op jit(solution)/shard_map/ppermute | solution.py:67
  22.1 2.9 %collective-permute-start.6 = (f32[168,128]{1,0:T(8,128)S(1)}, f32[168,128]{1,0:T(8,128)S(1)}, u32[]{:S(2)}, u32[]{:S(2)}) collective-permute-start(f32[168,128]{1,0:T(8,128)S(1)} %get-tuple-element.50), channel_id=1, source_target_pairs={{0,1},{1,0},{2,3},{3,2},{4,5},{5,4},{6,7},{7,6},{8,9},{9,8},{10,11... | collective-permute-start | bytes 258056 | tf_op jit(solution)/shard_map/ppermute | solution.py:67
  22.2 4.6 %collective-permute-start.7 = (f32[168,128]{1,0:T(8,128)S(1)}, f32[168,128]{1,0:T(8,128)S(1)}, u32[]{:S(2)}, u32[]{:S(2)}) collective-permute-start(f32[168,128]{1,0:T(8,128)S(1)} %get-tuple-element.51), channel_id=1, source_target_pairs={{0,64},{1,2},{2,1},{3,67},{4,68},{5,6},{6,5},{7,71},{8,72},{9,10},... | collective-permute-start | bytes 258056 | tf_op jit(solution)/shard_map/ppermute | solution.py:67
  26.8 7.3 %copy-start = (f32[4,16,128]{2,1,0:T(8,128)S(1)}, f32[4,16,128]{2,1,0:T(8,128)}, u32[]{:S(2)}) copy-start(f32[4,16,128]{2,1,0:T(8,128)} %injury.1) | copy-start | bytes 98308
  29.6 4.3 %collective-permute-start.8 = (f32[96,128]{1,0:T(8,128)S(1)}, f32[96,128]{1,0:T(8,128)S(1)}, u32[]{:S(2)}, u32[]{:S(2)}) collective-permute-start(f32[96,128]{1,0:T(8,128)S(1)} %get-tuple-element.63), channel_id=1, source_target_pairs={{0,64},{1,65},{2,66},{3,67},{4,68},{5,69},{6,70},{7,71},{8,72},{9,... | collective-permute-start | bytes 147464 | tf_op jit(solution)/shard_map/ppermute | solution.py:67
  30.0 4.1 %collective-permute-start.9 = (f32[96,128]{1,0:T(8,128)S(1)}, f32[96,128]{1,0:T(8,128)S(1)}, u32[]{:S(2)}, u32[]{:S(2)}) collective-permute-start(f32[96,128]{1,0:T(8,128)S(1)} %get-tuple-element.64), channel_id=1, source_target_pairs={{0,1},{1,0},{2,3},{3,2},{4,5},{5,4},{6,7},{7,6},{8,9},{9,8},{10,11... | collective-permute-start | bytes 147464 | tf_op jit(solution)/shard_map/ppermute | solution.py:67

commit v5 on v4

--- a/solution.py
+++ b/solution.py
@@ -64,11 +64,11 @@
 
 def exchange(pair, axis):
     sizes = [lax.axis_size(name) for name in AXES]
-    return [lax.ppermute(buffer, AXES, swaps(sizes, axis, (axis == 1) != (k == 1))) for k, buffer in enumerate(pair)]
+    return [lax.ppermute(buffer, AXES, swaps(sizes, axis, bool(k))) for k, buffer in enumerate(pair)]
 
 
 def is_even(axis):
-    return lax.axis_index(AXES[axis]) % 2 == (1 if axis == 1 else 0)
+    return lax.axis_index(AXES[axis]) % 2 == 0
 
 
 class Sender:
@@ -429,10 +429,15 @@
     return tiles[0] if len(tiles) == 1 else jnp.concatenate(tiles, axis=1)
 
 
-def smooth_inner(wave_t, damp_t, wide, narrow, source, spread, gather, out, power, grown,
-                 fine, first, second, gain_r, gain_i, pool):
+def smooth_inner(wave_t, damp_t, wide, narrow, source, spread, gather, spread_strip, out, power, ends, fine_ends,
+                 grown, fine, first, second, gain_r, gain_i, pool):
     coarse_rows(lambda at: narrow[pl.ds(N_COARSE + at, 32), :], None, grown)
     fine[...] = exact_dot(grown[...], spread[...])
+    fine_ends[...] = exact_dot(grown[...], spread_strip[pl.ds(0, 128), :])
+    lane = iota((48, 128), 1)
+    for at in range(0, WIDE, 48):
+        turned = pltpu.roll(wide[pl.ds(at, 48), pl.ds(128, 128)], 64, 1)
+        ends[pl.ds(at, 48), :] = jnp.where(lane < 32, wide[pl.ds(at, 48), pl.ds(0, 128)], turned)
 
     def own(at):
         return wide[pl.ds(at, 48), :]
@@ -445,7 +450,7 @@
     power[...] = exact_dot(sums, gather[...]) * 0.125
 
 
-def smooth_ends(wave_t, damp_t, wide, z_one, z_two, source, spread, gather, inner, power_inner, grown,
+def smooth_ends(wave_t, damp_t, ends, z_one, z_two, source, spread, gather, inner, power_inner, fine_ends,
                 out, power, power_halo, one, two, tiles,
                 halo, grown_halo, fine, first, second, gain_r, gain_i, pool):
     lane = iota((ZB, 128), 1)
@@ -464,13 +469,12 @@
     after_ok, before_ok = flag(at_z < 3), flag(at_z > 0)
     z_ok = jnp.where(iota((32, 128), 1) < 96, after_ok, before_ok)
     coarse_rows(lambda at: halo[pl.ds(WIDE + N_COARSE + at, 32), :], z_ok, grown_halo)
-    fine[...] = exact_dot(jnp.concatenate([grown[...], grown_halo[...]], axis=1), spread[...])
+    fine[...] = fine_ends[...] + exact_dot(grown_halo[...], spread[pl.ds(128, 128), :])
 
     lane = iota((48, 128), 1)
 
     def strip(at):
-        ends = jnp.where(lane < 32, wide[pl.ds(at, 48), pl.ds(0, 128)], pltpu.roll(wide[pl.ds(at, 48), pl.ds(128, 128)], 64, 1))
-        return jnp.where(lane < 64, ends, halo[pl.ds(at, 48), :])
+        return jnp.where(lane < 64, ends[pl.ds(at, 48), :], halo[pl.ds(at, 48), :])
 
     low, high = iota((32, 128), 1) < 8, iota((32, 128), 1) >= 120
 
@@ -501,10 +505,64 @@
     to.put(pl.ds(72, 24), every, packed(1), packed(0))
 
 
-def bioheat(narrow, tiles, power, power_halo, x_one, x_two, injury, wave, warm_out, dose_out, wave_out, now, later, sem):
+class Bioheat:
+    def __init__(self):
+        x_before, x_after = x_flags()
+        at_y, at_z = lax.axis_index("gy"), lax.axis_index("gz")
+        row, col = iota((24, 256), 0), iota((24, 256), 1)
+        y_ok = jnp.where(row < 16, 1.0, jnp.where(row < 20, flag(at_y < 15), flag(at_y > 0)))
+        z_ok = jnp.where(col < 128, 1.0, jnp.where(col < 192, flag(at_z < 3), flag(at_z > 0)))
+        inside = y_ok * z_ok
+        self.edge = [inside * (x_before if f < 4 else x_after) if not 4 <= f < 8 else inside for f in range(TX)]
+
+    def step(self, state, wash, f):
+        mid = state[f]
+        beside = state[f - 1] + state[f + 1]
+        beside = beside + pltpu.roll(mid, 1, 0) + pltpu.roll(mid, 23, 0)
+        beside = beside + pltpu.roll(mid, 1, 1) + pltpu.roll(mid, 255, 1)
+        return mid + DIFFUSION * (beside - 6.0 * mid) - wash[f - 1] * mid
+
+    def finish(self, cooled, heat, f):
+        return (cooled + HEATING * heat) * self.edge[f]
+
+
+def injury_of(warm):
+    own = warm[0:16, 0:128]
+    return jnp.exp(LN_PREFACTOR - ENERGY_BARRIER / (CORE_WARMTH + own))
+
+
+def own_heat(power, power_halo, f):
+    return jnp.concatenate([ref[pl.ds(24 * (f - 4), 24), :] for ref in (power, power_halo)], axis=1)
+
+
+def bioheat_inner(narrow, tiles, power, power_halo, injury, wave, begun, later, wash, dose, wave_out, now, sem):
     store = pltpu.make_async_copy(wave, wave_out, sem)
     store.start()
-    coord = [lax.axis_index(name) for name in AXES]
+    heat = Bioheat()
+
+    def extended(base, f):
+        at = base + f * 24
+        return jnp.concatenate([narrow[pl.ds(at, 24), :], tiles[pl.ds(at - N_THETA, 24), :]], axis=1)
+
+    for f in range(TX):
+        now[f] = extended(N_THETA, f) * heat.edge[f]
+    for f in range(QX):
+        wash[f] = extended(N_PERF, f)
+    for f in range(1, TX - 1):
+        new = heat.step(now, wash, f)
+        if 4 <= f < 8:
+            new = heat.finish(new, own_heat(power, power_halo, f), f)
+            dose[f - 4] = injury[f - 4] + injury_of(new)
+        begun[f] = new
+    for f in (5, 6):
+        new = heat.finish(heat.step(begun, wash, f), own_heat(power, power_halo, f), f)
+        later[f - 5] = new
+        dose[f - 4] = dose[f - 4] + injury_of(new)
+    store.wait()
+
+
+def bioheat(begun, later, wash, dose_in, power, power_halo, x_one, x_two, warm_out, dose_out, one, two):
+    heat = Bioheat()
     came = Receiver(x_one, x_two, 0)
 
     def sent(side, k):
@@ -512,43 +570,26 @@
         beyond = jnp.where(iota((24, 128), 1) // 16 == k, beyond, 0.0)
         return jnp.concatenate([side(pl.ds(24 * k, 24), pl.ds(0, 128)), pltpu.roll(beyond, 120 - 16 * k, 1)], axis=1)
 
-    own = [jnp.concatenate([ref[pl.ds(24 * i, 24), :] for ref in (power, power_halo)], axis=1) for i in range(4)]
+    own = [own_heat(power, power_halo, f) for f in range(4, 8)]
     heats = [None] + [sent(came.before, k) for k in range(3)] + own + [sent(came.after, k) for k in range(3)]
-
-    x_before, x_after = flag(coord[0] > 0), flag(coord[0] < 3)
-    row, col = iota((24, 256), 0), iota((24, 256), 1)
-    y_ok = jnp.where(row < 16, 1.0, jnp.where(row < 20, flag(coord[1] < 15), flag(coord[1] > 0)))
-    z_ok = jnp.where(col < 128, 1.0, jnp.where(col < 192, flag(coord[2] < 3), flag(coord[2] > 0)))
-    inside = y_ok * z_ok
-    edge = [inside * (x_before if f < 4 else x_after) if not 4 <= f < 8 else inside for f in range(TX)]
-
-    def extended(base, f):
-        at = base + f * 24
-        return jnp.concatenate([narrow[pl.ds(at, 24), :], tiles[pl.ds(at - N_THETA, 24), :]], axis=1)
-
-    for f in range(TX):
-        now[f] = extended(N_THETA, f) * edge[f]
-    dose = [injury[i] for i in range(4)]
-    state, other = now, later
-    for turn in range(4):
+    for f in range(1, TX - 1):
+        one[f] = begun[f] if 4 <= f < 8 else heat.finish(begun[f], heats[f], f)
+    dose = [dose_in[i] for i in range(4)]
+    state, other = one, two
+    for turn in range(1, 4):
         for f in range(1 + turn, TX - 1 - turn):
-            mid = state[f]
-            beside = state[f - 1] + state[f + 1]
-            beside = beside + pltpu.roll(mid, 1, 0) + pltpu.roll(mid, 23, 0)
-            beside = beside + pltpu.roll(mid, 1, 1) + pltpu.roll(mid, 255, 1)
-            heat = heats[f]
-            wash = extended(N_PERF, f - 1)
-            new = mid + DIFFUSION * (beside - 6.0 * mid) - wash * mid + HEATING * heat
-            other[f] = new * edge[f]
+            if turn == 1 and f in (5, 6):
+                other[f] = later[f - 5]
+                continue
+            new = heat.finish(heat.step(state, wash, f), heats[f], f)
+            other[f] = new
             if 4 <= f < 8:
-                own = new[0:16, 0:128]
-                dose[f - 4] = dose[f - 4] + jnp.exp(LN_PREFACTOR - ENERGY_BARRIER / (CORE_WARMTH + own))
+                dose[f - 4] = dose[f - 4] + injury_of(new)
                 if turn == 3:
-                    warm_out[f - 4] = own
+                    warm_out[f - 4] = new[0:16, 0:128]
         state, other = other, state
     for i in range(4):
         dose_out[i] = jnp.log(dose[i])
-    store.wait()
 
 
 def shaped(*shape, dtype=F32):
@@ -639,11 +680,11 @@
             pltpu.VMEM((width // 128, 192, 128), F32),
         ]
 
-    inner, power_inner, grown = call(
-        smooth_inner, "smooth_inner", [smem()] * 2 + [vmem()] * 5,
-        [shaped(2, 8, 32, 256), shaped(96, 128), shaped(2 * LX * 48, 128)],
-        scratch(256),
-    )(class_wavespeed, class_damping, wide, narrow, field, weights[0], weights[1])
+    inner, power_inner, ends, fine_ends = call(
+        smooth_inner, "smooth_inner", [smem()] * 2 + [vmem()] * 6,
+        [shaped(2, 8, 32, 256), shaped(96, 128), shaped(WIDE, 128), shaped(2 * LX * 48, 128)],
+        [pltpu.VMEM((2 * LX * 48, 128), F32)] + scratch(256),
+    )(class_wavespeed, class_damping, wide, narrow, field, weights[0], weights[1], weights[2])
     pressure, power, power_halo, *sent, tiles = call(
         smooth_ends, "smooth_ends", [smem()] * 2 + [vmem()] * 9,
         [
@@ -655,15 +696,21 @@
             shaped(NARROW - N_THETA, 128),
         ],
         [pltpu.VMEM((WIDE + NARROW, 128), F32), pltpu.VMEM((2 * LX * 48, 128), F32)] + scratch(128),
-    )(class_wavespeed, class_damping, wide, *z_came, strip, weights[2], weights[3], inner, power_inner, grown)
+    )(class_wavespeed, class_damping, ends, *z_came, strip, weights[2], weights[3], inner, power_inner, fine_ends)
     x_came = exchange(sent, 0)
 
-    warmth, dose, pressure = call(
+    block = shaped(TX, 24, 256)
+    begun, later, wash, dose, pressure = call(
+        bioheat_inner, "bioheat_inner", [vmem()] * 6,
+        [block, shaped(2, 24, 256), shaped(QX, 24, 256), shaped(4, 16, 128), shaped(2, 8, 32, 256)],
+        [pltpu.VMEM((TX, 24, 256), F32), pltpu.SemaphoreType.DMA],
+        [vmem()] * 4 + [hbm()],
+    )(narrow, tiles, power, power_halo, injury_integral, pressure)
+    warmth, dose = call(
         bioheat, "bioheat", [vmem()] * 8,
-        [shaped(4, 16, 128), shaped(4, 16, 128), shaped(2, 8, 32, 256)],
-        [pltpu.VMEM((TX, 24, 256), F32), pltpu.VMEM((TX, 24, 256), F32), pltpu.SemaphoreType.DMA],
-        [vmem(), vmem(), hbm()],
-    )(narrow, tiles, power, power_halo, *x_came, injury_integral, pressure)
+        [shaped(4, 16, 128), shaped(4, 16, 128)],
+        [pltpu.VMEM((TX, 24, 256), F32), pltpu.VMEM((TX, 24, 256), F32)],
+    )(begun, later, wash, dose, power, power_halo, *x_came)
     return pressure, warmth, dose
 
 

time: 36.1 us -> 35.1 us (0.972)
  waiting for transfers between devices: 13 us -> 11.1 us
  starting transfers between devices: 8.8 us -> 9.98 us
    ppermute x10, waiting for transfers between devices: 13 us -> 11.1 us  [exchange(): lax.ppermute(buffer, AXES, swaps(sizes, axis, bool(k)))]
    ppermute x10, starting transfers between devices: 8.8 us -> 9.98 us  [exchange(): lax.ppermute(buffer, AXES, swaps(sizes, axis, bool(k)))]
    pallas_call x1 -> x2, Pallas kernels: 2.71 us -> 3.73 us  [the longest x1 2.91 us: on_device(): call(smooth_inner, 'smooth_inner', [smem()] * 2 + [vmem()] * 6, [shaped(2...]
    pallas_call x1, Pallas kernels: 1.44 us -> 0.97 us  [on_device(): call(bioheat, 'bioheat', [vmem()] * 8, [shaped(4, 16, 128), shaped(4, 16,...]
  transfers between devices with their start and end apart: 10 -> 10, of which waited for: 8 -> 7; matrix products, arithmetic and copies ran while one was open for 0% -> 0% of each run, Pallas kernels for 18% -> 21%
where the time goes in v5:
time: 35.1 us; the launch traced here: 34.8 us
  Pallas kernels  13 us (37%)
  waiting for transfers between devices  11.1 us (32%)
  starting transfers between devices  9.98 us (28%)
  between operations  0.76 us (2%)
    ppermute x10, waiting for transfers between devices, exchange(): lax.ppermute(buffer, AXES, swaps(sizes, axis, bool(k)))  11.1 us
    ppermute x10, starting transfers between devices, exchange(): lax.ppermute(buffer, AXES, swaps(sizes, axis, bool(k)))  9.98 us
    pallas_call x1, Pallas kernels, on_device(): call(sources, 'sources', [hbm(), hbm(), vmem()], [shaped(2, CX, 48, 256),...  3.6 us
    pallas_call x1, Pallas kernels, on_device(): call(smooth_inner, 'smooth_inner', [smem()] * 2 + [vmem()] * 6, [shaped(2...  2.91 us
    pallas_call x1, Pallas kernels, on_device(): call(smooth_ends, 'smooth_ends', [smem()] * 2 + [vmem()] * 9, [shaped(2,...  2.44 us
    pallas_call x1, Pallas kernels, on_device(): call(pack_x, 'pack_x', [hbm()] * 5, [shaped(XB, 256), shaped(XB, 256), sh...  1.43 us
    pallas_call x1, Pallas kernels, on_device(): call(bioheat, 'bioheat', [vmem()] * 8, [shaped(4, 16, 128), shaped(4, 16,...  0.97 us
    pallas_call x1, Pallas kernels, on_device(): call(bioheat_inner, 'bioheat_inner', [vmem()] * 6, [block, shaped(2, 24,...  0.82 us
  transfers between devices with their start and end apart: 10, of which 7 were waited for; matrix products, arithmetic and copies ran while one was open for 0% of the time, Pallas kernels for 21%

profile of v5, /device:TPU:20, one launch (start us, length us, event | category | flops | bytes accessed | tf_op | source)
XLA Modules:
  0.0 34.8 jit_solution(6167070846980914050)
XLA Ops:
  0.6 0.0 copy-start.2
  0.6 0.0 copy-start.1
  0.7 1.4 %pack_x.1 = (f32[256,256]{1,0:T(8,128)S(1)}, f32[256,256]{1,0:T(8,128)S(1)}, f32[232,256]{1,0:T(8,128)S(1)}, f32[232,256]{1,0:T(8,128)S(1)}, f32[4,16,128]{2,1,0...) custom-call(f32[4]{0:T(128)} %wash_h.1, ...), custom_call_target="tpu_custom_call" | custom-call | flops 2000000 | bytes 2000000 | tf_op jit(solution)/shard_map/pack_x/pallas_call | solution.py:627
  2.1 2.0 %collective-permute-start.2 = (f32[232,256]{1,0:T(8,128)S(1)}, f32[232,256]{1,0:T(8,128)S(1)}, u32[]{:S(2)}, u32[]{:S(2)}) collective-permute-start(f32[232,256]{1,0:T(8,128)S(1)} %get-tuple-element.48), channel_id=1, source_target_pairs={{0,4},{1,5},{2,6},{3,7},{4,0},{5,1},{6,2},{7,3},{8,12},{9,13},{10,... | collective-permute-start | bytes 712712 | tf_op jit(solution)/shard_map/ppermute | solution.py:67
  4.1 4.7 %collective-permute-start.3 = (f32[232,256]{1,0:T(8,128)S(1)}, f32[232,256]{1,0:T(8,128)S(1)}, u32[]{:S(2)}, u32[]{:S(2)}) collective-permute-start(f32[232,256]{1,0:T(8,128)S(1)} %get-tuple-element.49), channel_id=1, source_target_pairs={{0,1},{1,0},{2,3},{3,2},{4,8},{5,9},{6,10},{7,11},{8,4},{9,5},{10,... | collective-permute-start | bytes 712712 | tf_op jit(solution)/shard_map/ppermute | solution.py:67
  8.8 1.2 %collective-permute-start = (f32[256,256]{1,0:T(8,128)S(1)}, f32[256,256]{1,0:T(8,128)S(1)}, u32[]{:S(2)}, u32[]{:S(2)}) collective-permute-start(f32[256,256]{1,0:T(8,128)S(1)} %get-tuple-element.46), channel_id=1, source_target_pairs={{0,64},{1,65},{2,66},{3,67},{4,68},{5,69},{6,70},{7,71},{8,72},{9,... | collective-permute-start | bytes 786440 | tf_op jit(solution)/shard_map/ppermute | solution.py:67
  10.0 0.0 collective-permute-start.1
  10.0 3.6 %sources.1 = (f32[2,10,48,256]{3,2,1,0:T(8,128)S(1)}, f32[2,10,48,128]{3,2,1,0:T(8,128)S(1)}, bf16[128,256]{1,0:T(8,128)(2,1)S(1)}, bf16[256,128]{1,0:T(8,128)(2...) custom-call(s32[3,1024]{1,0:T(4,128)} %bitcast.1, f32[2,1024]{1,0:T(2,128)} %exc_h.1, ...), custom_call_target="tpu_custom_call" | custom-call | flops 8000000 | bytes 8000000 | tf_op jit(solution)/shard_map/sources/pallas_call | solution.py:646
  13.6 0.0 collective-permute-done.2.y_one
  13.6 1.3 %collective-permute-done.3.y_two = f32[232,256]{1,0:T(8,128)S(1)} collective-permute-done((f32[232,256]{1,0:T(8,128)S(1)}, f32[232,256]{1,0:T(8,128)S(1)}, u32[]{:S(2)}, u32[]{:S(2)}) %collective-permute-start.3) | collective-permute-done | bytes 237600 | tf_op jit(solution)/shard_map/ppermute | solution.py:67
  15.0 1.3 %collective-permute-start.4 = (f32[128,256]{1,0:T(8,128)S(1)}, f32[128,256]{1,0:T(8,128)S(1)}, u32[]{:S(2)}, u32[]{:S(2)}) collective-permute-start(f32[128,256]{1,0:T(8,128)S(1)} %get-tuple-element.51), channel_id=1, source_target_pairs={{0,64},{1,65},{2,66},{3,67},{4,68},{5,69},{6,70},{7,71},{8,72},{9,... | collective-permute-start | bytes 393224 | tf_op jit(solution)/shard_map/ppermute | solution.py:67
  16.3 0.0 collective-permute-start.5
  16.3 0.0 collective-permute-done.x_one
  16.3 0.9 %collective-permute-done.1.x_two = f32[256,256]{1,0:T(8,128)S(1)} collective-permute-done((f32[256,256]{1,0:T(8,128)S(1)}, f32[256,256]{1,0:T(8,128)S(1)}, u32[]{:S(2)}, u32[]{:S(2)}) %collective-permute-start.1) | collective-permute-done | bytes 262176 | tf_op jit(solution)/shard_map/ppermute | solution.py:67
  17.2 2.8 %collective-permute-done.4.k_one = f32[128,256]{1,0:T(8,128)S(1)} collective-permute-done((f32[128,256]{1,0:T(8,128)S(1)}, f32[128,256]{1,0:T(8,128)S(1)}, u32[]{:S(2)}, u32[]{:S(2)}) %collective-permute-start.4) | collective-permute-done | bytes 131104 | tf_op jit(solution)/shard_map/ppermute | solution.py:67
  20.1 1.2 %collective-permute-done.5.k_two = f32[128,256]{1,0:T(8,128)S(1)} collective-permute-done((f32[128,256]{1,0:T(8,128)S(1)}, f32[128,256]{1,0:T(8,128)S(1)}, u32[]{:S(2)}, u32[]{:S(2)}) %collective-permute-start.5) | collective-permute-done | bytes 131104 | tf_op jit(solution)/shard_map/ppermute | solution.py:67
  21.2 0.8 %pack_z.1 = (f32[1632,256]{1,0:T(8,128)S(1)}, f32[1056,128]{1,0:T(8,128)S(1)}, f32[168,128]{1,0:T(8,128)S(1)}, f32[168,128]{1,0:T(8,128)S(1)}) custom-call(f32[2,8,32,256]{3,2,1,0:T(8,128)S(1)} %get-tuple-element.41.it, f32[2,4,16,128]{3,2,1,0:T(8,128)S(1)} %get-tuple-element.42.co, s32[8,32,256]{2,1,0:T(8,128)S(1)} %get-tuple-element.43.codes, ...), custom_call_target="tpu_custom_call" | custom-call | flops 2000000 | bytes 2000000 | tf_op jit(solution)/shard_map/pack_z/pallas_call | solution.py:667
  22.0 0.1 collective-permute-start.6
  22.1 0.1 collective-permute-start.7
  22.2 0.0 copy-done.2
  22.3 0.0 copy-done.1
  22.3 2.9 %smooth_inner.1 = (f32[2,8,32,256]{3,2,1,0:T(8,128)S(1)}, f32[96,128]{1,0:T(8,128)S(1)}, f32[1632,128]{1,0:T(8,128)S(1)}, f32[768,128]{1,0:T(8,128)S(1)}) custom-call(f32[4]{0:T(128)S(1)} %copy-done.1, f32[4]{0:T(128)S(1)} %copy-done.2, f32[1632,256]{1,0:T(8,128)S(1)} %get-tuple-element.54.wide, f32[1056,128]{1,0:T(8,128)S(1)} %get-tuple-element.53.narrow, ...), custom_call_target="tpu_custom_call" | custom-call | flops 2000000 | bytes 2000000 | tf_op jit(solution)/shard_map/smooth_inner/pallas_call | solution.py:683
  25.2 0.0 copy-start
  25.2 0.0 collective-permute-done.6.z_one
  25.2 1.5 %collective-permute-done.7.z_two = f32[168,128]{1,0:T(8,128)S(1)} collective-permute-done((f32[168,128]{1,0:T(8,128)S(1)}, f32[168,128]{1,0:T(8,128)S(1)}, u32[]{:S(2)}, u32[]{:S(2)}) %collective-permute-start.7) | collective-permute-done | bytes 86048 | tf_op jit(solution)/shard_map/ppermute | solution.py:67
  26.7 2.4 %smooth_ends.1 = (f32[2,8,32,256]{3,2,1,0:T(8,128)S(1)}, f32[96,128]{1,0:T(8,128)S(1)}, f32[96,128]{1,0:T(8,128)S(1)}, f32[96,128]{1,0:T(8,128)S(1)}, f32[96,128]{1,0:T(8,128)S(1)}, /*index=5*/f32[544,128]{1,0:T(8,128)S(1)}) custom-call(f32[4]{0:T(128)S(1)} %copy-done.1, f32[4]{0:T(128)S(1)} %copy-done.2, f32[1632,128]{1,0:T(8,128)S(1)} %get-tuple-element.58.ends, ...), custom_call_target="tpu_custom_call" | custom-call | flops 2000000 | bytes 2000000 | tf_op jit(solution)/shard_map/smooth_ends/pallas_call | solution.py:688
  29.2 0.6 %collective-permute-start.8 = (f32[96,128]{1,0:T(8,128)S(1)}, f32[96,128]{1,0:T(8,128)S(1)}, u32[]{:S(2)}, u32[]{:S(2)}) collective-permute-start(f32[96,128]{1,0:T(8,128)S(1)} %get-tuple-element.75), channel_id=1, source_target_pairs={{0,64},{1,65},{2,66},{3,67},{4,68},{5,69},{6,70},{7,71},{8,72},{9,... | collective-permute-start | bytes 147464 | tf_op jit(solution)/shard_map/ppermute | solution.py:67
  29.8 0.0 collective-permute-start.9
  29.8 0.0 copy-done
  29.8 0.8 %bioheat_inner.1 = (f32[12,24,256]{2,1,0:T(8,128)S(1)}, f32[2,24,256]{2,1,0:T(8,128)S(1)}, f32[10,24,256]{2,1,0:T(8,128)S(1)}, f32[4,16,128]{2,1,0:T(8,128)S(1)}, f32[2,8,32,256]{3,2,1,0:T(8,128)}) custom-call(f32[1056,128]{1,0:T(8,128)S(1)} %get-tuple-element.53.narrow, f32[544,128]{1,0:T(8,128)S(1)} %get-tuple-element.66.tiles, ...), custom_call_target="tpu_custom_call" | custom-call | flops 2000000 | bytes 2000000 | tf_op jit(solution)/shard_map/bioheat_inner/pallas_call | solution.py:703
  30.6 2.8 %collective-permute-done.8.x_one = f32[96,128]{1,0:T(8,128)S(1)} collective-permute-done((f32[96,128]{1,0:T(8,128)S(1)}, f32[96,128]{1,0:T(8,128)S(1)}, u32[]{:S(2)}, u32[]{:S(2)}) %collective-permute-start.8) | collective-permute-done | bytes 49184 | tf_op jit(solution)/shard_map/ppermute | solution.py:67
  33.3 0.5 %collective-permute-done.9.x_two = f32[96,128]{1,0:T(8,128)S(1)} collective-permute-done((f32[96,128]{1,0:T(8,128)S(1)}, f32[96,128]{1,0:T(8,128)S(1)}, u32[]{:S(2)}, u32[]{:S(2)}) %collective-permute-start.9) | collective-permute-done | bytes 49184 | tf_op jit(solution)/shard_map/ppermute | solution.py:67
  33.8 1.0 %bioheat.1 = (f32[4,16,128]{2,1,0:T(8,128)}, f32[4,16,128]{2,1,0:T(8,128)}) custom-call(f32[12,24,256]{2,1,0:T(8,128)S(1)} %get-tuple-element.71.begun, f32[2,24,256]{2,1,0:T(8,128)S(1)} %get-tuple-element.72.later, f32[10,24,256]{2,1,0:T(8,128)S(1)} %get-tuple-element.73.wash, f32[4,16,128]{2,1,0:T(8,128)S(1)} %get-tuple-element.74.dose_in, ...), custom_call_target="tpu_custom_call" | custom-call | flops 2000000 | bytes 2000000 | tf_op jit(solution)/shard_map/bioheat/pallas_call | solution.py:709
  (1 shorter events, 0.0 us)
Async XLA Ops:
  0.6 21.6 %copy-start.2 = (f32[4]{0:T(128)S(1)}, f32[4]{0:T(128)}, u32[]{:S(2)}) copy-start(f32[4]{0:T(128)} %damp_t.3) | copy-start | bytes 52
  0.6 21.6 %copy-start.1 = (f32[4]{0:T(128)S(1)}, f32[4]{0:T(128)}, u32[]{:S(2)}) copy-start(f32[4]{0:T(128)} %wave_t.3) | copy-start | bytes 52
  2.1 11.5 %collective-permute-start.2 = (f32[232,256]{1,0:T(8,128)S(1)}, f32[232,256]{1,0:T(8,128)S(1)}, u32[]{:S(2)}, u32[]{:S(2)}) collective-permute-start(f32[232,256]{1,0:T(8,128)S(1)} %get-tuple-element.48), channel_id=1, source_target_pairs={{0,4},{1,5},{2,6},{3,7},{4,0},{5,1},{6,2},{7,3},{8,12},{9,13},{10,... | collective-permute-start | bytes 712712 | tf_op jit(solution)/shard_map/ppermute | solution.py:67
  4.1 10.9 %collective-permute-start.3 = (f32[232,256]{1,0:T(8,128)S(1)}, f32[232,256]{1,0:T(8,128)S(1)}, u32[]{:S(2)}, u32[]{:S(2)}) collective-permute-start(f32[232,256]{1,0:T(8,128)S(1)} %get-tuple-element.49), channel_id=1, source_target_pairs={{0,1},{1,0},{2,3},{3,2},{4,8},{5,9},{6,10},{7,11},{8,4},{9,5},{10,... | collective-permute-start | bytes 712712 | tf_op jit(solution)/shard_map/ppermute | solution.py:67
  8.8 7.5 %collective-permute-start = (f32[256,256]{1,0:T(8,128)S(1)}, f32[256,256]{1,0:T(8,128)S(1)}, u32[]{:S(2)}, u32[]{:S(2)}) collective-permute-start(f32[256,256]{1,0:T(8,128)S(1)} %get-tuple-element.46), channel_id=1, source_target_pairs={{0,64},{1,65},{2,66},{3,67},{4,68},{5,69},{6,70},{7,71},{8,72},{9,... | collective-permute-start | bytes 786440 | tf_op jit(solution)/shard_map/ppermute | solution.py:67
  10.0 7.2 %collective-permute-start.1 = (f32[256,256]{1,0:T(8,128)S(1)}, f32[256,256]{1,0:T(8,128)S(1)}, u32[]{:S(2)}, u32[]{:S(2)}) collective-permute-start(f32[256,256]{1,0:T(8,128)S(1)} %get-tuple-element.47), channel_id=1, source_target_pairs={{0,1},{1,0},{2,3},{3,2},{4,5},{5,4},{6,7},{7,6},{8,9},{9,8},{10,11... | collective-permute-start | bytes 786440 | tf_op jit(solution)/shard_map/ppermute | solution.py:67
  15.0 5.1 %collective-permute-start.4 = (f32[128,256]{1,0:T(8,128)S(1)}, f32[128,256]{1,0:T(8,128)S(1)}, u32[]{:S(2)}, u32[]{:S(2)}) collective-permute-start(f32[128,256]{1,0:T(8,128)S(1)} %get-tuple-element.51), channel_id=1, source_target_pairs={{0,64},{1,65},{2,66},{3,67},{4,68},{5,69},{6,70},{7,71},{8,72},{9,... | collective-permute-start | bytes 393224 | tf_op jit(solution)/shard_map/ppermute | solution.py:67
  16.3 5.0 %collective-permute-start.5 = (f32[128,256]{1,0:T(8,128)S(1)}, f32[128,256]{1,0:T(8,128)S(1)}, u32[]{:S(2)}, u32[]{:S(2)}) collective-permute-start(f32[128,256]{1,0:T(8,128)S(1)} %get-tuple-element.52), channel_id=1, source_target_pairs={{0,1},{1,0},{2,3},{3,2},{4,5},{5,4},{6,7},{7,6},{8,9},{9,8},{10,11... | collective-permute-start | bytes 393224 | tf_op jit(solution)/shard_map/ppermute | solution.py:67
  22.0 3.2 %collective-permute-start.6 = (f32[168,128]{1,0:T(8,128)S(1)}, f32[168,128]{1,0:T(8,128)S(1)}, u32[]{:S(2)}, u32[]{:S(2)}) collective-permute-start(f32[168,128]{1,0:T(8,128)S(1)} %get-tuple-element.59), channel_id=1, source_target_pairs={{0,1},{1,0},{2,3},{3,2},{4,5},{5,4},{6,7},{7,6},{8,9},{9,8},{10,11... | collective-permute-start | bytes 258056 | tf_op jit(solution)/shard_map/ppermute | solution.py:67
  22.1 4.6 %collective-permute-start.7 = (f32[168,128]{1,0:T(8,128)S(1)}, f32[168,128]{1,0:T(8,128)S(1)}, u32[]{:S(2)}, u32[]{:S(2)}) collective-permute-start(f32[168,128]{1,0:T(8,128)S(1)} %get-tuple-element.60), channel_id=1, source_target_pairs={{0,64},{1,2},{2,1},{3,67},{4,68},{5,6},{6,5},{7,71},{8,72},{9,10},... | collective-permute-start | bytes 258056 | tf_op jit(solution)/shard_map/ppermute | solution.py:67
  25.2 4.6 %copy-start = (f32[4,16,128]{2,1,0:T(8,128)S(1)}, f32[4,16,128]{2,1,0:T(8,128)}, u32[]{:S(2)}) copy-start(f32[4,16,128]{2,1,0:T(8,128)} %injury.1) | copy-start | bytes 98308
  29.2 4.2 %collective-permute-start.8 = (f32[96,128]{1,0:T(8,128)S(1)}, f32[96,128]{1,0:T(8,128)S(1)}, u32[]{:S(2)}, u32[]{:S(2)}) collective-permute-start(f32[96,128]{1,0:T(8,128)S(1)} %get-tuple-element.75), channel_id=1, source_target_pairs={{0,64},{1,65},{2,66},{3,67},{4,68},{5,69},{6,70},{7,71},{8,72},{9,... | collective-permute-start | bytes 147464 | tf_op jit(solution)/shard_map/ppermute | solution.py:67
  29.8 4.1 %collective-permute-start.9 = (f32[96,128]{1,0:T(8,128)S(1)}, f32[96,128]{1,0:T(8,128)S(1)}, u32[]{:S(2)}, u32[]{:S(2)}) collective-permute-start(f32[96,128]{1,0:T(8,128)S(1)} %get-tuple-element.76), channel_id=1, source_target_pairs={{0,1},{1,0},{2,3},{3,2},{4,5},{5,4},{6,7},{7,6},{8,9},{9,8},{10,11... | collective-permute-start | bytes 147464 | tf_op jit(solution)/shard_map/ppermute | solution.py:67

commit v6 on v5

--- a/solution.py
+++ b/solution.py
@@ -18,13 +18,14 @@
 
 FX, CX, LX, TX, QX = 12, 10, 8, 12, 10
 XB_CODE, XB_COARSE, XB_THERM, XB = 128, 160, 192, 256
-YB_CODE, YB_COARSE, YB_THERM, YB = 128, 192, 212, 232
-KB_CODE, KB_COARSE, KB_THERM, KB = 64, 80, 100, 128
+YB_CODE, YB_COARSE, YB_THERM, YB = 128, 184, 204, 224
+KB_CODE, KB_COARSE, KB_THERM, KB = 64, 78, 98, 128
 WIDE = 2 * FX * 48 + CX * 48
 N_CODE = 2 * FX * 48
 N_COARSE, N_THETA, N_PERF, NARROW = 0, 512, 800, 1056
 GROUPS = 16
 ZB = (WIDE + NARROW) // GROUPS
+WARM = (WIDE + N_THETA) // ZB
 AXES = ("gx", "gy", "gz")
 
 
@@ -122,8 +123,8 @@
         load.start()
     lane, col = iota((256, 128), 0), iota((256, 128), 1)
     pairs = jnp.where(lane // 2 == col, 1.0, 0.0).astype(BF16)
-    for load in loads:
-        load.wait()
+    loads[0].wait()
+    loads[2].wait()
     entries = [wash[k] for k in range(4)]
     for i in range(4):
         both = pick(codes[2 * i].astype(F32), entries) + pick(codes[2 * i + 1].astype(F32), entries)
@@ -131,6 +132,8 @@
             pool[half, i * 32 : i * 32 + 32, :] = both[:, half * 128 : half * 128 + 128]
     rows = jnp.concatenate([pool[h, pl.ds(0, 64, 2), :] + pool[h, pl.ds(1, 64, 2), :] for h in range(2)], axis=1)
     washed = exact_dot(rows, pairs) * 0.125
+    for k in (1, 3, 4):
+        loads[k].wait()
     for i in range(4):
         perf[i] = washed[i * 16 : i * 16 + 16]
     to, every = Sender(x_one, x_two, 0), pl.ds(0, 256)
@@ -149,7 +152,7 @@
         for k in range(8):
             to.put(pl.ds((c * 8 + k) * 8, 8), every, it[c, k, 24:32, :], it[c, k, 0:8, :])
     for k in range(8):
-        to.put(pl.ds(YB_CODE + k * 8, 8), every, codes[k, 24:32, :].astype(F32), codes[k, 0:8, :].astype(F32))
+        to.put(pl.ds(YB_CODE + k * 7, 7), every, codes[k, 25:32, :].astype(F32), codes[k, 0:7, :].astype(F32))
     for k in range(4):
         for c in range(2):
             to.put(pl.ds(YB_COARSE + k * 5, 5), pl.ds(128 * c, 128), co[c, k, 11:16, :], co[c, k, 0:5, :])
@@ -203,7 +206,7 @@
     for c in range(2):
         for k in range(2):
             put((c * 2 + k) * 16, 8, every, (c * 8 + 6 + k) * 8, (c * 8 + k) * 8)
-    put(KB_CODE, 8, every, YB_CODE + 56, YB_CODE)
+    put(KB_CODE, 7, every, YB_CODE + 49, YB_CODE)
     for k in range(2):
         put(KB_COARSE + k * 10, 5, every, YB_COARSE + (2 + k) * 5, YB_COARSE + k * 5)
     for k in range(3):
@@ -242,7 +245,8 @@
     for f in range(CX):
         at = N_CODE + f * 48
         wide[pl.ds(at, 32), :] = block.code(f, 0, 32)
-        wide[pl.ds(at + 32, 8), :], wide[pl.ds(at + 40, 8), :] = beside(f, 1, 8, 8, YB_CODE, KB_CODE, every)
+        wide[pl.ds(at + 32, 16), :] = jnp.zeros((16, 256), F32)
+        wide[pl.ds(at + 32, 7), :], wide[pl.ds(at + 41, 7), :] = beside(f, 1, 8, 7, YB_CODE, KB_CODE, every)
     for c in range(2):
         for f in range(LX):
             at = N_COARSE + (c * LX + f) * 32
@@ -267,8 +271,7 @@
         over, under = beside(f + 1, 4, 4, 4, YB_THERM, KB_THERM, pl.ds(128, 128), 1)
         narrow[pl.ds(at + 16, 4), :], narrow[pl.ds(at + 20, 4), :] = over, under
     narrow[pl.ds(N_PERF + QX * 24, NARROW - N_PERF - QX * 24), :] = jnp.zeros((NARROW - N_PERF - QX * 24, 128), F32)
-    lane = iota((ZB, 128), 1) // 8
-    ends = []
+    lane, ends = iota((ZB, 128), 1) // 8, []
     for half, shift in ((1, 8), (0, 0)):
         packed = None
         for g in range(GROUPS):
@@ -278,6 +281,18 @@
             packed = part if packed is None else jnp.where(lane == g, part, packed)
         ends.append(packed)
     Sender(one, two, 2).put(pl.ds(0, ZB), pl.ds(0, 128), *ends)
+
+
+def unpack_z(one, two, groups, lane_after, halo):
+    lane = iota((ZB, 128), 1)
+    came, every = Receiver(one, two, 2), (pl.ds(0, ZB), pl.ds(0, 128))
+    right, left = came.after(*every), came.before(*every)
+    for k, g in enumerate(groups):
+        turn = (128 + lane_after - 8 * g) % 128
+        after = pltpu.roll(right, turn, 1) if turn else right
+        turn = (120 - 8 * g) % 128
+        before = pltpu.roll(left, turn, 1) if turn else left
+        halo[pl.ds(k * ZB, ZB), :] = jnp.where(lane < 96, after, before)
 
 
 def strip_cell(lane):
@@ -450,21 +465,10 @@
     power[...] = exact_dot(sums, gather[...]) * 0.125
 
 
-def smooth_ends(wave_t, damp_t, ends, z_one, z_two, source, spread, gather, inner, power_inner, fine_ends,
-                out, power, power_halo, one, two, tiles,
+def smooth_ends(wave_t, damp_t, ends, z_one, z_two, source, spread, gather, power_inner, fine_ends,
+                out, power, power_halo, one, two,
                 halo, grown_halo, fine, first, second, gain_r, gain_i, pool):
-    lane = iota((ZB, 128), 1)
-    came, every = Receiver(z_one, z_two, 2), (pl.ds(0, ZB), pl.ds(0, 128))
-    right, left = came.after(*every), came.before(*every)
-    for g in range(GROUPS):
-        turn = (192 - 8 * g) % 128
-        after = pltpu.roll(right, turn, 1) if turn else right
-        turn = (120 - 8 * g) % 128
-        before = pltpu.roll(left, turn, 1) if turn else left
-        halo[pl.ds(g * ZB, ZB), :] = jnp.where(lane < 96, after, before)
-    beyond = halo[pl.ds(WIDE + N_THETA, NARROW - N_THETA), :]
-    tiles[...] = jnp.where(iota(beyond.shape, 1) < 64, pltpu.roll(beyond, 64, 1), beyond)
-
+    unpack_z(z_one, z_two, range(WARM + 1), 64, halo)
     at_z = lax.axis_index("gz")
     after_ok, before_ok = flag(at_z < 3), flag(at_z > 0)
     z_ok = jnp.where(iota((32, 128), 1) < 96, after_ok, before_ok)
@@ -476,12 +480,9 @@
     def strip(at):
         return jnp.where(lane < 64, ends[pl.ds(at, 48), :], halo[pl.ds(at, 48), :])
 
-    low, high = iota((32, 128), 1) < 8, iota((32, 128), 1) >= 120
-
     def emit(f, new_r, new_i):
-        for c, new in enumerate((new_r[0:32], new_i[0:32])):
-            out[c, f, :, pl.ds(0, 128)] = jnp.where(low, new, inner[c, f, :, pl.ds(0, 128)])
-            out[c, f, :, pl.ds(128, 128)] = jnp.where(high, pltpu.roll(new, 64, 1), inner[c, f, :, pl.ds(128, 128)])
+        out[0, f] = new_r[0:32]
+        out[1, f] = new_i[0:32]
 
     z_ok = jnp.where(lane < 64, 1.0, jnp.where(lane < 96, after_ok, before_ok))
     live = jnp.where((lane < 72) | (lane >= 120), z_ok, 0.0)
@@ -535,14 +536,23 @@
     return jnp.concatenate([ref[pl.ds(24 * (f - 4), 24), :] for ref in (power, power_halo)], axis=1)
 
 
-def bioheat_inner(narrow, tiles, power, power_halo, injury, wave, begun, later, wash, dose, wave_out, now, sem):
+def bioheat_inner(narrow, z_one, z_two, power, power_halo, injury, inner, ends, begun, later, wash, dose, wave_out,
+                  now, tiles, wave, sem):
+    low, high = iota((32, 128), 1) < 8, iota((32, 128), 1) >= 120
+    for c in range(2):
+        for f in range(8):
+            new = ends[c, f]
+            wave[c, f, :, pl.ds(0, 128)] = jnp.where(low, new, inner[c, f, :, pl.ds(0, 128)])
+            turned = pltpu.roll(new, 64, 1)
+            wave[c, f, :, pl.ds(128, 128)] = jnp.where(high, turned, inner[c, f, :, pl.ds(128, 128)])
     store = pltpu.make_async_copy(wave, wave_out, sem)
     store.start()
+    unpack_z(z_one, z_two, range(WARM, GROUPS), 0, tiles)
     heat = Bioheat()
 
     def extended(base, f):
         at = base + f * 24
-        return jnp.concatenate([narrow[pl.ds(at, 24), :], tiles[pl.ds(at - N_THETA, 24), :]], axis=1)
+        return jnp.concatenate([narrow[pl.ds(at, 24), :], tiles[pl.ds(WIDE + at - WARM * ZB, 24), :]], axis=1)
 
     for f in range(TX):
         now[f] = extended(N_THETA, f) * heat.edge[f]
@@ -582,7 +592,8 @@
                 other[f] = later[f - 5]
                 continue
             new = heat.finish(heat.step(state, wash, f), heats[f], f)
-            other[f] = new
+            if turn < 3:
+                other[f] = new
             if 4 <= f < 8:
                 dose[f - 4] = dose[f - 4] + injury_of(new)
                 if turn == 3:
@@ -666,7 +677,7 @@
 
     wide, narrow, *sent = call(
         pack_z, "pack_z", [vmem()] * 11,
-        [shaped(WIDE, 256), shaped(NARROW, 128), shaped(ZB, 128), shaped(ZB, 128)],
+        [shaped(WIDE, 256), shaped(NARROW, 128)] + [shaped(ZB, 128)] * 2,
     )(*own, *x_came, *y_came, *corners)
     z_came = exchange(sent, 2)
 
@@ -685,27 +696,25 @@
         [shaped(2, 8, 32, 256), shaped(96, 128), shaped(WIDE, 128), shaped(2 * LX * 48, 128)],
         [pltpu.VMEM((2 * LX * 48, 128), F32)] + scratch(256),
     )(class_wavespeed, class_damping, wide, narrow, field, weights[0], weights[1], weights[2])
-    pressure, power, power_halo, *sent, tiles = call(
-        smooth_ends, "smooth_ends", [smem()] * 2 + [vmem()] * 9,
-        [
-            shaped(2, 8, 32, 256),
-            shaped(96, 128),
-            shaped(96, 128),
-            shaped(96, 128),
-            shaped(96, 128),
-            shaped(NARROW - N_THETA, 128),
-        ],
-        [pltpu.VMEM((WIDE + NARROW, 128), F32), pltpu.VMEM((2 * LX * 48, 128), F32)] + scratch(128),
-    )(class_wavespeed, class_damping, ends, *z_came, strip, weights[2], weights[3], inner, power_inner, fine_ends)
+    ends, power, power_halo, *sent = call(
+        smooth_ends, "smooth_ends", [smem()] * 2 + [vmem()] * 8,
+        [shaped(2, 8, 32, 128)] + [shaped(96, 128)] * 4,
+        [pltpu.VMEM(((WARM + 1) * ZB, 128), F32), pltpu.VMEM((2 * LX * 48, 128), F32)] + scratch(128),
+    )(class_wavespeed, class_damping, ends, *z_came, strip, weights[2], weights[3], power_inner, fine_ends)
     x_came = exchange(sent, 0)
 
     block = shaped(TX, 24, 256)
     begun, later, wash, dose, pressure = call(
-        bioheat_inner, "bioheat_inner", [vmem()] * 6,
+        bioheat_inner, "bioheat_inner", [vmem()] * 8,
         [block, shaped(2, 24, 256), shaped(QX, 24, 256), shaped(4, 16, 128), shaped(2, 8, 32, 256)],
-        [pltpu.VMEM((TX, 24, 256), F32), pltpu.SemaphoreType.DMA],
+        [
+            pltpu.VMEM((TX, 24, 256), F32),
+            pltpu.VMEM(((GROUPS - WARM) * ZB, 128), F32),
+            pltpu.VMEM((2, 8, 32, 256), F32),
+            pltpu.SemaphoreType.DMA,
+        ],
         [vmem()] * 4 + [hbm()],
-    )(narrow, tiles, power, power_halo, injury_integral, pressure)
+    )(narrow, *z_came, power, power_halo, injury_integral, inner, ends)
     warmth, dose = call(
         bioheat, "bioheat", [vmem()] * 8,
         [shaped(4, 16, 128), shaped(4, 16, 128)],

time: 35.1 us -> 34.7 us (0.989)
  Pallas kernels: 13 us -> 11.7 us
  waiting for transfers between devices: 11.1 us -> 12 us
    pallas_call x1, Pallas kernels: 3.6 us -> 2.35 us  [on_device(): call(sources, 'sources', [hbm(), hbm(), vmem()], [shaped(2, CX, 48, 256),...]
    ppermute x10, waiting for transfers between devices: 11.1 us -> 12 us  [exchange(): lax.ppermute(buffer, AXES, swaps(sizes, axis, bool(k)))]
  transfers between devices with their start and end apart: 10 -> 10, of which waited for: 7 -> 8; matrix products, arithmetic and copies ran while one was open for 0% -> 0% of each run, Pallas kernels for 21% -> 18%
where the time goes in v6:
time: 34.7 us; the launch traced here: 34.5 us
  waiting for transfers between devices  12 us (35%)
  Pallas kernels  11.7 us (34%)
  starting transfers between devices  10 us (29%)
  between operations  0.76 us (2%)
    ppermute x10, waiting for transfers between devices, exchange(): lax.ppermute(buffer, AXES, swaps(sizes, axis, bool(k)))  12 us
    ppermute x10, starting transfers between devices, exchange(): lax.ppermute(buffer, AXES, swaps(sizes, axis, bool(k)))  10 us
    pallas_call x1, Pallas kernels, on_device(): call(smooth_inner, 'smooth_inner', [smem()] * 2 + [vmem()] * 6, [shaped(2...  2.9 us
    pallas_call x1, Pallas kernels, on_device(): call(smooth_ends, 'smooth_ends', [smem()] * 2 + [vmem()] * 8, [shaped(2,...  2.35 us
    pallas_call x1, Pallas kernels, on_device(): call(sources, 'sources', [hbm(), hbm(), vmem()], [shaped(2, CX, 48, 256),...  2.35 us
    pallas_call x1, Pallas kernels, on_device(): call(pack_x, 'pack_x', [hbm()] * 5, [shaped(XB, 256), shaped(XB, 256), sh...  1.33 us
    pallas_call x1, Pallas kernels, on_device(): call(bioheat, 'bioheat', [vmem()] * 8, [shaped(4, 16, 128), shaped(4, 16,...  0.97 us
    pallas_call x1, Pallas kernels, on_device(): call(bioheat_inner, 'bioheat_inner', [vmem()] * 8, [block, shaped(2, 24,...  0.94 us
  transfers between devices with their start and end apart: 10, of which 8 were waited for; matrix products, arithmetic and copies ran while one was open for 0% of the time, Pallas kernels for 18%

profile of v6, /device:TPU:20, one launch (start us, length us, event | category | flops | bytes accessed | tf_op | source)
XLA Modules:
  0.0 34.5 jit_solution(8421943519713489144)
XLA Ops:
  0.6 0.0 copy-start.2
  0.6 0.0 copy-start.1
  0.7 1.3 %pack_x.1 = (f32[256,256]{1,0:T(8,128)S(1)}, f32[256,256]{1,0:T(8,128)S(1)}, f32[224,256]{1,0:T(8,128)S(1)}, f32[224,256]{1,0:T(8,128)S(1)}, f32[4,16,128]{2,1,0...) custom-call(f32[4]{0:T(128)} %wash_h.1, ...), custom_call_target="tpu_custom_call" | custom-call | flops 2000000 | bytes 2000000 | tf_op jit(solution)/shard_map/pack_x/pallas_call | solution.py:638
  2.0 2.0 %collective-permute-start.2 = (f32[224,256]{1,0:T(8,128)S(1)}, f32[224,256]{1,0:T(8,128)S(1)}, u32[]{:S(2)}, u32[]{:S(2)}) collective-permute-start(f32[224,256]{1,0:T(8,128)S(1)} %get-tuple-element.47), channel_id=1, source_target_pairs={{0,4},{1,5},{2,6},{3,7},{4,0},{5,1},{6,2},{7,3},{8,12},{9,13},{10,... | collective-permute-start | bytes 688136 | tf_op jit(solution)/shard_map/ppermute | solution.py:68
  4.0 4.7 %collective-permute-start.3 = (f32[224,256]{1,0:T(8,128)S(1)}, f32[224,256]{1,0:T(8,128)S(1)}, u32[]{:S(2)}, u32[]{:S(2)}) collective-permute-start(f32[224,256]{1,0:T(8,128)S(1)} %get-tuple-element.48), channel_id=1, source_target_pairs={{0,1},{1,0},{2,3},{3,2},{4,8},{5,9},{6,10},{7,11},{8,4},{9,5},{10,... | collective-permute-start | bytes 688136 | tf_op jit(solution)/shard_map/ppermute | solution.py:68
  8.7 1.2 %collective-permute-start = (f32[256,256]{1,0:T(8,128)S(1)}, f32[256,256]{1,0:T(8,128)S(1)}, u32[]{:S(2)}, u32[]{:S(2)}) collective-permute-start(f32[256,256]{1,0:T(8,128)S(1)} %get-tuple-element.45), channel_id=1, source_target_pairs={{0,64},{1,65},{2,66},{3,67},{4,68},{5,69},{6,70},{7,71},{8,72},{9,... | collective-permute-start | bytes 786440 | tf_op jit(solution)/shard_map/ppermute | solution.py:68
  9.9 0.0 collective-permute-start.1
  9.9 2.3 %sources.1 = (f32[2,10,48,256]{3,2,1,0:T(8,128)S(1)}, f32[2,10,48,128]{3,2,1,0:T(8,128)S(1)}, bf16[128,256]{1,0:T(8,128)(2,1)S(1)}, bf16[256,128]{1,0:T(8,128)(2...) custom-call(s32[3,1024]{1,0:T(4,128)} %bitcast.1, f32[2,1024]{1,0:T(2,128)} %exc_h.1, ...), custom_call_target="tpu_custom_call" | custom-call | flops 8000000 | bytes 8000000 | tf_op jit(solution)/shard_map/sources/pallas_call | solution.py:657
  12.3 0.0 collective-permute-done.2.y_one
  12.3 2.4 %collective-permute-done.3.y_two = f32[224,256]{1,0:T(8,128)S(1)} collective-permute-done((f32[224,256]{1,0:T(8,128)S(1)}, f32[224,256]{1,0:T(8,128)S(1)}, u32[]{:S(2)}, u32[]{:S(2)}) %collective-permute-start.3) | collective-permute-done | bytes 229408 | tf_op jit(solution)/shard_map/ppermute | solution.py:68
  14.7 1.3 %collective-permute-start.4 = (f32[128,256]{1,0:T(8,128)S(1)}, f32[128,256]{1,0:T(8,128)S(1)}, u32[]{:S(2)}, u32[]{:S(2)}) collective-permute-start(f32[128,256]{1,0:T(8,128)S(1)} %get-tuple-element.50), channel_id=1, source_target_pairs={{0,64},{1,65},{2,66},{3,67},{4,68},{5,69},{6,70},{7,71},{8,72},{9,... | collective-permute-start | bytes 393224 | tf_op jit(solution)/shard_map/ppermute | solution.py:68
  16.0 0.0 collective-permute-start.5
  16.0 0.3 collective-permute-done.x_one
  16.3 0.9 %collective-permute-done.1.x_two = f32[256,256]{1,0:T(8,128)S(1)} collective-permute-done((f32[256,256]{1,0:T(8,128)S(1)}, f32[256,256]{1,0:T(8,128)S(1)}, u32[]{:S(2)}, u32[]{:S(2)}) %collective-permute-start.1) | collective-permute-done | bytes 262176 | tf_op jit(solution)/shard_map/ppermute | solution.py:68
  17.2 2.6 %collective-permute-done.4.k_one = f32[128,256]{1,0:T(8,128)S(1)} collective-permute-done((f32[128,256]{1,0:T(8,128)S(1)}, f32[128,256]{1,0:T(8,128)S(1)}, u32[]{:S(2)}, u32[]{:S(2)}) %collective-permute-start.4) | collective-permute-done | bytes 131104 | tf_op jit(solution)/shard_map/ppermute | solution.py:68
  19.8 1.2 %collective-permute-done.5.k_two = f32[128,256]{1,0:T(8,128)S(1)} collective-permute-done((f32[128,256]{1,0:T(8,128)S(1)}, f32[128,256]{1,0:T(8,128)S(1)}, u32[]{:S(2)}, u32[]{:S(2)}) %collective-permute-start.5) | collective-permute-done | bytes 131104 | tf_op jit(solution)/shard_map/ppermute | solution.py:68
  21.0 0.8 %pack_z.1 = (f32[1632,256]{1,0:T(8,128)S(1)}, f32[1056,128]{1,0:T(8,128)S(1)}, f32[168,128]{1,0:T(8,128)S(1)}, f32[168,128]{1,0:T(8,128)S(1)}) custom-call(f32[2,8,32,256]{3,2,1,0:T(8,128)S(1)} %get-tuple-element.40.it, f32[2,4,16,128]{3,2,1,0:T(8,128)S(1)} %get-tuple-element.41.co, s32[8,32,256]{2,1,0:T(8,128)S(1)} %get-tuple-element.42.codes, ...), custom_call_target="tpu_custom_call" | custom-call | flops 2000000 | bytes 2000000 | tf_op jit(solution)/shard_map/pack_z/pallas_call | solution.py:678
  21.8 0.1 collective-permute-start.6
  21.9 0.1 collective-permute-start.7
  22.0 0.0 copy-done.2
  22.0 0.0 copy-done.1
  22.0 2.9 %smooth_inner.1 = (f32[2,8,32,256]{3,2,1,0:T(8,128)S(1)}, f32[96,128]{1,0:T(8,128)S(1)}, f32[1632,128]{1,0:T(8,128)S(1)}, f32[768,128]{1,0:T(8,128)S(1)}) custom-call(f32[4]{0:T(128)S(1)} %copy-done.1, f32[4]{0:T(128)S(1)} %copy-done.2, f32[1632,256]{1,0:T(8,128)S(1)} %get-tuple-element.55.wide, f32[1056,128]{1,0:T(8,128)S(1)} %get-tuple-element.52.narrow, ...), custom_call_target="tpu_custom_call" | custom-call | flops 2000000 | bytes 2000000 | tf_op jit(solution)/shard_map/smooth_inner/pallas_call | solution.py:694
  24.9 0.0 copy-start
  24.9 0.0 collective-permute-done.6.z_one
  24.9 1.5 %collective-permute-done.7.z_two = f32[168,128]{1,0:T(8,128)S(1)} collective-permute-done((f32[168,128]{1,0:T(8,128)S(1)}, f32[168,128]{1,0:T(8,128)S(1)}, u32[]{:S(2)}, u32[]{:S(2)}) %collective-permute-start.7) | collective-permute-done | bytes 86048 | tf_op jit(solution)/shard_map/ppermute | solution.py:68
  26.5 2.3 %smooth_ends.1 = (f32[2,8,32,128]{3,2,1,0:T(8,128)S(1)}, f32[96,128]{1,0:T(8,128)S(1)}, f32[96,128]{1,0:T(8,128)S(1)}, f32[96,128]{1,0:T(8,128)S(1)}, f32[96,128]{1,0:T(8,128)S(1)}) custom-call(f32[4]{0:T(128)S(1)} %copy-done.1, f32[4]{0:T(128)S(1)} %copy-done.2, f32[1632,128]{1,0:T(8,128)S(1)} %get-tuple-element.59.ends, ...), custom_call_target="tpu_custom_call" | custom-call | flops 2000000 | bytes 2000000 | tf_op jit(solution)/shard_map/smooth_ends/pallas_call | solution.py:699
  28.8 0.6 %collective-permute-start.8 = (f32[96,128]{1,0:T(8,128)S(1)}, f32[96,128]{1,0:T(8,128)S(1)}, u32[]{:S(2)}, u32[]{:S(2)}) collective-permute-start(f32[96,128]{1,0:T(8,128)S(1)} %get-tuple-element.73), channel_id=1, source_target_pairs={{0,64},{1,65},{2,66},{3,67},{4,68},{5,69},{6,70},{7,71},{8,72},{9,... | collective-permute-start | bytes 147464 | tf_op jit(solution)/shard_map/ppermute | solution.py:68
  29.4 0.0 collective-permute-start.9
  29.4 0.0 copy-done
  29.4 0.9 %bioheat_inner.1 = (f32[12,24,256]{2,1,0:T(8,128)S(1)}, f32[2,24,256]{2,1,0:T(8,128)S(1)}, f32[10,24,256]{2,1,0:T(8,128)S(1)}, f32[4,16,128]{2,1,0:T(8,128)S(1)}, f32[2,8,32,256]{3,2,1,0:T(8,128)}) custom-call(f32[1056,128]{1,0:T(8,128)S(1)} %get-tuple-element.52.narrow, f32[168,128]{1,0:T(8,128)S(1)} %collective-permute-done.6.z_one, ...), custom_call_target="tpu_custom_call" | custom-call | flops 2000000 | bytes 2000000 | tf_op jit(solution)/shard_map/bioheat_inner/pallas_call | solution.py:707
  30.4 2.6 %collective-permute-done.8.x_one = f32[96,128]{1,0:T(8,128)S(1)} collective-permute-done((f32[96,128]{1,0:T(8,128)S(1)}, f32[96,128]{1,0:T(8,128)S(1)}, u32[]{:S(2)}, u32[]{:S(2)}) %collective-permute-start.8) | collective-permute-done | bytes 49184 | tf_op jit(solution)/shard_map/ppermute | solution.py:68
  33.0 0.5 %collective-permute-done.9.x_two = f32[96,128]{1,0:T(8,128)S(1)} collective-permute-done((f32[96,128]{1,0:T(8,128)S(1)}, f32[96,128]{1,0:T(8,128)S(1)}, u32[]{:S(2)}, u32[]{:S(2)}) %collective-permute-start.9) | collective-permute-done | bytes 49184 | tf_op jit(solution)/shard_map/ppermute | solution.py:68
  33.5 1.0 %bioheat.1 = (f32[4,16,128]{2,1,0:T(8,128)}, f32[4,16,128]{2,1,0:T(8,128)}) custom-call(f32[12,24,256]{2,1,0:T(8,128)S(1)} %get-tuple-element.69.begun, f32[2,24,256]{2,1,0:T(8,128)S(1)} %get-tuple-element.70.later, f32[10,24,256]{2,1,0:T(8,128)S(1)} %get-tuple-element.71.wash, f32[4,16,128]{2,1,0:T(8,128)S(1)} %get-tuple-element.72.dose_in, ...), custom_call_target="tpu_custom_call" | custom-call | flops 2000000 | bytes 2000000 | tf_op jit(solution)/shard_map/bioheat/pallas_call | solution.py:718
  (1 shorter events, 0.0 us)
Async XLA Ops:
  0.6 21.4 %copy-start.2 = (f32[4]{0:T(128)S(1)}, f32[4]{0:T(128)}, u32[]{:S(2)}) copy-start(f32[4]{0:T(128)} %damp_t.3) | copy-start | bytes 52
  0.6 21.4 %copy-start.1 = (f32[4]{0:T(128)S(1)}, f32[4]{0:T(128)}, u32[]{:S(2)}) copy-start(f32[4]{0:T(128)} %wave_t.3) | copy-start | bytes 52
  2.0 10.3 %collective-permute-start.2 = (f32[224,256]{1,0:T(8,128)S(1)}, f32[224,256]{1,0:T(8,128)S(1)}, u32[]{:S(2)}, u32[]{:S(2)}) collective-permute-start(f32[224,256]{1,0:T(8,128)S(1)} %get-tuple-element.47), channel_id=1, source_target_pairs={{0,4},{1,5},{2,6},{3,7},{4,0},{5,1},{6,2},{7,3},{8,12},{9,13},{10,... | collective-permute-start | bytes 688136 | tf_op jit(solution)/shard_map/ppermute | solution.py:68
  4.0 10.7 %collective-permute-start.3 = (f32[224,256]{1,0:T(8,128)S(1)}, f32[224,256]{1,0:T(8,128)S(1)}, u32[]{:S(2)}, u32[]{:S(2)}) collective-permute-start(f32[224,256]{1,0:T(8,128)S(1)} %get-tuple-element.48), channel_id=1, source_target_pairs={{0,1},{1,0},{2,3},{3,2},{4,8},{5,9},{6,10},{7,11},{8,4},{9,5},{10,... | collective-permute-start | bytes 688136 | tf_op jit(solution)/shard_map/ppermute | solution.py:68
  8.7 7.6 %collective-permute-start = (f32[256,256]{1,0:T(8,128)S(1)}, f32[256,256]{1,0:T(8,128)S(1)}, u32[]{:S(2)}, u32[]{:S(2)}) collective-permute-start(f32[256,256]{1,0:T(8,128)S(1)} %get-tuple-element.45), channel_id=1, source_target_pairs={{0,64},{1,65},{2,66},{3,67},{4,68},{5,69},{6,70},{7,71},{8,72},{9,... | collective-permute-start | bytes 786440 | tf_op jit(solution)/shard_map/ppermute | solution.py:68
  9.9 7.3 %collective-permute-start.1 = (f32[256,256]{1,0:T(8,128)S(1)}, f32[256,256]{1,0:T(8,128)S(1)}, u32[]{:S(2)}, u32[]{:S(2)}) collective-permute-start(f32[256,256]{1,0:T(8,128)S(1)} %get-tuple-element.46), channel_id=1, source_target_pairs={{0,1},{1,0},{2,3},{3,2},{4,5},{5,4},{6,7},{7,6},{8,9},{9,8},{10,11... | collective-permute-start | bytes 786440 | tf_op jit(solution)/shard_map/ppermute | solution.py:68
  14.7 5.1 %collective-permute-start.4 = (f32[128,256]{1,0:T(8,128)S(1)}, f32[128,256]{1,0:T(8,128)S(1)}, u32[]{:S(2)}, u32[]{:S(2)}) collective-permute-start(f32[128,256]{1,0:T(8,128)S(1)} %get-tuple-element.50), channel_id=1, source_target_pairs={{0,64},{1,65},{2,66},{3,67},{4,68},{5,69},{6,70},{7,71},{8,72},{9,... | collective-permute-start | bytes 393224 | tf_op jit(solution)/shard_map/ppermute | solution.py:68
  16.0 5.0 %collective-permute-start.5 = (f32[128,256]{1,0:T(8,128)S(1)}, f32[128,256]{1,0:T(8,128)S(1)}, u32[]{:S(2)}, u32[]{:S(2)}) collective-permute-start(f32[128,256]{1,0:T(8,128)S(1)} %get-tuple-element.51), channel_id=1, source_target_pairs={{0,1},{1,0},{2,3},{3,2},{4,5},{5,4},{6,7},{7,6},{8,9},{9,8},{10,11... | collective-permute-start | bytes 393224 | tf_op jit(solution)/shard_map/ppermute | solution.py:68
  21.8 3.1 %collective-permute-start.6 = (f32[168,128]{1,0:T(8,128)S(1)}, f32[168,128]{1,0:T(8,128)S(1)}, u32[]{:S(2)}, u32[]{:S(2)}) collective-permute-start(f32[168,128]{1,0:T(8,128)S(1)} %get-tuple-element.53), channel_id=1, source_target_pairs={{0,1},{1,0},{2,3},{3,2},{4,5},{5,4},{6,7},{7,6},{8,9},{9,8},{10,11... | collective-permute-start | bytes 258056 | tf_op jit(solution)/shard_map/ppermute | solution.py:68
  21.9 4.6 %collective-permute-start.7 = (f32[168,128]{1,0:T(8,128)S(1)}, f32[168,128]{1,0:T(8,128)S(1)}, u32[]{:S(2)}, u32[]{:S(2)}) collective-permute-start(f32[168,128]{1,0:T(8,128)S(1)} %get-tuple-element.54), channel_id=1, source_target_pairs={{0,64},{1,2},{2,1},{3,67},{4,68},{5,6},{6,5},{7,71},{8,72},{9,10},... | collective-permute-start | bytes 258056 | tf_op jit(solution)/shard_map/ppermute | solution.py:68
  24.9 4.5 %copy-start = (f32[4,16,128]{2,1,0:T(8,128)S(1)}, f32[4,16,128]{2,1,0:T(8,128)}, u32[]{:S(2)}) copy-start(f32[4,16,128]{2,1,0:T(8,128)} %injury.1) | copy-start | bytes 98308
  28.8 4.2 %collective-permute-start.8 = (f32[96,128]{1,0:T(8,128)S(1)}, f32[96,128]{1,0:T(8,128)S(1)}, u32[]{:S(2)}, u32[]{:S(2)}) collective-permute-start(f32[96,128]{1,0:T(8,128)S(1)} %get-tuple-element.73), channel_id=1, source_target_pairs={{0,64},{1,65},{2,66},{3,67},{4,68},{5,69},{6,70},{7,71},{8,72},{9,... | collective-permute-start | bytes 147464 | tf_op jit(solution)/shard_map/ppermute | solution.py:68
  29.4 4.1 %collective-permute-start.9 = (f32[96,128]{1,0:T(8,128)S(1)}, f32[96,128]{1,0:T(8,128)S(1)}, u32[]{:S(2)}, u32[]{:S(2)}) collective-permute-start(f32[96,128]{1,0:T(8,128)S(1)} %get-tuple-element.74), channel_id=1, source_target_pairs={{0,1},{1,0},{2,3},{3,2},{4,5},{5,4},{6,7},{7,6},{8,9},{9,8},{10,11... | collective-permute-start | bytes 147464 | tf_op jit(solution)/shard_map/ppermute | solution.py:68

commit v7 on v6

--- a/solution.py
+++ b/solution.py
@@ -447,8 +447,8 @@
 def smooth_inner(wave_t, damp_t, wide, narrow, source, spread, gather, spread_strip, out, power, ends, fine_ends,
                  grown, fine, first, second, gain_r, gain_i, pool):
     coarse_rows(lambda at: narrow[pl.ds(N_COARSE + at, 32), :], None, grown)
-    fine[...] = exact_dot(grown[...], spread[...])
-    fine_ends[...] = exact_dot(grown[...], spread_strip[pl.ds(0, 128), :])
+    fine[...] = exact_dot(grown[pl.ds(0, 2 * LX * 48), :], spread[...])
+    fine_ends[...] = exact_dot(grown[pl.ds(0, 2 * LX * 48), :], spread_strip[pl.ds(0, 128), :])
     lane = iota((48, 128), 1)
     for at in range(0, WIDE, 48):
         turned = pltpu.roll(wide[pl.ds(at, 48), pl.ds(128, 128)], 64, 1)
@@ -473,7 +473,7 @@
     after_ok, before_ok = flag(at_z < 3), flag(at_z > 0)
     z_ok = jnp.where(iota((32, 128), 1) < 96, after_ok, before_ok)
     coarse_rows(lambda at: halo[pl.ds(WIDE + N_COARSE + at, 32), :], z_ok, grown_halo)
-    fine[...] = fine_ends[...] + exact_dot(grown_halo[...], spread[pl.ds(128, 128), :])
+    fine[...] = fine_ends[...] + exact_dot(grown_halo[pl.ds(0, 2 * LX * 48), :], spread[pl.ds(128, 128), :])
 
     lane = iota((48, 128), 1)
 
@@ -648,7 +648,7 @@
             shaped(8, 32, 256, dtype=jnp.int32),
             shaped(4, 16, 128),
         ],
-        [pltpu.VMEM((2, 128, 128), F32), pltpu.SMEM((4,), F32), pltpu.SemaphoreType.DMA((5,))],
+        [pltpu.VMEM((2, 128 + 8, 128), F32), pltpu.SMEM((4,), F32), pltpu.SemaphoreType.DMA((5,))],
     )(*in_hbm(washout_fraction, acoustic_iterate, coarse_update, class_codes_volume, thermal_excess))
     own = (it, co, codes, theta, perf)
     y_came = exchange(sent[2:], 1)
@@ -688,18 +688,18 @@
             pltpu.VMEM((2, CX, 48, width), F32),
             pltpu.VMEM((CX, 48, width), F32),
             pltpu.VMEM((CX, 48, width), F32),
-            pltpu.VMEM((width // 128, 192, 128), F32),
+            pltpu.VMEM((width // 128, 192 + 8, 128), F32),
         ]
 
     inner, power_inner, ends, fine_ends = call(
         smooth_inner, "smooth_inner", [smem()] * 2 + [vmem()] * 6,
         [shaped(2, 8, 32, 256), shaped(96, 128), shaped(WIDE, 128), shaped(2 * LX * 48, 128)],
-        [pltpu.VMEM((2 * LX * 48, 128), F32)] + scratch(256),
+        [pltpu.VMEM((2 * LX * 48 + 8, 128), F32)] + scratch(256),
     )(class_wavespeed, class_damping, wide, narrow, field, weights[0], weights[1], weights[2])
     ends, power, power_halo, *sent = call(
         smooth_ends, "smooth_ends", [smem()] * 2 + [vmem()] * 8,
         [shaped(2, 8, 32, 128)] + [shaped(96, 128)] * 4,
-        [pltpu.VMEM(((WARM + 1) * ZB, 128), F32), pltpu.VMEM((2 * LX * 48, 128), F32)] + scratch(128),
+        [pltpu.VMEM(((WARM + 1) * ZB, 128), F32), pltpu.VMEM((2 * LX * 48 + 8, 128), F32)] + scratch(128),
     )(class_wavespeed, class_damping, ends, *z_came, strip, weights[2], weights[3], power_inner, fine_ends)
     x_came = exchange(sent, 0)
 

time: 34.7 us -> 34.7 us (level)
  waiting for transfers between devices: 12 us -> 10.8 us
  Pallas kernels: 11.7 us -> 12.7 us
    ppermute x10, waiting for transfers between devices: 12 us -> 10.8 us  [exchange(): lax.ppermute(buffer, AXES, swaps(sizes, axis, bool(k)))]
    pallas_call x1, Pallas kernels: 2.35 us -> 3.39 us  [on_device(): call(sources, 'sources', [hbm(), hbm(), vmem()], [shaped(2, CX, 48, 256),...]
  transfers between devices with their start and end apart: 10 -> 10, of which waited for: 8 -> 8; matrix products, arithmetic and copies ran while one was open for 0% -> 0% of each run, Pallas kernels for 18% -> 21%
where the time goes in v7:
time: 34.7 us; the launch traced here: 34.5 us
  Pallas kernels  12.7 us (37%)
  waiting for transfers between devices  10.8 us (31%)
  starting transfers between devices  10.1 us (29%)
  between operations  0.76 us (2%)
    ppermute x10, waiting for transfers between devices, exchange(): lax.ppermute(buffer, AXES, swaps(sizes, axis, bool(k)))  10.8 us
    ppermute x10, starting transfers between devices, exchange(): lax.ppermute(buffer, AXES, swaps(sizes, axis, bool(k)))  10.1 us
    pallas_call x1, Pallas kernels, on_device(): call(sources, 'sources', [hbm(), hbm(), vmem()], [shaped(2, CX, 48, 256),...  3.39 us
    pallas_call x1, Pallas kernels, on_device(): call(smooth_inner, 'smooth_inner', [smem()] * 2 + [vmem()] * 6, [shaped(2...  2.91 us
    pallas_call x1, Pallas kernels, on_device(): call(smooth_ends, 'smooth_ends', [smem()] * 2 + [vmem()] * 8, [shaped(2,...  2.34 us
    pallas_call x1, Pallas kernels, on_device(): call(pack_x, 'pack_x', [hbm()] * 5, [shaped(XB, 256), shaped(XB, 256), sh...  1.33 us
    pallas_call x1, Pallas kernels, on_device(): call(bioheat, 'bioheat', [vmem()] * 8, [shaped(4, 16, 128), shaped(4, 16,...  0.97 us
    pallas_call x1, Pallas kernels, on_device(): call(bioheat_inner, 'bioheat_inner', [vmem()] * 8, [block, shaped(2, 24,...  0.94 us
  transfers between devices with their start and end apart: 10, of which 8 were waited for; matrix products, arithmetic and copies ran while one was open for 0% of the time, Pallas kernels for 21%

profile of v7, /device:TPU:20, one launch (start us, length us, event | category | flops | bytes accessed | tf_op | source)
XLA Modules:
  0.0 34.5 jit_solution(6534348324650582987)
XLA Ops:
  0.6 0.0 copy-start.2
  0.6 0.0 copy-start.1
  0.7 1.3 %pack_x.1 = (f32[256,256]{1,0:T(8,128)S(1)}, f32[256,256]{1,0:T(8,128)S(1)}, f32[224,256]{1,0:T(8,128)S(1)}, f32[224,256]{1,0:T(8,128)S(1)}, f32[4,16,128]{2,1,0...) custom-call(f32[4]{0:T(128)} %wash_h.1, ...), custom_call_target="tpu_custom_call" | custom-call | flops 2000000 | bytes 2000000 | tf_op jit(solution)/shard_map/pack_x/pallas_call | solution.py:638
  2.0 2.0 %collective-permute-start.2 = (f32[224,256]{1,0:T(8,128)S(1)}, f32[224,256]{1,0:T(8,128)S(1)}, u32[]{:S(2)}, u32[]{:S(2)}) collective-permute-start(f32[224,256]{1,0:T(8,128)S(1)} %get-tuple-element.47), channel_id=1, source_target_pairs={{0,4},{1,5},{2,6},{3,7},{4,0},{5,1},{6,2},{7,3},{8,12},{9,13},{10,... | collective-permute-start | bytes 688136 | tf_op jit(solution)/shard_map/ppermute | solution.py:68
  4.0 4.7 %collective-permute-start.3 = (f32[224,256]{1,0:T(8,128)S(1)}, f32[224,256]{1,0:T(8,128)S(1)}, u32[]{:S(2)}, u32[]{:S(2)}) collective-permute-start(f32[224,256]{1,0:T(8,128)S(1)} %get-tuple-element.48), channel_id=1, source_target_pairs={{0,1},{1,0},{2,3},{3,2},{4,8},{5,9},{6,10},{7,11},{8,4},{9,5},{10,... | collective-permute-start | bytes 688136 | tf_op jit(solution)/shard_map/ppermute | solution.py:68
  8.7 1.2 %collective-permute-start = (f32[256,256]{1,0:T(8,128)S(1)}, f32[256,256]{1,0:T(8,128)S(1)}, u32[]{:S(2)}, u32[]{:S(2)}) collective-permute-start(f32[256,256]{1,0:T(8,128)S(1)} %get-tuple-element.45), channel_id=1, source_target_pairs={{0,64},{1,65},{2,66},{3,67},{4,68},{5,69},{6,70},{7,71},{8,72},{9,... | collective-permute-start | bytes 786440 | tf_op jit(solution)/shard_map/ppermute | solution.py:68
  9.9 0.0 collective-permute-start.1
  9.9 3.4 %sources.1 = (f32[2,10,48,256]{3,2,1,0:T(8,128)S(1)}, f32[2,10,48,128]{3,2,1,0:T(8,128)S(1)}, bf16[128,256]{1,0:T(8,128)(2,1)S(1)}, bf16[256,128]{1,0:T(8,128)(2...) custom-call(s32[3,1024]{1,0:T(4,128)} %bitcast.1, f32[2,1024]{1,0:T(2,128)} %exc_h.1, ...), custom_call_target="tpu_custom_call" | custom-call | flops 8000000 | bytes 8000000 | tf_op jit(solution)/shard_map/sources/pallas_call | solution.py:657
  13.3 0.0 collective-permute-done.2.y_one
  13.3 1.4 %collective-permute-done.3.y_two = f32[224,256]{1,0:T(8,128)S(1)} collective-permute-done((f32[224,256]{1,0:T(8,128)S(1)}, f32[224,256]{1,0:T(8,128)S(1)}, u32[]{:S(2)}, u32[]{:S(2)}) %collective-permute-start.3) | collective-permute-done | bytes 229408 | tf_op jit(solution)/shard_map/ppermute | solution.py:68
  14.7 1.3 %collective-permute-start.4 = (f32[128,256]{1,0:T(8,128)S(1)}, f32[128,256]{1,0:T(8,128)S(1)}, u32[]{:S(2)}, u32[]{:S(2)}) collective-permute-start(f32[128,256]{1,0:T(8,128)S(1)} %get-tuple-element.50), channel_id=1, source_target_pairs={{0,64},{1,65},{2,66},{3,67},{4,68},{5,69},{6,70},{7,71},{8,72},{9,... | collective-permute-start | bytes 393224 | tf_op jit(solution)/shard_map/ppermute | solution.py:68
  16.0 0.0 collective-permute-start.5
  16.0 0.3 collective-permute-done.x_one
  16.3 0.9 %collective-permute-done.1.x_two = f32[256,256]{1,0:T(8,128)S(1)} collective-permute-done((f32[256,256]{1,0:T(8,128)S(1)}, f32[256,256]{1,0:T(8,128)S(1)}, u32[]{:S(2)}, u32[]{:S(2)}) %collective-permute-start.1) | collective-permute-done | bytes 262176 | tf_op jit(solution)/shard_map/ppermute | solution.py:68
  17.2 2.6 %collective-permute-done.4.k_one = f32[128,256]{1,0:T(8,128)S(1)} collective-permute-done((f32[128,256]{1,0:T(8,128)S(1)}, f32[128,256]{1,0:T(8,128)S(1)}, u32[]{:S(2)}, u32[]{:S(2)}) %collective-permute-start.4) | collective-permute-done | bytes 131104 | tf_op jit(solution)/shard_map/ppermute | solution.py:68
  19.8 1.2 %collective-permute-done.5.k_two = f32[128,256]{1,0:T(8,128)S(1)} collective-permute-done((f32[128,256]{1,0:T(8,128)S(1)}, f32[128,256]{1,0:T(8,128)S(1)}, u32[]{:S(2)}, u32[]{:S(2)}) %collective-permute-start.5) | collective-permute-done | bytes 131104 | tf_op jit(solution)/shard_map/ppermute | solution.py:68
  21.0 0.8 %pack_z.1 = (f32[1632,256]{1,0:T(8,128)S(1)}, f32[1056,128]{1,0:T(8,128)S(1)}, f32[168,128]{1,0:T(8,128)S(1)}, f32[168,128]{1,0:T(8,128)S(1)}) custom-call(f32[2,8,32,256]{3,2,1,0:T(8,128)S(1)} %get-tuple-element.40.it, f32[2,4,16,128]{3,2,1,0:T(8,128)S(1)} %get-tuple-element.41.co, s32[8,32,256]{2,1,0:T(8,128)S(1)} %get-tuple-element.42.codes, ...), custom_call_target="tpu_custom_call" | custom-call | flops 2000000 | bytes 2000000 | tf_op jit(solution)/shard_map/pack_z/pallas_call | solution.py:678
  21.8 0.1 collective-permute-start.6
  21.9 0.1 collective-permute-start.7
  22.0 0.0 copy-done.2
  22.0 0.0 copy-done.1
  22.0 2.9 %smooth_inner.1 = (f32[2,8,32,256]{3,2,1,0:T(8,128)S(1)}, f32[96,128]{1,0:T(8,128)S(1)}, f32[1632,128]{1,0:T(8,128)S(1)}, f32[768,128]{1,0:T(8,128)S(1)}) custom-call(f32[4]{0:T(128)S(1)} %copy-done.1, f32[4]{0:T(128)S(1)} %copy-done.2, f32[1632,256]{1,0:T(8,128)S(1)} %get-tuple-element.55.wide, f32[1056,128]{1,0:T(8,128)S(1)} %get-tuple-element.52.narrow, ...), custom_call_target="tpu_custom_call" | custom-call | flops 2000000 | bytes 2000000 | tf_op jit(solution)/shard_map/smooth_inner/pallas_call | solution.py:694
  24.9 0.0 copy-start
  24.9 0.0 collective-permute-done.6.z_one
  24.9 1.5 %collective-permute-done.7.z_two = f32[168,128]{1,0:T(8,128)S(1)} collective-permute-done((f32[168,128]{1,0:T(8,128)S(1)}, f32[168,128]{1,0:T(8,128)S(1)}, u32[]{:S(2)}, u32[]{:S(2)}) %collective-permute-start.7) | collective-permute-done | bytes 86048 | tf_op jit(solution)/shard_map/ppermute | solution.py:68
  26.5 2.3 %smooth_ends.1 = (f32[2,8,32,128]{3,2,1,0:T(8,128)S(1)}, f32[96,128]{1,0:T(8,128)S(1)}, f32[96,128]{1,0:T(8,128)S(1)}, f32[96,128]{1,0:T(8,128)S(1)}, f32[96,128]{1,0:T(8,128)S(1)}) custom-call(f32[4]{0:T(128)S(1)} %copy-done.1, f32[4]{0:T(128)S(1)} %copy-done.2, f32[1632,128]{1,0:T(8,128)S(1)} %get-tuple-element.59.ends, ...), custom_call_target="tpu_custom_call" | custom-call | flops 2000000 | bytes 2000000 | tf_op jit(solution)/shard_map/smooth_ends/pallas_call | solution.py:699
  28.8 0.6 %collective-permute-start.8 = (f32[96,128]{1,0:T(8,128)S(1)}, f32[96,128]{1,0:T(8,128)S(1)}, u32[]{:S(2)}, u32[]{:S(2)}) collective-permute-start(f32[96,128]{1,0:T(8,128)S(1)} %get-tuple-element.73), channel_id=1, source_target_pairs={{0,64},{1,65},{2,66},{3,67},{4,68},{5,69},{6,70},{7,71},{8,72},{9,... | collective-permute-start | bytes 147464 | tf_op jit(solution)/shard_map/ppermute | solution.py:68
  29.4 0.1 collective-permute-start.9
  29.5 0.0 copy-done
  29.5 0.9 %bioheat_inner.1 = (f32[12,24,256]{2,1,0:T(8,128)S(1)}, f32[2,24,256]{2,1,0:T(8,128)S(1)}, f32[10,24,256]{2,1,0:T(8,128)S(1)}, f32[4,16,128]{2,1,0:T(8,128)S(1)}, f32[2,8,32,256]{3,2,1,0:T(8,128)}) custom-call(f32[1056,128]{1,0:T(8,128)S(1)} %get-tuple-element.52.narrow, f32[168,128]{1,0:T(8,128)S(1)} %collective-permute-done.6.z_one, ...), custom_call_target="tpu_custom_call" | custom-call | flops 2000000 | bytes 2000000 | tf_op jit(solution)/shard_map/bioheat_inner/pallas_call | solution.py:707
  30.5 2.5 %collective-permute-done.8.x_one = f32[96,128]{1,0:T(8,128)S(1)} collective-permute-done((f32[96,128]{1,0:T(8,128)S(1)}, f32[96,128]{1,0:T(8,128)S(1)}, u32[]{:S(2)}, u32[]{:S(2)}) %collective-permute-start.8) | collective-permute-done | bytes 49184 | tf_op jit(solution)/shard_map/ppermute | solution.py:68
  33.0 0.5 %collective-permute-done.9.x_two = f32[96,128]{1,0:T(8,128)S(1)} collective-permute-done((f32[96,128]{1,0:T(8,128)S(1)}, f32[96,128]{1,0:T(8,128)S(1)}, u32[]{:S(2)}, u32[]{:S(2)}) %collective-permute-start.9) | collective-permute-done | bytes 49184 | tf_op jit(solution)/shard_map/ppermute | solution.py:68
  33.5 1.0 %bioheat.1 = (f32[4,16,128]{2,1,0:T(8,128)}, f32[4,16,128]{2,1,0:T(8,128)}) custom-call(f32[12,24,256]{2,1,0:T(8,128)S(1)} %get-tuple-element.69.begun, f32[2,24,256]{2,1,0:T(8,128)S(1)} %get-tuple-element.70.later, f32[10,24,256]{2,1,0:T(8,128)S(1)} %get-tuple-element.71.wash, f32[4,16,128]{2,1,0:T(8,128)S(1)} %get-tuple-element.72.dose_in, ...), custom_call_target="tpu_custom_call" | custom-call | flops 2000000 | bytes 2000000 | tf_op jit(solution)/shard_map/bioheat/pallas_call | solution.py:718
  (1 shorter events, 0.0 us)
Async XLA Ops:
  0.6 21.4 %copy-start.2 = (f32[4]{0:T(128)S(1)}, f32[4]{0:T(128)}, u32[]{:S(2)}) copy-start(f32[4]{0:T(128)} %damp_t.3) | copy-start | bytes 52
  0.6 21.4 %copy-start.1 = (f32[4]{0:T(128)S(1)}, f32[4]{0:T(128)}, u32[]{:S(2)}) copy-start(f32[4]{0:T(128)} %wave_t.3) | copy-start | bytes 52
  2.0 11.3 %collective-permute-start.2 = (f32[224,256]{1,0:T(8,128)S(1)}, f32[224,256]{1,0:T(8,128)S(1)}, u32[]{:S(2)}, u32[]{:S(2)}) collective-permute-start(f32[224,256]{1,0:T(8,128)S(1)} %get-tuple-element.47), channel_id=1, source_target_pairs={{0,4},{1,5},{2,6},{3,7},{4,0},{5,1},{6,2},{7,3},{8,12},{9,13},{10,... | collective-permute-start | bytes 688136 | tf_op jit(solution)/shard_map/ppermute | solution.py:68
  4.0 10.7 %collective-permute-start.3 = (f32[224,256]{1,0:T(8,128)S(1)}, f32[224,256]{1,0:T(8,128)S(1)}, u32[]{:S(2)}, u32[]{:S(2)}) collective-permute-start(f32[224,256]{1,0:T(8,128)S(1)} %get-tuple-element.48), channel_id=1, source_target_pairs={{0,1},{1,0},{2,3},{3,2},{4,8},{5,9},{6,10},{7,11},{8,4},{9,5},{10,... | collective-permute-start | bytes 688136 | tf_op jit(solution)/shard_map/ppermute | solution.py:68
  8.7 7.6 %collective-permute-start = (f32[256,256]{1,0:T(8,128)S(1)}, f32[256,256]{1,0:T(8,128)S(1)}, u32[]{:S(2)}, u32[]{:S(2)}) collective-permute-start(f32[256,256]{1,0:T(8,128)S(1)} %get-tuple-element.45), channel_id=1, source_target_pairs={{0,64},{1,65},{2,66},{3,67},{4,68},{5,69},{6,70},{7,71},{8,72},{9,... | collective-permute-start | bytes 786440 | tf_op jit(solution)/shard_map/ppermute | solution.py:68
  9.9 7.3 %collective-permute-start.1 = (f32[256,256]{1,0:T(8,128)S(1)}, f32[256,256]{1,0:T(8,128)S(1)}, u32[]{:S(2)}, u32[]{:S(2)}) collective-permute-start(f32[256,256]{1,0:T(8,128)S(1)} %get-tuple-element.46), channel_id=1, source_target_pairs={{0,1},{1,0},{2,3},{3,2},{4,5},{5,4},{6,7},{7,6},{8,9},{9,8},{10,11... | collective-permute-start | bytes 786440 | tf_op jit(solution)/shard_map/ppermute | solution.py:68
  14.7 5.1 %collective-permute-start.4 = (f32[128,256]{1,0:T(8,128)S(1)}, f32[128,256]{1,0:T(8,128)S(1)}, u32[]{:S(2)}, u32[]{:S(2)}) collective-permute-start(f32[128,256]{1,0:T(8,128)S(1)} %get-tuple-element.50), channel_id=1, source_target_pairs={{0,64},{1,65},{2,66},{3,67},{4,68},{5,69},{6,70},{7,71},{8,72},{9,... | collective-permute-start | bytes 393224 | tf_op jit(solution)/shard_map/ppermute | solution.py:68
  16.0 5.0 %collective-permute-start.5 = (f32[128,256]{1,0:T(8,128)S(1)}, f32[128,256]{1,0:T(8,128)S(1)}, u32[]{:S(2)}, u32[]{:S(2)}) collective-permute-start(f32[128,256]{1,0:T(8,128)S(1)} %get-tuple-element.51), channel_id=1, source_target_pairs={{0,1},{1,0},{2,3},{3,2},{4,5},{5,4},{6,7},{7,6},{8,9},{9,8},{10,11... | collective-permute-start | bytes 393224 | tf_op jit(solution)/shard_map/ppermute | solution.py:68
  21.8 3.2 %collective-permute-start.6 = (f32[168,128]{1,0:T(8,128)S(1)}, f32[168,128]{1,0:T(8,128)S(1)}, u32[]{:S(2)}, u32[]{:S(2)}) collective-permute-start(f32[168,128]{1,0:T(8,128)S(1)} %get-tuple-element.53), channel_id=1, source_target_pairs={{0,1},{1,0},{2,3},{3,2},{4,5},{5,4},{6,7},{7,6},{8,9},{9,8},{10,11... | collective-permute-start | bytes 258056 | tf_op jit(solution)/shard_map/ppermute | solution.py:68
  21.9 4.6 %collective-permute-start.7 = (f32[168,128]{1,0:T(8,128)S(1)}, f32[168,128]{1,0:T(8,128)S(1)}, u32[]{:S(2)}, u32[]{:S(2)}) collective-permute-start(f32[168,128]{1,0:T(8,128)S(1)} %get-tuple-element.54), channel_id=1, source_target_pairs={{0,64},{1,2},{2,1},{3,67},{4,68},{5,6},{6,5},{7,71},{8,72},{9,10},... | collective-permute-start | bytes 258056 | tf_op jit(solution)/shard_map/ppermute | solution.py:68
  24.9 4.6 %copy-start = (f32[4,16,128]{2,1,0:T(8,128)S(1)}, f32[4,16,128]{2,1,0:T(8,128)}, u32[]{:S(2)}) copy-start(f32[4,16,128]{2,1,0:T(8,128)} %injury.1) | copy-start | bytes 98308
  28.8 4.2 %collective-permute-start.8 = (f32[96,128]{1,0:T(8,128)S(1)}, f32[96,128]{1,0:T(8,128)S(1)}, u32[]{:S(2)}, u32[]{:S(2)}) collective-permute-start(f32[96,128]{1,0:T(8,128)S(1)} %get-tuple-element.73), channel_id=1, source_target_pairs={{0,64},{1,65},{2,66},{3,67},{4,68},{5,69},{6,70},{7,71},{8,72},{9,... | collective-permute-start | bytes 147464 | tf_op jit(solution)/shard_map/ppermute | solution.py:68
  29.4 4.1 %collective-permute-start.9 = (f32[96,128]{1,0:T(8,128)S(1)}, f32[96,128]{1,0:T(8,128)S(1)}, u32[]{:S(2)}, u32[]{:S(2)}) collective-permute-start(f32[96,128]{1,0:T(8,128)S(1)} %get-tuple-element.74), channel_id=1, source_target_pairs={{0,1},{1,0},{2,3},{3,2},{4,5},{5,4},{6,7},{7,6},{8,9},{9,8},{10,11... | collective-permute-start | bytes 147464 | tf_op jit(solution)/shard_map/ppermute | solution.py:68

commit v8 on v7

--- a/solution.py
+++ b/solution.py
@@ -521,7 +521,7 @@
         beside = state[f - 1] + state[f + 1]
         beside = beside + pltpu.roll(mid, 1, 0) + pltpu.roll(mid, 23, 0)
         beside = beside + pltpu.roll(mid, 1, 1) + pltpu.roll(mid, 255, 1)
-        return mid + DIFFUSION * (beside - 6.0 * mid) - wash[f - 1] * mid
+        return wash[f - 1] * mid + DIFFUSION * beside
 
     def finish(self, cooled, heat, f):
         return (cooled + HEATING * heat) * self.edge[f]
@@ -557,7 +557,7 @@
     for f in range(TX):
         now[f] = extended(N_THETA, f) * heat.edge[f]
     for f in range(QX):
-        wash[f] = extended(N_PERF, f)
+        wash[f] = (1.0 - 6.0 * DIFFUSION) - extended(N_PERF, f)
     for f in range(1, TX - 1):
         new = heat.step(now, wash, f)
         if 4 <= f < 8:

time: 34.7 us -> 34.9 us (level)
  waiting for transfers between devices: 10.8 us -> 11.4 us
  Pallas kernels: 12.7 us -> 12.3 us
    ppermute x10, waiting for transfers between devices: 10.8 us -> 11.4 us  [exchange(): lax.ppermute(buffer, AXES, swaps(sizes, axis, bool(k)))]
    pallas_call x1, Pallas kernels: 3.39 us -> 2.97 us  [on_device(): call(sources, 'sources', [hbm(), hbm(), vmem()], [shaped(2, CX, 48, 256),...]
  transfers between devices with their start and end apart: 10 -> 10, of which waited for: 8 -> 8; matrix products, arithmetic and copies ran while one was open for 0% -> 0% of each run, Pallas kernels for 21% -> 20%
where the time goes in v8:
time: 34.9 us; the launch traced here: 34.5 us
  Pallas kernels  12.3 us (35%)
  waiting for transfers between devices  11.4 us (33%)
  starting transfers between devices  9.98 us (29%)
  between operations  0.76 us (2%)
    ppermute x10, waiting for transfers between devices, exchange(): lax.ppermute(buffer, AXES, swaps(sizes, axis, bool(k)))  11.4 us
    ppermute x10, starting transfers between devices, exchange(): lax.ppermute(buffer, AXES, swaps(sizes, axis, bool(k)))  9.98 us
    pallas_call x1, Pallas kernels, on_device(): call(sources, 'sources', [hbm(), hbm(), vmem()], [shaped(2, CX, 48, 256),...  2.97 us
    pallas_call x1, Pallas kernels, on_device(): call(smooth_inner, 'smooth_inner', [smem()] * 2 + [vmem()] * 6, [shaped(2...  2.91 us
    pallas_call x1, Pallas kernels, on_device(): call(smooth_ends, 'smooth_ends', [smem()] * 2 + [vmem()] * 8, [shaped(2,...  2.34 us
    pallas_call x1, Pallas kernels, on_device(): call(pack_x, 'pack_x', [hbm()] * 5, [shaped(XB, 256), shaped(XB, 256), sh...  1.33 us
    pallas_call x1, Pallas kernels, on_device(): call(bioheat, 'bioheat', [vmem()] * 8, [shaped(4, 16, 128), shaped(4, 16,...  0.98 us
    pallas_call x1, Pallas kernels, on_device(): call(bioheat_inner, 'bioheat_inner', [vmem()] * 8, [block, shaped(2, 24,...  0.94 us
  transfers between devices with their start and end apart: 10, of which 8 were waited for; matrix products, arithmetic and copies ran while one was open for 0% of the time, Pallas kernels for 20%

profile of v8, /device:TPU:20, one launch (start us, length us, event | category | flops | bytes accessed | tf_op | source)
XLA Modules:
  0.0 34.5 jit_solution(3599666128723707885)
XLA Ops:
  0.6 0.0 copy-start.2
  0.6 0.0 copy-start.1
  0.7 1.3 %pack_x.1 = (f32[256,256]{1,0:T(8,128)S(1)}, f32[256,256]{1,0:T(8,128)S(1)}, f32[224,256]{1,0:T(8,128)S(1)}, f32[224,256]{1,0:T(8,128)S(1)}, f32[4,16,128]{2,1,0...) custom-call(f32[4]{0:T(128)} %wash_h.1, ...), custom_call_target="tpu_custom_call" | custom-call | flops 2000000 | bytes 2000000 | tf_op jit(solution)/shard_map/pack_x/pallas_call | solution.py:638
  2.0 2.0 %collective-permute-start.2 = (f32[224,256]{1,0:T(8,128)S(1)}, f32[224,256]{1,0:T(8,128)S(1)}, u32[]{:S(2)}, u32[]{:S(2)}) collective-permute-start(f32[224,256]{1,0:T(8,128)S(1)} %get-tuple-element.47), channel_id=1, source_target_pairs={{0,4},{1,5},{2,6},{3,7},{4,0},{5,1},{6,2},{7,3},{8,12},{9,13},{10,... | collective-permute-start | bytes 688136 | tf_op jit(solution)/shard_map/ppermute | solution.py:68
  4.0 4.7 %collective-permute-start.3 = (f32[224,256]{1,0:T(8,128)S(1)}, f32[224,256]{1,0:T(8,128)S(1)}, u32[]{:S(2)}, u32[]{:S(2)}) collective-permute-start(f32[224,256]{1,0:T(8,128)S(1)} %get-tuple-element.48), channel_id=1, source_target_pairs={{0,1},{1,0},{2,3},{3,2},{4,8},{5,9},{6,10},{7,11},{8,4},{9,5},{10,... | collective-permute-start | bytes 688136 | tf_op jit(solution)/shard_map/ppermute | solution.py:68
  8.7 1.2 %collective-permute-start = (f32[256,256]{1,0:T(8,128)S(1)}, f32[256,256]{1,0:T(8,128)S(1)}, u32[]{:S(2)}, u32[]{:S(2)}) collective-permute-start(f32[256,256]{1,0:T(8,128)S(1)} %get-tuple-element.45), channel_id=1, source_target_pairs={{0,64},{1,65},{2,66},{3,67},{4,68},{5,69},{6,70},{7,71},{8,72},{9,... | collective-permute-start | bytes 786440 | tf_op jit(solution)/shard_map/ppermute | solution.py:68
  9.9 0.0 collective-permute-start.1
  9.9 3.0 %sources.1 = (f32[2,10,48,256]{3,2,1,0:T(8,128)S(1)}, f32[2,10,48,128]{3,2,1,0:T(8,128)S(1)}, bf16[128,256]{1,0:T(8,128)(2,1)S(1)}, bf16[256,128]{1,0:T(8,128)(2...) custom-call(s32[3,1024]{1,0:T(4,128)} %bitcast.1, f32[2,1024]{1,0:T(2,128)} %exc_h.1, ...), custom_call_target="tpu_custom_call" | custom-call | flops 8000000 | bytes 8000000 | tf_op jit(solution)/shard_map/sources/pallas_call | solution.py:657
  12.9 0.0 collective-permute-done.2.y_one
  12.9 1.8 %collective-permute-done.3.y_two = f32[224,256]{1,0:T(8,128)S(1)} collective-permute-done((f32[224,256]{1,0:T(8,128)S(1)}, f32[224,256]{1,0:T(8,128)S(1)}, u32[]{:S(2)}, u32[]{:S(2)}) %collective-permute-start.3) | collective-permute-done | bytes 229408 | tf_op jit(solution)/shard_map/ppermute | solution.py:68
  14.7 1.3 %collective-permute-start.4 = (f32[128,256]{1,0:T(8,128)S(1)}, f32[128,256]{1,0:T(8,128)S(1)}, u32[]{:S(2)}, u32[]{:S(2)}) collective-permute-start(f32[128,256]{1,0:T(8,128)S(1)} %get-tuple-element.50), channel_id=1, source_target_pairs={{0,64},{1,65},{2,66},{3,67},{4,68},{5,69},{6,70},{7,71},{8,72},{9,... | collective-permute-start | bytes 393224 | tf_op jit(solution)/shard_map/ppermute | solution.py:68
  16.0 0.0 collective-permute-start.5
  16.0 0.3 collective-permute-done.x_one
  16.3 0.8 %collective-permute-done.1.x_two = f32[256,256]{1,0:T(8,128)S(1)} collective-permute-done((f32[256,256]{1,0:T(8,128)S(1)}, f32[256,256]{1,0:T(8,128)S(1)}, u32[]{:S(2)}, u32[]{:S(2)}) %collective-permute-start.1) | collective-permute-done | bytes 262176 | tf_op jit(solution)/shard_map/ppermute | solution.py:68
  17.1 2.7 %collective-permute-done.4.k_one = f32[128,256]{1,0:T(8,128)S(1)} collective-permute-done((f32[128,256]{1,0:T(8,128)S(1)}, f32[128,256]{1,0:T(8,128)S(1)}, u32[]{:S(2)}, u32[]{:S(2)}) %collective-permute-start.4) | collective-permute-done | bytes 131104 | tf_op jit(solution)/shard_map/ppermute | solution.py:68
  19.8 1.2 %collective-permute-done.5.k_two = f32[128,256]{1,0:T(8,128)S(1)} collective-permute-done((f32[128,256]{1,0:T(8,128)S(1)}, f32[128,256]{1,0:T(8,128)S(1)}, u32[]{:S(2)}, u32[]{:S(2)}) %collective-permute-start.5) | collective-permute-done | bytes 131104 | tf_op jit(solution)/shard_map/ppermute | solution.py:68
  21.0 0.8 %pack_z.1 = (f32[1632,256]{1,0:T(8,128)S(1)}, f32[1056,128]{1,0:T(8,128)S(1)}, f32[168,128]{1,0:T(8,128)S(1)}, f32[168,128]{1,0:T(8,128)S(1)}) custom-call(f32[2,8,32,256]{3,2,1,0:T(8,128)S(1)} %get-tuple-element.40.it, f32[2,4,16,128]{3,2,1,0:T(8,128)S(1)} %get-tuple-element.41.co, s32[8,32,256]{2,1,0:T(8,128)S(1)} %get-tuple-element.42.codes, ...), custom_call_target="tpu_custom_call" | custom-call | flops 2000000 | bytes 2000000 | tf_op jit(solution)/shard_map/pack_z/pallas_call | solution.py:678
  21.8 0.1 collective-permute-start.6
  21.9 0.1 collective-permute-start.7
  22.0 0.0 copy-done.2
  22.0 0.0 copy-done.1
  22.0 2.9 %smooth_inner.1 = (f32[2,8,32,256]{3,2,1,0:T(8,128)S(1)}, f32[96,128]{1,0:T(8,128)S(1)}, f32[1632,128]{1,0:T(8,128)S(1)}, f32[768,128]{1,0:T(8,128)S(1)}) custom-call(f32[4]{0:T(128)S(1)} %copy-done.1, f32[4]{0:T(128)S(1)} %copy-done.2, f32[1632,256]{1,0:T(8,128)S(1)} %get-tuple-element.55.wide, f32[1056,128]{1,0:T(8,128)S(1)} %get-tuple-element.52.narrow, ...), custom_call_target="tpu_custom_call" | custom-call | flops 2000000 | bytes 2000000 | tf_op jit(solution)/shard_map/smooth_inner/pallas_call | solution.py:694
  24.9 0.0 copy-start
  24.9 0.0 collective-permute-done.6.z_one
  24.9 1.5 %collective-permute-done.7.z_two = f32[168,128]{1,0:T(8,128)S(1)} collective-permute-done((f32[168,128]{1,0:T(8,128)S(1)}, f32[168,128]{1,0:T(8,128)S(1)}, u32[]{:S(2)}, u32[]{:S(2)}) %collective-permute-start.7) | collective-permute-done | bytes 86048 | tf_op jit(solution)/shard_map/ppermute | solution.py:68
  26.5 2.3 %smooth_ends.1 = (f32[2,8,32,128]{3,2,1,0:T(8,128)S(1)}, f32[96,128]{1,0:T(8,128)S(1)}, f32[96,128]{1,0:T(8,128)S(1)}, f32[96,128]{1,0:T(8,128)S(1)}, f32[96,128]{1,0:T(8,128)S(1)}) custom-call(f32[4]{0:T(128)S(1)} %copy-done.1, f32[4]{0:T(128)S(1)} %copy-done.2, f32[1632,128]{1,0:T(8,128)S(1)} %get-tuple-element.59.ends, ...), custom_call_target="tpu_custom_call" | custom-call | flops 2000000 | bytes 2000000 | tf_op jit(solution)/shard_map/smooth_ends/pallas_call | solution.py:699
  28.8 0.6 %collective-permute-start.8 = (f32[96,128]{1,0:T(8,128)S(1)}, f32[96,128]{1,0:T(8,128)S(1)}, u32[]{:S(2)}, u32[]{:S(2)}) collective-permute-start(f32[96,128]{1,0:T(8,128)S(1)} %get-tuple-element.73), channel_id=1, source_target_pairs={{0,64},{1,65},{2,66},{3,67},{4,68},{5,69},{6,70},{7,71},{8,72},{9,... | collective-permute-start | bytes 147464 | tf_op jit(solution)/shard_map/ppermute | solution.py:68
  29.4 0.0 collective-permute-start.9
  29.4 0.0 copy-done
  29.4 0.9 %bioheat_inner.1 = (f32[12,24,256]{2,1,0:T(8,128)S(1)}, f32[2,24,256]{2,1,0:T(8,128)S(1)}, f32[10,24,256]{2,1,0:T(8,128)S(1)}, f32[4,16,128]{2,1,0:T(8,128)S(1)}, f32[2,8,32,256]{3,2,1,0:T(8,128)}) custom-call(f32[1056,128]{1,0:T(8,128)S(1)} %get-tuple-element.52.narrow, f32[168,128]{1,0:T(8,128)S(1)} %collective-permute-done.6.z_one, ...), custom_call_target="tpu_custom_call" | custom-call | flops 2000000 | bytes 2000000 | tf_op jit(solution)/shard_map/bioheat_inner/pallas_call | solution.py:707
  30.3 2.6 %collective-permute-done.8.x_one = f32[96,128]{1,0:T(8,128)S(1)} collective-permute-done((f32[96,128]{1,0:T(8,128)S(1)}, f32[96,128]{1,0:T(8,128)S(1)}, u32[]{:S(2)}, u32[]{:S(2)}) %collective-permute-start.8) | collective-permute-done | bytes 49184 | tf_op jit(solution)/shard_map/ppermute | solution.py:68
  33.0 0.5 %collective-permute-done.9.x_two = f32[96,128]{1,0:T(8,128)S(1)} collective-permute-done((f32[96,128]{1,0:T(8,128)S(1)}, f32[96,128]{1,0:T(8,128)S(1)}, u32[]{:S(2)}, u32[]{:S(2)}) %collective-permute-start.9) | collective-permute-done | bytes 49184 | tf_op jit(solution)/shard_map/ppermute | solution.py:68
  33.5 1.0 %bioheat.1 = (f32[4,16,128]{2,1,0:T(8,128)}, f32[4,16,128]{2,1,0:T(8,128)}) custom-call(f32[12,24,256]{2,1,0:T(8,128)S(1)} %get-tuple-element.69.begun, f32[2,24,256]{2,1,0:T(8,128)S(1)} %get-tuple-element.70.later, f32[10,24,256]{2,1,0:T(8,128)S(1)} %get-tuple-element.71.wash, f32[4,16,128]{2,1,0:T(8,128)S(1)} %get-tuple-element.72.dose_in, ...), custom_call_target="tpu_custom_call" | custom-call | flops 2000000 | bytes 2000000 | tf_op jit(solution)/shard_map/bioheat/pallas_call | solution.py:718
  (1 shorter events, 0.0 us)
Async XLA Ops:
  0.6 21.4 %copy-start.2 = (f32[4]{0:T(128)S(1)}, f32[4]{0:T(128)}, u32[]{:S(2)}) copy-start(f32[4]{0:T(128)} %damp_t.3) | copy-start | bytes 52
  0.6 21.4 %copy-start.1 = (f32[4]{0:T(128)S(1)}, f32[4]{0:T(128)}, u32[]{:S(2)}) copy-start(f32[4]{0:T(128)} %wave_t.3) | copy-start | bytes 52
  2.0 10.9 %collective-permute-start.2 = (f32[224,256]{1,0:T(8,128)S(1)}, f32[224,256]{1,0:T(8,128)S(1)}, u32[]{:S(2)}, u32[]{:S(2)}) collective-permute-start(f32[224,256]{1,0:T(8,128)S(1)} %get-tuple-element.47), channel_id=1, source_target_pairs={{0,4},{1,5},{2,6},{3,7},{4,0},{5,1},{6,2},{7,3},{8,12},{9,13},{10,... | collective-permute-start | bytes 688136 | tf_op jit(solution)/shard_map/ppermute | solution.py:68
  4.0 10.7 %collective-permute-start.3 = (f32[224,256]{1,0:T(8,128)S(1)}, f32[224,256]{1,0:T(8,128)S(1)}, u32[]{:S(2)}, u32[]{:S(2)}) collective-permute-start(f32[224,256]{1,0:T(8,128)S(1)} %get-tuple-element.48), channel_id=1, source_target_pairs={{0,1},{1,0},{2,3},{3,2},{4,8},{5,9},{6,10},{7,11},{8,4},{9,5},{10,... | collective-permute-start | bytes 688136 | tf_op jit(solution)/shard_map/ppermute | solution.py:68
  8.7 7.6 %collective-permute-start = (f32[256,256]{1,0:T(8,128)S(1)}, f32[256,256]{1,0:T(8,128)S(1)}, u32[]{:S(2)}, u32[]{:S(2)}) collective-permute-start(f32[256,256]{1,0:T(8,128)S(1)} %get-tuple-element.45), channel_id=1, source_target_pairs={{0,64},{1,65},{2,66},{3,67},{4,68},{5,69},{6,70},{7,71},{8,72},{9,... | collective-permute-start | bytes 786440 | tf_op jit(solution)/shard_map/ppermute | solution.py:68
  9.9 7.2 %collective-permute-start.1 = (f32[256,256]{1,0:T(8,128)S(1)}, f32[256,256]{1,0:T(8,128)S(1)}, u32[]{:S(2)}, u32[]{:S(2)}) collective-permute-start(f32[256,256]{1,0:T(8,128)S(1)} %get-tuple-element.46), channel_id=1, source_target_pairs={{0,1},{1,0},{2,3},{3,2},{4,5},{5,4},{6,7},{7,6},{8,9},{9,8},{10,11... | collective-permute-start | bytes 786440 | tf_op jit(solution)/shard_map/ppermute | solution.py:68
  14.7 5.1 %collective-permute-start.4 = (f32[128,256]{1,0:T(8,128)S(1)}, f32[128,256]{1,0:T(8,128)S(1)}, u32[]{:S(2)}, u32[]{:S(2)}) collective-permute-start(f32[128,256]{1,0:T(8,128)S(1)} %get-tuple-element.50), channel_id=1, source_target_pairs={{0,64},{1,65},{2,66},{3,67},{4,68},{5,69},{6,70},{7,71},{8,72},{9,... | collective-permute-start | bytes 393224 | tf_op jit(solution)/shard_map/ppermute | solution.py:68
  16.0 5.0 %collective-permute-start.5 = (f32[128,256]{1,0:T(8,128)S(1)}, f32[128,256]{1,0:T(8,128)S(1)}, u32[]{:S(2)}, u32[]{:S(2)}) collective-permute-start(f32[128,256]{1,0:T(8,128)S(1)} %get-tuple-element.51), channel_id=1, source_target_pairs={{0,1},{1,0},{2,3},{3,2},{4,5},{5,4},{6,7},{7,6},{8,9},{9,8},{10,11... | collective-permute-start | bytes 393224 | tf_op jit(solution)/shard_map/ppermute | solution.py:68
  21.8 3.2 %collective-permute-start.6 = (f32[168,128]{1,0:T(8,128)S(1)}, f32[168,128]{1,0:T(8,128)S(1)}, u32[]{:S(2)}, u32[]{:S(2)}) collective-permute-start(f32[168,128]{1,0:T(8,128)S(1)} %get-tuple-element.53), channel_id=1, source_target_pairs={{0,1},{1,0},{2,3},{3,2},{4,5},{5,4},{6,7},{7,6},{8,9},{9,8},{10,11... | collective-permute-start | bytes 258056 | tf_op jit(solution)/shard_map/ppermute | solution.py:68
  21.9 4.6 %collective-permute-start.7 = (f32[168,128]{1,0:T(8,128)S(1)}, f32[168,128]{1,0:T(8,128)S(1)}, u32[]{:S(2)}, u32[]{:S(2)}) collective-permute-start(f32[168,128]{1,0:T(8,128)S(1)} %get-tuple-element.54), channel_id=1, source_target_pairs={{0,64},{1,2},{2,1},{3,67},{4,68},{5,6},{6,5},{7,71},{8,72},{9,10},... | collective-permute-start | bytes 258056 | tf_op jit(solution)/shard_map/ppermute | solution.py:68
  24.9 4.5 %copy-start = (f32[4,16,128]{2,1,0:T(8,128)S(1)}, f32[4,16,128]{2,1,0:T(8,128)}, u32[]{:S(2)}) copy-start(f32[4,16,128]{2,1,0:T(8,128)} %injury.1) | copy-start | bytes 98308
  28.8 4.2 %collective-permute-start.8 = (f32[96,128]{1,0:T(8,128)S(1)}, f32[96,128]{1,0:T(8,128)S(1)}, u32[]{:S(2)}, u32[]{:S(2)}) collective-permute-start(f32[96,128]{1,0:T(8,128)S(1)} %get-tuple-element.73), channel_id=1, source_target_pairs={{0,64},{1,65},{2,66},{3,67},{4,68},{5,69},{6,70},{7,71},{8,72},{9,... | collective-permute-start | bytes 147464 | tf_op jit(solution)/shard_map/ppermute | solution.py:68
  29.4 4.1 %collective-permute-start.9 = (f32[96,128]{1,0:T(8,128)S(1)}, f32[96,128]{1,0:T(8,128)S(1)}, u32[]{:S(2)}, u32[]{:S(2)}) collective-permute-start(f32[96,128]{1,0:T(8,128)S(1)} %get-tuple-element.74), channel_id=1, source_target_pairs={{0,1},{1,0},{2,3},{3,2},{4,5},{5,4},{6,7},{7,6},{8,9},{9,8},{10,11... | collective-permute-start | bytes 147464 | tf_op jit(solution)/shard_map/ppermute | solution.py:68
